TPU v7x, 32 devices: a whole 2x2x4 slice. The times are simulated.
32 devices in a mesh: rows: 16 (over z, y, x), tgt: 2 (over core).
Axes of the slice: x: 2, y: 2, z: 4, core: 2. Of those that a mesh axis runs over, the one named last changes fastest.
Arguments:
- counts: int32 [16], P('rows'), may hold values from 512 to 2048, as said below
- samples: float32 [32768, 256], P('rows'), may hold values from -6 to 6
- targets: float32 [32768, 256], P('rows', 'tgt'), may hold values from -6 to 6
- point_ids: int32 [2, 512], replicated, may hold values from 0 to 32767, as said below
- block_inverse: float32 [2, 512, 512], replicated, may hold values from -1.34869915e-06 to 1.6607488e-05
Outputs:
- residual: float32 [32768, 256], P('rows', 'tgt')
Inputs may be any that keep to these rules, and one draw needn't show every extreme that they name: `counts`: some device has exactly 2048 live rows. `point_ids`: every id is d * 2048 + s with s < counts[d].
All inputs are finite; a program needn't handle non-finite values.
Results may differ from a plain program's by a relative error of at most 0.0003.
Values sent between devices are 32-bit elements; how exact they have to be, the bound alone decides.
No kernel may reach another device: no remote copies, remote signals or barrier semaphores. Data moves between devices by JAX's collectives and lax.ppermute only.
A program may use at most 64 MiB of HBM per device.

v0:
```python
import jax
import jax.numpy as jnp
from jax import lax
from jax.sharding import PartitionSpec as P


def kernel_columns(rows_in, points):
    scaled = lax.dot_general(
        rows_in,
        points,
        (((1,), (1,)), ((), ())),
        precision=lax.Precision.HIGHEST,
        preferred_element_type=jnp.float32,
    )
    scaled = scaled * (1.0 / rows_in.shape[1] ** 0.5)
    return (0.5 * scaled + 1.0) ** 3


def pick_rows(samples, wanted, device):
    rows_here = samples.shape[0]
    local = wanted - device * rows_here
    owned = (local >= 0) & (local < rows_here)
    taken = jnp.take(samples, jnp.clip(local, 0, rows_here - 1), axis=0)
    return jnp.where(owned[:, None], taken, 0.0)


def on_device(counts, samples, targets, point_ids, block_inverse):
    rows_here = samples.shape[0]
    live_count = counts[0]
    device = lax.axis_index("rows")
    row_block = min(512, rows_here)
    block_total = rows_here // row_block
    residual = targets
    block_size = point_ids.shape[1]
    for block_index in range(point_ids.shape[0]):
        wanted = point_ids[block_index]
        points = lax.psum(pick_rows(samples, wanted, device), "rows")

        def accumulate(index, carry):
            stored, totals = carry
            start = index * row_block
            rows_in = lax.dynamic_slice_in_dim(samples, start, row_block, 0)
            current = lax.dynamic_slice_in_dim(residual, start, row_block, 0)
            slot_ids = start + jnp.arange(row_block, dtype=jnp.int32)
            columns = jnp.where(
                (slot_ids < live_count)[:, None], kernel_columns(rows_in, points), 0.0
            )
            totals = totals + lax.dot_general(
                columns,
                current,
                (((0,), (0,)), ((), ())),
                precision=lax.Precision.HIGHEST,
                preferred_element_type=jnp.float32,
            )
            stored = lax.dynamic_update_slice_in_dim(stored, columns, start, 0)
            return (stored, totals)

        start_state = (
            jnp.zeros((rows_here, block_size), jnp.float32),
            jnp.zeros((block_size, residual.shape[1]), jnp.float32),
        )
        stored, totals = lax.fori_loop(0, block_total, accumulate, start_state)
        sums = lax.psum(totals, "rows")
        coefs = jnp.dot(
            block_inverse[block_index],
            sums,
            precision=lax.Precision.HIGHEST,
            preferred_element_type=jnp.float32,
        )
        residual = residual - jnp.dot(
            stored, coefs, precision=lax.Precision.HIGHEST, preferred_element_type=jnp.float32
        )
    return residual


def solution(mesh):
    return jax.shard_map(
        on_device,
        mesh=mesh,
        in_specs=(P("rows"), P("rows", None), P("rows", "tgt"), P(), P()),
        out_specs=P("rows", "tgt"),
        check_vma=False,
    )
```

profile of v0, /device:TPU:0, one launch (start us, length us, event | category | flops | bytes accessed | tf_op | source)
XLA Modules:
  0.0 426.6 jit_solution(17519809654846827084)
XLA Ops:
  6.5 0.0 copy-start
  6.5 0.0 all-reduce.5.cloned.1.call-start
  6.5 0.9 broadcast_clamp_fusion
  7.4 0.8 and_reduce_fusion
  8.2 3.2 gather_fusion
  11.4 1.0 select_select_fusion.1
  12.4 0.0 all-reduce.5.cloned.1.call-update
  12.4 0.0 all-reduce.9.cloned.1.call-start
  12.5 0.0 copy-done
  12.5 1.6 gather_fusion.1
  14.1 1.0 select_select_fusion
  15.1 109.3 %all-reduce.5.cloned.1.call-done = f32[512,256]{1,0:T(8,128)} async-done(((f32[512,256]{1,0:T(8,128)}), f32[512,256]{1,0:T(8,128)}) %all-reduce.5.cloned.1.call-update) | async-done | bytes 524304 | tf_op jit(solution)/shard_map/psum | solution.py:37
  124.4 2.5 broadcast.133.clone
  126.9 26.6 %while.36 = (s32[]{:T(128)}, f32[2048,512]{1,0:T(8,128)}, f32[512,128]{1,0:T(8,128)S(1)}, s32[]{:T(128)}, f32[2048,256]{1,0:T(8,128)S(1)}, /*index=5*/f32[512,25...) while((s32[]{:T(128)}, f32[2048,512]{1,0:T(8,128)}, ...), condition=%wide.region_2.4_spmd.clone, body=%wide.region_1.3_spmd.clone.sunk | while | flops 1209402368 | bytes 4982961 | solution.py:62
  126.9 0.7 add_compare_fusion.4
  127.5 3.2 constant_dynamic-update-slice_fusion.4
  130.7 2.8 convolution_add_fusion.4
  133.5 0.7 add_compare_fusion.4
  134.2 3.2 constant_dynamic-update-slice_fusion.4
  137.4 2.8 convolution_add_fusion.4
  140.2 0.7 add_compare_fusion.4
  140.8 3.2 constant_dynamic-update-slice_fusion.4
  144.0 2.8 convolution_add_fusion.4
  146.8 0.7 add_compare_fusion.4
  147.5 3.2 constant_dynamic-update-slice_fusion.4
  150.7 2.8 convolution_add_fusion.4
  153.5 0.0 copy-start.2
  153.5 0.7 copy-done.2
  154.2 0.0 all-reduce.9.cloned.1.call-update
  154.2 0.0 all-reduce.7.cloned.1.call-start
  154.3 110.1 %all-reduce.9.cloned.1.call-done = (f32[512,128]{1,0:T(8,128)}, f32[512,256]{1,0:T(8,128)}) async-done(((f32[512,128]{1,0:T(8,128)}, f32[512,256]{1,0:T(8,128)}), (f32[512,128]{1,0:T(8,128)}, f32[512,256]{1,0:T(8,128)})) %all-reduce.9.cloned.1.call-update) | async-done | bytes 786448 | tf_op jit(solution)/shard_map/psum | solution.py:63
  264.4 2.6 fusion.14
  266.9 6.9 %convolution_subtract_fusion.1 = f32[2048,128]{1,0:T(8,128)} fusion(f32[2048,128]{1,0:T(8,128)} %get-tuple-element.625, f32[2048,512]{1,0:T(8,128)} %get-tuple-element.360, f32[128,512]{1,0:T(8,128)S(1)} %fusion.14), kind=kOutput, calls=%fused_computation.25 | convolution fusion | flops 1610874880 | bytes 6553600 | tf_op jit(solution)/shard_map/dot_general | solution.py:70
  273.9 2.5 broadcast.133
  276.3 26.6 %while.37 = (s32[]{:T(128)}, f32[2048,512]{1,0:T(8,128)}, f32[512,128]{1,0:T(8,128)S(1)}, s32[]{:T(128)}, f32[2048,256]{1,0:T(8,128)S(1)}, /*index=5*/f32[512,25...) while((s32[]{:T(128)}, f32[2048,512]{1,0:T(8,128)}, ...), condition=%wide.region_6.8_spmd.clone, body=%wide.region_5.7_spmd.clone.sunk | while | flops 1209402368 | bytes 4982961 | solution.py:62
  276.3 0.7 add_compare_fusion.5
  277.0 3.2 constant_dynamic-update-slice_fusion.5
  280.1 2.8 convolution_add_fusion.5
  283.0 0.7 add_compare_fusion.5
  283.6 3.2 constant_dynamic-update-slice_fusion.5
  286.8 2.8 convolution_add_fusion.5
  289.7 0.7 add_compare_fusion.5
  290.3 3.2 constant_dynamic-update-slice_fusion.5
  293.5 2.8 convolution_add_fusion.5
  296.3 0.7 add_compare_fusion.5
  297.0 3.2 constant_dynamic-update-slice_fusion.5
  300.1 2.8 convolution_add_fusion.5
  302.9 0.0 copy-start.1
  303.0 0.7 copy-done.1
  303.7 0.0 all-reduce.7.cloned.1.call-update
  303.7 106.9 %all-reduce.7.cloned.1.call-done = f32[512,128]{1,0:T(8,128)} async-done(((f32[512,128]{1,0:T(8,128)}), f32[512,128]{1,0:T(8,128)}) %all-reduce.7.cloned.1.call-update) | async-done | bytes 262160 | tf_op jit(solution)/shard_map/psum | solution.py:63
  410.6 2.6 fusion.12
  413.1 6.9 %convolution_subtract_fusion = f32[2048,128]{1,0:T(8,128)} fusion(f32[2048,128]{1,0:T(8,128)} %get-tuple-element.620, f32[2048,512]{1,0:T(8,128)} %get-tuple-element.362, f32[128,512]{1,0:T(8,128)S(1)} %fusion.12), kind=kOutput, calls=%fused_computation.24 | convolution fusion | flops 1610874880 | bytes 6553600 | tf_op jit(solution)/shard_map/dot_general | solution.py:70
  (8 shorter events, 0.0 us)
Async XLA Ops:
  6.5 6.0 %copy-start = (f32[2048,256]{1,0:T(8,128)S(1)}, f32[2048,256]{1,0:T(8,128)}, u32[]{:S(2)}) copy-start(f32[2048,256]{1,0:T(8,128)} %param.12) | copy-start | bytes 6291460
  6.5 117.9 %all-reduce.5.cloned.1.call-start = ((), (), s32[]{:S(2)}) async-start(), calls=%async_computation | async-start | bytes 1048576 | tf_op jit(solution)/shard_map/psum | solution.py:37
  12.4 252.0 %all-reduce.9.cloned.1.call-start = ((), (), s32[]{:S(2)}) async-start(), calls=%async_computation.2 | async-start | bytes 1572864 | tf_op jit(solution)/shard_map/psum | solution.py:63
  153.5 0.7 copy-start.2
  154.2 256.4 %all-reduce.7.cloned.1.call-start = ((), (), s32[]{:S(2)}) async-start(), calls=%async_computation.1 | async-start | bytes 524288 | tf_op jit(solution)/shard_map/psum | solution.py:63
  302.9 0.7 copy-start.1
Sparse Core Ops, SparseCore 0:
  12.5 111.7 all-reduce.4
  154.3 110.0 all-reduce.8
  303.8 106.7 all-reduce.6
where the time goes:
time: 427 us
  waiting for transfers between devices  326 us (76%)
  matrix products  66.7 us (16%)
  between operations  13.2 us (3%)
  local copies, waits for them, and re-layouts  11.1 us (3%)
  other arithmetic  8.92 us (2%)
    psum x2, waiting for transfers between devices, on_device(): sums = lax.psum(totals, 'rows')  217 us
    psum x1, waiting for transfers between devices, on_device(): points = lax.psum(pick_rows(samples, wanted, device), 'rows')  109 us
    dot_general x8, matrix products, kernel_columns(): lax.dot_general(rows_in, points, (((1,), (1,)), ((), ())), precision=lax....  25.5 us
    dot_general x8, matrix products, accumulate(): lax.dot_general(columns, current, (((0,), (0,)), ((), ())), precision=lax...  22.3 us
    dot_general x2, matrix products, on_device(): jnp.dot(stored, coefs, precision=lax.Precision.HIGHEST, preferred_element...  13.8 us
  transfers between devices with their start and end apart: 3, of which 3 were waited for; matrix products, arithmetic and copies ran while one was open for 1% of the time, Pallas kernels for 0%

commit v1 on v0

v1 whole, which is shorter than its diff:
```python
import functools

import jax
import jax.numpy as jnp
from jax import lax
from jax.experimental import pallas as pl
from jax.experimental.pallas import tpu as pltpu
from jax.sharding import PartitionSpec as P

F32 = jnp.float32
BF16 = jnp.bfloat16
ROWS_STEP = 512


def round_up(value, unit):
    return -(-value // unit) * unit


def split(x):
    high = x.astype(BF16)
    return high, (x - high.astype(F32)).astype(BF16)


def dot(a, b, dims):
    return lax.dot_general(a, b, (dims, ((), ())), preferred_element_type=F32)


def dot3(a, b, dims):
    return dot(a[0], b[0], dims) + dot(a[0], b[1], dims) + dot(a[1], b[0], dims)


def pick_kernel(groups, cores, cap, ids_ref, samples_ref, rows_ref, slots_ref, most_ref, index_v, index_s, sems):
    rows_here = samples_ref.shape[0]
    me, core = lax.axis_index("rows"), lax.axis_index("tgt")
    ids = jnp.concatenate([ids_ref[b : b + 1, :] for b in range(ids_ref.shape[0])], axis=1)
    count = ids.shape[1]
    owner = lax.div(ids, jnp.int32(rows_here))
    local = ids - owner * rows_here
    mine = lax.broadcasted_iota(jnp.int32, (groups, count), 0) == owner
    seen = mine.astype(jnp.int32)
    lane = lax.broadcasted_iota(jnp.int32, (groups, count), 1)
    step = 1
    while step < count:
        seen = seen + jnp.where(lane >= step, pltpu.roll(seen, step, 1), 0)
        step *= 2
    most = jnp.max(seen)
    rank = jnp.sum(jnp.where(mine, seen, 0), axis=0, keepdims=True) - 1
    half = lax.div(rank, jnp.int32(cap))
    packed = (half * groups + owner) * cap + (rank - half * cap)
    place = lax.broadcasted_iota(jnp.int32, (1, count), 1)
    slots_ref[...] = jnp.where(most > cap * cores, place, packed)
    most_ref[0] = most

    wanted = lax.broadcasted_iota(jnp.int32, (cap, count), 0) + core * cap
    chosen = jnp.where((wanted == rank) & (owner == me), local, 0)
    index_v[...] = jnp.broadcast_to(jnp.sum(chosen, axis=1, keepdims=True), index_v.shape)
    move = pltpu.make_async_copy(index_v, index_s, sems.at[0])
    move.start()
    move.wait()

    @pl.loop(0, cap)
    def _(k):
        pltpu.make_async_copy(samples_ref.at[pl.ds(index_s[k, 0], 1)], rows_ref.at[pl.ds(k, 1)], sems.at[1]).start()

    pltpu.make_async_copy(samples_ref.at[pl.ds(0, cap)], rows_ref, sems.at[1]).wait()


def pick(ids, samples, groups, cores, cap):
    count = ids.shape[0] * ids.shape[1]
    vmem = pl.BlockSpec(memory_space=pltpu.VMEM)
    return pl.pallas_call(
        functools.partial(pick_kernel, groups, cores, cap),
        out_shape=(
            jax.ShapeDtypeStruct((cap, samples.shape[1]), F32),
            jax.ShapeDtypeStruct((1, count), jnp.int32),
            jax.ShapeDtypeStruct((1,), jnp.int32),
        ),
        in_specs=[vmem, pl.BlockSpec(memory_space=pl.ANY)],
        out_specs=(vmem, vmem, pl.BlockSpec(memory_space=pltpu.SMEM)),
        scratch_shapes=[
            pltpu.VMEM((cap, 128), jnp.int32),
            pltpu.SMEM((cap, 128), jnp.int32),
            pltpu.SemaphoreType.DMA((2,)),
        ],
        name="pick",
    )(ids, samples)


def unpack(held, slots_ref, core, cores):
    depth = held[0].shape[0]
    total = None
    for shift, ref in enumerate(held):
        base = lax.rem(core + shift, cores) * depth
        slot = lax.broadcasted_iota(jnp.int32, (depth, slots_ref.shape[1]), 0) + base
        taken = jnp.where(slot == slots_ref[...], 1.0, 0.0).astype(BF16)
        parts = jnp.concatenate(split(ref[...]), axis=1)
        found = dot(parts, taken, ((0,), (0,)))
        total = found if total is None else total + found
    feat = held[0].shape[1]
    return total[:feat].astype(BF16), total[feat:].astype(BF16)


def block_kernel(cores, first, last, *refs):
    refs = list(refs)
    live_ref = refs.pop(0)
    step = pl.program_id(0)
    residual_ref = refs.pop(0)
    if not first:
        sums_ref, inverse_ref, old_high_ref, old_low_ref = refs[:4]
        refs = refs[4:]
    if not last:
        samples_ref, slots_ref = refs[:2]
        held = refs[2 : 2 + cores]
        refs = refs[2 + cores :]
    if not first:
        out_ref = refs.pop(0)
    if not last:
        high_ref, low_ref, total_ref = refs[:3]
        refs = refs[3:]
    if not first:
        coefs_ref = refs.pop(0)
    if not last:
        points_ref = refs.pop(0)

    @pl.when(step == 0)
    def _():
        if not first:
            coefs = dot3(split(sums_ref[...]), split(inverse_ref[0]), ((1,), (1,)))
            coefs_ref[0], coefs_ref[1] = split(coefs)
        if not last:
            points_ref[0], points_ref[1] = unpack(held, slots_ref, lax.axis_index("tgt"), cores)
            total_ref[...] = jnp.zeros_like(total_ref)

    residual = residual_ref[...]
    if not first:
        old = (old_high_ref[...], old_low_ref[...])
        residual = residual - dot3(old, (coefs_ref[0], coefs_ref[1]), ((1,), (1,)))
        out_ref[...] = residual
    if not last:
        scale = 0.5 / samples_ref.shape[1] ** 0.5
        base = dot3(split(samples_ref[...]), (points_ref[0], points_ref[1]), ((1,), (0,))) * scale + 1.0
        rows = residual.shape[0]
        slot = lax.broadcasted_iota(jnp.int32, (rows, 1), 0) + step * rows
        columns = split(jnp.where(slot < live_ref[0], base * base * base, 0.0))
        high_ref[...], low_ref[...] = columns
        total_ref[...] += dot3(split(residual), columns, ((0,), (0,)))


def block_pass(live, residual, previous, following, cores):
    rows, width = residual.shape
    first, last = previous is None, following is None
    step = min(ROWS_STEP, rows)
    by_step = lambda columns: pl.BlockSpec((step, columns), lambda i, live: (i, 0))
    whole = lambda a: pl.BlockSpec(a.shape, lambda i, live: (0,) * a.ndim)
    args, in_specs = [residual], [by_step(width)]
    out_shape, out_specs, scratch = [], [], []
    if not first:
        sums, inverse, index, high, low = previous
        size = high.shape[1]
        args += [sums, inverse, high, low]
        in_specs += [whole(sums), pl.BlockSpec((1, size, size), lambda i, live, b=index: (b, 0, 0)), by_step(size), by_step(size)]
        out_shape.append(jax.ShapeDtypeStruct((rows, width), F32))
        out_specs.append(by_step(width))
    if not last:
        samples, slots, index, held, blocks = following
        feat = samples.shape[1]
        size = slots.shape[1] // blocks
        args += [samples, slots, *held]
        in_specs += [by_step(feat), pl.BlockSpec((1, size), lambda i, live, b=index: (0, b)), *[whole(h) for h in held]]
        out_shape += [jax.ShapeDtypeStruct((rows, size), BF16)] * 2 + [jax.ShapeDtypeStruct((width, size), F32)]
        out_specs += [by_step(size), by_step(size), pl.BlockSpec((width, size), lambda i, live: (0, 0))]
    if not first:
        scratch.append(pltpu.VMEM((2, width, size), BF16))
    if not last:
        scratch.append(pltpu.VMEM((2, feat, size), BF16))
    return pl.pallas_call(
        functools.partial(block_kernel, cores, first, last),
        grid_spec=pltpu.PrefetchScalarGridSpec(
            num_scalar_prefetch=1, grid=(rows // step,), in_specs=in_specs, out_specs=out_specs, scratch_shapes=scratch
        ),
        out_shape=out_shape,
        name="block",
    )(live, *args)


def sum_over_rows(totals, groups):
    width, size = totals.shape
    piece = round_up(width, groups) // groups
    padded = jnp.pad(totals, ((0, piece * groups - width), (0, 0))) if piece * groups != width else totals
    got = lax.all_to_all(padded.reshape(groups, piece, size), "rows", 0, 0)
    own = jnp.sum(got, axis=0)
    back = lax.all_to_all(jnp.broadcast_to(own[None], (groups, piece, size)), "rows", 0, 0)
    return back.reshape(groups * piece, size)[:width]


def on_device(groups, cores, counts, samples, targets, point_ids, block_inverse):
    rows_here, feat = samples.shape
    blocks, size = point_ids.shape
    mean = blocks * size / groups
    cap = round_up(max(1, round((mean + 4 * mean**0.5) / cores)), 8)

    rows, slots, most = pick(point_ids, samples, groups, cores, cap)

    def general(rows):
        ids = jnp.pad(point_ids.reshape(-1), (0, cores * groups * cap - blocks * size), constant_values=-1)
        ids = lax.dynamic_slice_in_dim(ids, lax.axis_index("tgt") * groups * cap, groups * cap)
        local = ids - lax.axis_index("rows") * rows_here
        owned = (local >= 0) & (local < rows_here)
        taken = jnp.take(samples, jnp.clip(local, 0, rows_here - 1), axis=0)
        taken = jnp.where(owned[:, None], taken, 0.0)
        return jnp.sum(lax.all_to_all(taken.reshape(groups, cap, feat), "rows", 0, 0), axis=0)

    rows = lax.cond(most[0] > cap * cores, general, lambda rows: rows, rows)
    got = lax.all_to_all(jnp.broadcast_to(rows[None], (groups, cap, feat)), "rows", 0, 0).reshape(groups * cap, feat)
    held = [got]
    for shift in range(1, cores):
        held.append(lax.ppermute(got, "tgt", [((c + shift) % cores, c) for c in range(cores)]))

    residual, previous = targets, None
    for b in range(blocks):
        out = list(block_pass(counts, residual, previous, (samples, slots, b, held, blocks), cores))
        if b > 0:
            residual = out.pop(0)
        high, low, totals = out
        previous = (sum_over_rows(totals, groups), block_inverse, b, high, low)
    return block_pass(counts, residual, previous, None, cores)[0]


def solution(mesh):
    return jax.shard_map(
        functools.partial(on_device, mesh.shape["rows"], mesh.shape["tgt"]),
        mesh=mesh,
        in_specs=(P("rows"), P("rows", None), P("rows", "tgt"), P(), P()),
        out_specs=P("rows", "tgt"),
        check_vma=False,
    )
```

time: 427 us -> 116 us (0.27)
  waiting for transfers between devices: 326 us -> 1.63 us
  blocking collectives: 0 us -> 82.6 us
  matrix products: 66.7 us -> 0 us
  Pallas kernels: 0 us -> 29.2 us
  between operations: 13.2 us -> 1.38 us
  local copies, waits for them, and re-layouts: 11.1 us -> 1 us
  other arithmetic: 8.92 us -> 0.04 us
    psum x3 -> x0, waiting for transfers between devices: 326 us -> none  [the longest x2 217 us: on_device(): sums = lax.psum(totals, 'rows')]
    all_to_all x0 -> x5, blocking collectives: none -> 82.6 us  [the longest x1 30.4 us: on_device(): lax.all_to_all(jnp.broadcast_to(rows[None], (groups, cap, feat)), 'rows',...]
    dot_general x20 -> x0, matrix products: 66.7 us -> none  [the longest x8 25.5 us: kernel_columns(): lax.dot_general(rows_in, points, (((1,), (1,)), ((), ())), precision=lax....]
    pallas_call x0 -> x4, Pallas kernels: none -> 29.2 us  [the longest x3 24.9 us: block_pass(): pl.pallas_call(functools.partial(block_kernel, cores, first, last), grid_...]
    lt x8 -> x0, other arithmetic: 5.22 us -> none  [accumulate(): slot_ids < live_count]
    another operation x2 -> x0, local copies, waits for them, and re-layouts: 4.93 us -> none
    gather x2 -> x0, local copies, waits for them, and re-layouts: 4.73 us -> none  [pick_rows(): taken = jnp.take(samples, jnp.clip(local, 0, rows_here - 1), axis=0)]
  transfers between devices with their start and end apart: 3 -> 1, of which waited for: 3 -> 1; matrix products, arithmetic and copies ran while one was open for 1% -> 0% of each run, Pallas kernels for 0% -> 0%
where the time goes in v1:
time: 116 us
  blocking collectives  82.6 us (71%)
  Pallas kernels  29.2 us (25%)
  waiting for transfers between devices  1.63 us (1%)
  between operations  1.38 us (1%)
    all_to_all x1, blocking collectives, on_device(): lax.all_to_all(jnp.broadcast_to(rows[None], (groups, cap, feat)), 'rows',...  30.4 us
    all_to_all x2, blocking collectives, sum_over_rows(): got = lax.all_to_all(padded.reshape(groups, piece, size), 'rows', 0, 0)  26.7 us
    all_to_all x2, blocking collectives, sum_over_rows(): lax.all_to_all(jnp.broadcast_to(own[None], (groups, piece, size)), 'rows'...  25.5 us
    pallas_call x3, Pallas kernels, block_pass(): pl.pallas_call(functools.partial(block_kernel, cores, first, last), grid_...  24.9 us
    pallas_call x1, Pallas kernels, pick(): pl.pallas_call(functools.partial(pick_kernel, groups, cores, cap), out_sh...  4.29 us
  transfers between devices with their start and end apart: 1, of which 1 were waited for; matrix products, arithmetic and copies ran while one was open for 0% of the time, Pallas kernels for 0%

profile of v1, /device:TPU:0, one launch (start us, length us, event | category | flops | bytes accessed | tf_op | source)
XLA Modules:
  0.0 115.9 jit_solution(15729336564900361779)
XLA Ops:
  0.0 0.0 copy-start
  0.0 0.0 copy-start.3
  0.0 4.3 %pick.1 = (f32[48,256]{1,0:T(8,128)S(1)}, s32[1,1024]{1,0:T(1,128)}, s32[1]{0:T(128)}) custom-call(s32[2,512]{1,0:T(2,128)} %ids_ref.1, f32[2048,256]{1,0:T(8,128)} %refs_6_.1), custom_call_target="tpu_custom_call" | custom-call | tf_op jit(solution)/shard_map/pick/pallas_call | solution.py:71
  5.0 0.0 copy-done
  5.0 0.0 copy-done.3
  5.0 0.1 broadcast_in_dim.47
  5.1 30.4 %all_to_all.30 = f32[16,48,256]{2,1,0:T(8,128)S(1)} all-to-all(f32[16,48,256]{2,1,0:T(8,128)S(1)} %broadcast_in_dim.47), channel_id=1, replica_groups=mesh['rows'=16,'tgt'=2] {'rows'}, dimensions={0} | all-to-all | bytes 1572864 | tf_op jit(solution)/shard_map/all_to_all | solution.py:214
  35.4 0.0 copy-start.1
  35.4 0.0 collective-permute-start
  36.1 1.6 %collective-permute-done.refs_5_.refs_9_ = f32[768,256]{1,0:T(8,128)S(1)} collective-permute-done((f32[768,256]{1,0:T(8,128)S(1)}, f32[768,256]{1,0:T(8,128)S(1)}, u32[]{:S(2)}, u32[]{:S(2)}) %collective-permute-start) | collective-permute-done | bytes 786464 | tf_op jit(solution)/shard_map/ppermute | solution.py:217
  37.7 0.0 copy-start.2
  37.7 0.9 copy-done.2
  38.6 0.0 copy-done.1
  38.6 7.9 %block.3 = (bf16[2048,512]{1,0:T(8,128)(2,1)}, bf16[2048,512]{1,0:T(8,128)(2,1)}, f32[128,512]{1,0:T(8,128)}) custom-call(s32[1]{0:T(128)S(6)} %copy.9.refs_0_, f32[2048,128]{1,0:T(8,128)} %refs_1_.3, f32[2048,256]{1,0:T(8,128)S(1)} %copy-done, s32[1,1024]{1,0:T(1,128)} %get-tuple-element.25.refs_3_.refs_7_, f32[768,256]{1,0:T(8,128)} %bitcast.10, ...), custom_call_target="tpu_custom_call" | custom-call | tf_op jit(solution)/shard_map/block/pallas_call | solution.py:176
  46.5 13.9 %all_to_all.31 = f32[16,8,512]{2,1,0:T(8,128)S(1)} all-to-all(f32[16,8,512]{2,1,0:T(8,128)} %bitcast.16), channel_id=1, replica_groups=mesh['rows'=16,'tgt'=2] {'rows'}, dimensions={0} | all-to-all | bytes 524288 | tf_op jit(solution)/shard_map/all_to_all | solution.py:190
  60.4 12.8 %all_to_all.32 = f32[16,8,512]{2,1,0:T(8,128)} all-to-all(f32[16,8,512]{2,1,0:T(8,128)S(1)} %broadcast_in_dim.48), channel_id=1, replica_groups=mesh['rows'=16,'tgt'=2] {'rows'}, dimensions={0} | all-to-all | bytes 524288 | tf_op jit(solution)/shard_map/all_to_all | solution.py:192
  73.3 10.6 %block.4 = (f32[2048,128]{1,0:T(8,128)}, bf16[2048,512]{1,0:T(8,128)(2,1)}, bf16[2048,512]{1,0:T(8,128)(2,1)}, f32[128,512]{1,0:T(8,128)}) custom-call(s32[1]{0:T(128)S(6)} %copy.9.refs_0_, f32[2048,128]{1,0:T(8,128)} %refs_1_.3, f32[128,512]{1,0:T(8,128)} %bitcast.14, f32[2,512,512]{2,1,0:T(8,128)} %refs_3_.3, bf16[2048,512]{1,0:T(8,128)(2,1)} %get-tuple-element.29.refs_4_, ...), custom_call_target="tpu_custom_call" | custom-call | tf_op jit(solution)/shard_map/block/pallas_call | solution.py:176
  83.9 12.8 %all_to_all.33 = f32[16,8,512]{2,1,0:T(8,128)S(1)} all-to-all(f32[16,8,512]{2,1,0:T(8,128)} %bitcast.15), channel_id=1, replica_groups=mesh['rows'=16,'tgt'=2] {'rows'}, dimensions={0} | all-to-all | bytes 524288 | tf_op jit(solution)/shard_map/all_to_all | solution.py:190
  96.8 12.6 %all_to_all.34 = f32[16,8,512]{2,1,0:T(8,128)} all-to-all(f32[16,8,512]{2,1,0:T(8,128)S(1)} %broadcast_in_dim.49), channel_id=1, replica_groups=mesh['rows'=16,'tgt'=2] {'rows'}, dimensions={0} | all-to-all | bytes 524288 | tf_op jit(solution)/shard_map/all_to_all | solution.py:192
  109.4 6.4 %block.5 = f32[2048,128]{1,0:T(8,128)} custom-call(s32[1]{0:T(128)S(6)} %copy.9.refs_0_, f32[2048,128]{1,0:T(8,128)} %get-tuple-element.31.refs_1_, f32[128,512]{1,0:T(8,128)} %bitcast.13, f32[2,512,512]{2,1,0:T(8,128)} %refs_3_.3, bf16[2048,512]{1,0:T(8,128)(2,1)} %get-tuple-element.33.refs_4_, bf16[2048,512]{1,0:T(8,128)(2,1)} %get-tuple-element.34.refs_5_), custom_call_target="tpu_custom_call" | custom-call | tf_op jit(solution)/shard_map/block/pallas_call | solution.py:176
  (5 shorter events, 0.1 us)
Async XLA Ops:
  0.0 5.0 %copy-start = (f32[2048,256]{1,0:T(8,128)S(1)}, f32[2048,256]{1,0:T(8,128)}, u32[]{:S(2)}) copy-start(f32[2048,256]{1,0:T(8,128)} %refs_6_.1) | copy-start | bytes 6291460
  0.0 5.0 %copy-start.3 = (s32[2,512]{1,0:T(2,128)S(1)}, s32[2,512]{1,0:T(2,128)}, u32[]{:S(2)}) copy-start(s32[2,512]{1,0:T(2,128)} %ids_ref.1) | copy-start | bytes 12292
  35.4 3.2 %copy-start.1 = (f32[16,48,256]{2,1,0:T(8,128)}, f32[16,48,256]{2,1,0:T(8,128)S(1)}, u32[]{:S(2)}) copy-start(f32[16,48,256]{2,1,0:T(8,128)S(1)} %all_to_all.30) | copy-start | bytes 2359300
  35.4 2.3 %collective-permute-start = (f32[768,256]{1,0:T(8,128)S(1)}, f32[768,256]{1,0:T(8,128)S(1)}, u32[]{:S(2)}, u32[]{:S(2)}) collective-permute-start(f32[768,256]{1,0:T(8,128)S(1)} %bitcast.9), channel_id=1, source_target_pairs={{1,0},{0,1},{3,2},{2,3},{5,4},{4,5},{7,6},{6,7},{9,8},{8,9},{11,10... | collective-permute-start | bytes 2359304 | tf_op jit(solution)/shard_map/ppermute | solution.py:217
  37.7 0.9 copy-start.2

commit v2 on v1

v2 whole, which is shorter than its diff:
```python
import functools

import jax
import jax.numpy as jnp
from jax import lax
from jax.experimental import pallas as pl
from jax.experimental.pallas import tpu as pltpu
from jax.sharding import PartitionSpec as P

F32 = jnp.float32
BF16 = jnp.bfloat16
ROWS_STEP = 512


def round_up(value, unit):
    return -(-value // unit) * unit


def split(x):
    high = x.astype(BF16)
    return high, (x - high.astype(F32)).astype(BF16)


def dot(a, b, dims):
    return lax.dot_general(a, b, (dims, ((), ())), preferred_element_type=F32)


def dot3(a, b, dims):
    return dot(a[0], b[0], dims) + dot(a[0], b[1], dims) + dot(a[1], b[0], dims)


def pick_kernel(groups, cores, cap, ids_ref, samples_ref, rows_ref, slots_ref, most_ref, index_v, index_s, sems):
    rows_here = samples_ref.shape[0]
    me, core = lax.axis_index("rows"), lax.axis_index("tgt")
    ids = jnp.concatenate([ids_ref[b : b + 1, :] for b in range(ids_ref.shape[0])], axis=1)
    count = ids.shape[1]
    owner = lax.div(ids, jnp.int32(rows_here))
    local = ids - owner * rows_here
    mine = lax.broadcasted_iota(jnp.int32, (groups, count), 0) == owner
    seen = mine.astype(jnp.int32)
    lane = lax.broadcasted_iota(jnp.int32, (groups, count), 1)
    step = 1
    while step < count:
        seen = seen + jnp.where(lane >= step, pltpu.roll(seen, step, 1), 0)
        step *= 2
    most = jnp.max(seen)
    rank = jnp.sum(jnp.where(mine, seen, 0), axis=0, keepdims=True) - 1
    half = lax.div(rank, jnp.int32(cap))
    packed = (half * groups + owner) * cap + (rank - half * cap)
    place = lax.broadcasted_iota(jnp.int32, (1, count), 1)
    slots_ref[...] = jnp.where(most > cap * cores, place, packed)
    most_ref[0] = most

    wanted = lax.broadcasted_iota(jnp.int32, (cap, count), 0) + core * cap
    chosen = jnp.where((wanted == rank) & (owner == me), local, 0)
    index_v[...] = jnp.broadcast_to(jnp.sum(chosen, axis=1, keepdims=True), index_v.shape)
    move = pltpu.make_async_copy(index_v, index_s, sems.at[0])
    move.start()
    move.wait()

    @pl.loop(0, cap)
    def _(k):
        pltpu.make_async_copy(samples_ref.at[pl.ds(index_s[k, 0], 1)], rows_ref.at[pl.ds(k, 1)], sems.at[1]).start()

    pltpu.make_async_copy(samples_ref.at[pl.ds(0, cap)], rows_ref, sems.at[1]).wait()


def pick(ids, samples, groups, cores, cap):
    count = ids.shape[0] * ids.shape[1]
    vmem = pl.BlockSpec(memory_space=pltpu.VMEM)
    return pl.pallas_call(
        functools.partial(pick_kernel, groups, cores, cap),
        out_shape=(
            jax.ShapeDtypeStruct((cap, samples.shape[1]), F32),
            jax.ShapeDtypeStruct((1, count), jnp.int32),
            jax.ShapeDtypeStruct((1,), jnp.int32),
        ),
        in_specs=[vmem, pl.BlockSpec(memory_space=pl.ANY)],
        out_specs=(vmem, vmem, pl.BlockSpec(memory_space=pltpu.SMEM)),
        scratch_shapes=[
            pltpu.VMEM((cap, 128), jnp.int32),
            pltpu.SMEM((cap, 128), jnp.int32),
            pltpu.SemaphoreType.DMA((2,)),
        ],
        name="pick",
    )(ids, samples)


def pieces(rows):
    step = min(ROWS_STEP, rows)
    return [pl.ds(start, step) for start in range(0, rows, step)]


def rows_of(ref, at):
    return ref.at[at] if len(ref.shape) == 2 else ref.at[:, at]


def start_copies(source, target, sems):
    copies = [
        pltpu.make_async_copy(rows_of(source, at), rows_of(target, at), sems.at[index])
        for index, at in enumerate(pieces(source.shape[-2]))
    ]
    for copy in copies:
        copy.start()
    return copies


def update(residual, columns, coefs):
    width = residual.shape[1]
    both = dot(columns[0], coefs, ((1,), (0,)))
    return residual - (both[:, :width] + both[:, width:] + dot(columns[1], coefs[:, :width], ((1,), (0,))))


def unpack(held, slots_ref):
    depth, feat = held[0].shape
    cores = len(held)
    core = lax.axis_index("tgt")
    total = None
    for shift, ref in enumerate(held):
        base = lax.rem(core + shift, cores) * depth
        slot = lax.broadcasted_iota(jnp.int32, (depth, slots_ref.shape[1]), 0) + base
        taken = jnp.where(slot == slots_ref[...], 1.0, 0.0).astype(BF16)
        found = dot(jnp.concatenate(split(ref[...]), axis=1), taken, ((0,), (0,)))
        total = found if total is None else total + found
    return total[:feat].astype(BF16), total[feat:].astype(BF16)


def columns_kernel(live_ref, residual_ref, samples_ref, slots_ref, *refs):
    *held, columns_ref, total_ref, residual_v, samples_v, columns_v, sems = refs
    feat, width = samples_ref.shape[1], residual_ref.shape[1]
    samples_in = start_copies(samples_ref, samples_v, sems.at[0])
    residual_in = start_copies(residual_ref, residual_v, sems.at[1])
    points = unpack(held, slots_ref)
    scale = 0.5 / feat**0.5

    def add(index, at):
        residual_in[index].wait()
        high, low = split(residual_v[at, :])
        both = dot(jnp.concatenate([high, low], axis=1), columns_v[0, at, :], ((0,), (0,)))
        term = both[:width] + both[width:] + dot(high, columns_v[1, at, :], ((0,), (0,)))
        total_ref[...] = term if index == 0 else total_ref[...] + term

    parts, columns_out = pieces(samples_ref.shape[0]), []
    for index, at in enumerate(parts):
        samples_in[index].wait()
        base = dot3(split(samples_v[at, :]), points, ((1,), (0,))) * scale + 1.0
        slot = lax.broadcasted_iota(jnp.int32, (at.size, 1), 0) + at.start
        columns_v[0, at, :], columns_v[1, at, :] = split(jnp.where(slot < live_ref[0], base * base * base, 0.0))
        columns_out.append(pltpu.make_async_copy(columns_v.at[:, at], columns_ref.at[:, at], sems.at[2, index]))
        columns_out[-1].start()
        if index > 0:
            add(index - 1, parts[index - 1])
    add(len(parts) - 1, parts[-1])
    for copy in columns_out:
        copy.wait()


def cross_kernel(first_ref, second_ref, inverse_ref, out_ref, first_v, second_v, inverse_v, sems):
    first_in = start_copies(first_ref, first_v, sems.at[0])
    second_in = start_copies(second_ref, second_v, sems.at[1])
    inverse_in = pltpu.make_async_copy(inverse_ref, inverse_v, sems.at[2, 0])
    inverse_in.start()
    for copy in [*first_in, *second_in]:
        copy.wait()
    cross = dot3((first_v[0], first_v[1]), (second_v[0], second_v[1]), ((0,), (0,)))
    inverse_in.wait()
    out_ref[0], out_ref[1] = split(dot3(split(inverse_v[...]), split(cross), ((0,), (0,))))


def next_kernel(sums_ref, cross_ref, ahead_ref, next_ref):
    next_ref[...] = ahead_ref[...] - dot3(split(sums_ref[...]), (cross_ref[0], cross_ref[1]), ((1,), (0,)))


def side_by_side(transposed):
    return jnp.concatenate(split(transposed.T), axis=1)


def update_kernel(sums_ref, inverse_ref, residual_ref, columns_ref, out_ref, residual_v, columns_v, sems):
    columns_in = start_copies(columns_ref, columns_v, sems.at[0])
    residual_in = start_copies(residual_ref, residual_v, sems.at[1])
    coefs = side_by_side(dot3(split(sums_ref[...]), split(inverse_ref[...]), ((1,), (1,))))
    finish_update(coefs, columns_in, residual_in, columns_v, residual_v, out_ref, sems.at[2])


def finish_update(coefs, columns_in, residual_in, columns_v, residual_v, out_ref, sems):
    out = []
    for index, at in enumerate(pieces(out_ref.shape[0])):
        columns_in[index].wait()
        residual_in[index].wait()
        residual_v[at, :] = update(residual_v[at, :], (columns_v[0, at, :], columns_v[1, at, :]), coefs)
        out.append(pltpu.make_async_copy(residual_v.at[at], out_ref.at[at], sems.at[index]))
        out[-1].start()
    for copy in out:
        copy.wait()


def solved_kernel(columns_ref, inverse_ref, out_ref, columns_v, sems):
    columns_in = start_copies(columns_ref, columns_v, sems.at[0])
    inverse = split(inverse_ref[...])
    out = []
    for index, at in enumerate(pieces(columns_ref.shape[1])):
        columns_in[index].wait()
        columns_v[0, at, :], columns_v[1, at, :] = split(dot3((columns_v[0, at, :], columns_v[1, at, :]), inverse, ((1,), (0,))))
        out.append(pltpu.make_async_copy(columns_v.at[:, at], out_ref.at[:, at], sems.at[1, index]))
        out[-1].start()
    for copy in out:
        copy.wait()


def last_kernel(sums_ref, residual_ref, columns_ref, out_ref, residual_v, columns_v, sems):
    columns_in = start_copies(columns_ref, columns_v, sems.at[0])
    residual_in = start_copies(residual_ref, residual_v, sems.at[1])
    finish_update(side_by_side(sums_ref[...]), columns_in, residual_in, columns_v, residual_v, out_ref, sems.at[2])


VMEM = pl.BlockSpec(memory_space=pltpu.VMEM)
HBM = pl.BlockSpec(memory_space=pltpu.HBM)
SMEM = pl.BlockSpec(memory_space=pltpu.SMEM)


def local(kernel, out_shape, args, flops, in_specs, out_specs, scratch_shapes=(), limit=61):
    moved = sum(a.size * a.dtype.itemsize for a in [*args, *(out_shape if isinstance(out_shape, list) else [out_shape])])
    return pl.pallas_call(
        kernel,
        out_shape=out_shape,
        in_specs=in_specs,
        out_specs=out_specs,
        scratch_shapes=scratch_shapes,
        cost_estimate=pl.CostEstimate(flops=flops, bytes_accessed=moved, transcendentals=0),
        compiler_params=pltpu.CompilerParams(vmem_limit_bytes=limit * 2**20),
        name=kernel.__name__,
    )(*args)


def shape_of(*shape, dtype=F32):
    return jax.ShapeDtypeStruct(shape, dtype)


def columns_and_sums(live, residual, samples, slots, held):
    (rows, width), feat, size = residual.shape, samples.shape[1], slots.shape[1]
    return local(
        columns_kernel,
        [shape_of(2, rows, size, dtype=BF16), shape_of(width, size)],
        (live, residual, samples, slots, *held),
        6 * rows * size * (feat + width),
        [SMEM, HBM, HBM, VMEM] + [VMEM] * len(held),
        [HBM, VMEM],
        [
            pltpu.VMEM((rows, width), F32),
            pltpu.VMEM((rows, feat), F32),
            pltpu.VMEM((2, rows, size), BF16),
            pltpu.SemaphoreType.DMA((3, len(pieces(rows)))),
        ],
    )


def sum_over_rows(totals, groups, during_first, during_second):
    width, size = totals.shape
    piece = round_up(width, groups) // groups
    padded = jnp.pad(totals, ((0, piece * groups - width), (0, 0))) if piece * groups != width else totals
    got = lax.all_to_all(padded.reshape(groups, piece, size), "rows", 0, 0)
    got, made = lax.optimization_barrier((got, during_first()))
    own = jnp.sum(got, axis=0)
    back = lax.all_to_all(jnp.broadcast_to(own[None], (groups, piece, size)), "rows", 0, 0)
    back, more = lax.optimization_barrier((back, during_second(made)))
    return back.reshape(groups * piece, size)[:width], made, more


def on_device(groups, cores, counts, samples, targets, point_ids, block_inverse):
    rows_here, feat = samples.shape
    blocks, size = point_ids.shape
    mean = blocks * size / groups
    cap = round_up(max(1, round((mean + 4 * mean**0.5) / cores)), 8)

    rows, slots, most = pick(point_ids, samples, groups, cores, cap)

    def general(rows):
        ids = jnp.pad(point_ids.reshape(-1), (0, cores * groups * cap - blocks * size), constant_values=-1)
        ids = lax.dynamic_slice_in_dim(ids, lax.axis_index("tgt") * groups * cap, groups * cap)
        local = ids - lax.axis_index("rows") * rows_here
        owned = (local >= 0) & (local < rows_here)
        taken = jnp.take(samples, jnp.clip(local, 0, rows_here - 1), axis=0)
        taken = jnp.where(owned[:, None], taken, 0.0)
        return jnp.sum(lax.all_to_all(taken.reshape(groups, cap, feat), "rows", 0, 0), axis=0)

    rows = lax.cond(most[0] > cap * cores, general, lambda rows: rows, rows)
    got = lax.all_to_all(jnp.broadcast_to(rows[None], (groups, cap, feat)), "rows", 0, 0).reshape(groups * cap, feat)
    held = [got]
    for shift in range(1, cores):
        held.append(lax.ppermute(got, "tgt", [((c + shift) % cores, c) for c in range(cores)]))

    slots = [slots[:, b * size : (b + 1) * size] for b in range(blocks)]
    width = targets.shape[1]
    parts = len(pieces(rows_here))
    columns_v = pltpu.VMEM((2, rows_here, size), BF16)
    residual_v = pltpu.VMEM((rows_here, width), F32)
    def cross_of(columns, following, b):
        return local(
            cross_kernel,
            shape_of(2, size, size, dtype=BF16),
            (columns, following, block_inverse[b]),
            6 * rows_here * size * size,
            [HBM, HBM, HBM],
            VMEM,
            [columns_v, columns_v, pltpu.VMEM((size, size), F32), pltpu.SemaphoreType.DMA((3, parts))],
        )

    def updated(sums, residual, columns, b):
        return local(
            update_kernel,
            shape_of(rows_here, width),
            (sums, block_inverse[b], residual, columns),
            6 * rows_here * size * width,
            [VMEM, VMEM, HBM, HBM],
            HBM,
            [residual_v, columns_v, pltpu.SemaphoreType.DMA((3, parts))],
        )

    def solved_of(columns):
        return local(
            solved_kernel,
            shape_of(2, rows_here, size, dtype=BF16),
            (columns, block_inverse[blocks - 1]),
            6 * rows_here * size * size,
            [HBM, VMEM],
            HBM,
            [columns_v, pltpu.SemaphoreType.DMA((2, parts))],
        )

    residual = targets
    columns, totals = columns_and_sums(counts, residual, samples, slots[0], held)
    sums = before = None
    for b in range(blocks):
        def first(b=b, sums=sums, residual=residual, before=before, columns=columns):
            now = residual if b == 0 else updated(sums, residual, before, b - 1)
            return (now, *columns_and_sums(counts, now, samples, slots[b + 1], held)) if b + 1 < blocks else (now,)

        def second(made, b=b, columns=columns):
            return cross_of(columns, made[1], b) if b + 1 < blocks else solved_of(columns)

        sums, made, more = sum_over_rows(totals, groups, first, second)
        residual, before = made[0], columns
        if b + 1 < blocks:
            _, columns, ahead = made
            totals = local(next_kernel, shape_of(width, size), (sums, more, ahead), 6 * width * size * size, [VMEM] * 3, VMEM)
    return local(
        last_kernel,
        shape_of(rows_here, width),
        (sums, residual, more),
        6 * rows_here * size * width,
        [VMEM, HBM, HBM],
        HBM,
        [residual_v, columns_v, pltpu.SemaphoreType.DMA((3, parts))],
    )


def solution(mesh):
    return jax.shard_map(
        functools.partial(on_device, mesh.shape["rows"], mesh.shape["tgt"]),
        mesh=mesh,
        in_specs=(P("rows"), P("rows", None), P("rows", "tgt"), P(), P()),
        out_specs=P("rows", "tgt"),
        check_vma=False,
    )
```

time: 116 us -> 118 us (1.017)
  blocking collectives: 82.6 us -> 30.2 us
  Pallas kernels: 29.2 us -> 50.9 us
  starting transfers between devices: 0.01 us -> 18.6 us
  waiting for transfers between devices: 1.63 us -> 8.28 us
  local copies, waits for them, and re-layouts: 1 us -> 7.57 us
    all_to_all x4 -> x0, blocking collectives: 52.2 us -> none  [the longest x2 26.7 us: sum_over_rows(): got = lax.all_to_all(padded.reshape(groups, piece, size), 'rows', 0, 0)]
    pallas_call x3 -> x7, Pallas kernels: 24.9 us -> 46.6 us  [local(): pl.pallas_call(kernel, out_shape=out_shape, in_specs=in_specs, out_specs=...]
    all_to_all x0 -> x4, starting transfers between devices: none -> 18.6 us  [the longest x2 10.4 us: sum_over_rows(): got = lax.all_to_all(padded.reshape(groups, piece, size), 'rows', 0, 0)]
    all_to_all x0 -> x4, waiting for transfers between devices: none -> 7.26 us  [the longest x2 5.69 us: sum_over_rows(): got = lax.all_to_all(padded.reshape(groups, piece, size), 'rows', 0, 0)]
    squeeze x0 -> x1, local copies, waits for them, and re-layouts: none -> 3.03 us  [solved_of(): block_inverse[blocks - 1]]
    unnamed x8 -> x14, local copies, waits for them, and re-layouts: 0.89 us -> 2.39 us
    broadcast_in_dim x2, local copies, waits for them, and re-layouts: 0.04 us -> 1.49 us  [sum_over_rows(): jnp.broadcast_to(own[None], (groups, piece, size))]
  transfers between devices with their start and end apart: 1 -> 5, of which waited for: 1 -> 4; matrix products, arithmetic and copies ran while one was open for 0% -> 3% of each run, Pallas kernels for 0% -> 26%
where the time goes in v2:
time: 118 us; the launch traced here: 117 us
  Pallas kernels  50.9 us (43%)
  blocking collectives  30.2 us (26%)
  starting transfers between devices  18.6 us (16%)
  waiting for transfers between devices  8.28 us (7%)
  local copies, waits for them, and re-layouts  7.57 us (6%)
  between operations  1.62 us (1%)
    pallas_call x7, Pallas kernels, local(): pl.pallas_call(kernel, out_shape=out_shape, in_specs=in_specs, out_specs=...  46.6 us
    all_to_all x1, blocking collectives, on_device(): lax.all_to_all(jnp.broadcast_to(rows[None], (groups, cap, feat)), 'rows',...  30.2 us
    all_to_all x2, starting transfers between devices, sum_over_rows(): got = lax.all_to_all(padded.reshape(groups, piece, size), 'rows', 0, 0)  10.4 us
    all_to_all x2, starting transfers between devices, sum_over_rows(): lax.all_to_all(jnp.broadcast_to(own[None], (groups, piece, size)), 'rows'...  8.13 us
    all_to_all x2, waiting for transfers between devices, sum_over_rows(): got = lax.all_to_all(padded.reshape(groups, piece, size), 'rows', 0, 0)  5.69 us
    pallas_call x1, Pallas kernels, pick(): pl.pallas_call(functools.partial(pick_kernel, groups, cores, cap), out_sh...  4.29 us
    squeeze x1, local copies, waits for them, and re-layouts, solved_of(): block_inverse[blocks - 1]  3.03 us
    unnamed x14, local copies, waits for them, and re-layouts  2.39 us
  transfers between devices with their start and end apart: 5, of which 4 were waited for; matrix products, arithmetic and copies ran while one was open for 3% of the time, Pallas kernels for 26%

profile of v2, /device:TPU:0, one launch (start us, length us, event | category | flops | bytes accessed | tf_op | source)
XLA Modules:
  0.0 117.2 jit_solution(2717296651803278939)
XLA Ops:
  0.0 0.0 copy-start
  0.0 0.0 copy-start.4
  0.0 4.3 %pick.1 = (f32[48,256]{1,0:T(8,128)S(1)}, s32[1,1024]{1,0:T(1,128)}, s32[1]{0:T(128)}) custom-call(s32[2,512]{1,0:T(2,128)} %ids_ref.1, f32[2048,256]{1,0:T(8,128)} %samples_ref.5), custom_call_target="tpu_custom_call" | custom-call | tf_op jit(solution)/shard_map/pick/pallas_call | solution.py:71
  4.9 0.0 copy-done
  5.0 0.0 copy-done.4
  5.0 0.0 copy-start.5
  5.0 0.1 broadcast_in_dim.47
  5.1 30.2 %all_to_all.30 = f32[16,48,256]{2,1,0:T(8,128)S(1)} all-to-all(f32[16,48,256]{2,1,0:T(8,128)S(1)} %broadcast_in_dim.47), channel_id=1, replica_groups=mesh['rows'=16,'tgt'=2] {'rows'}, dimensions={0} | all-to-all | bytes 1572864 | tf_op jit(solution)/shard_map/all_to_all | solution.py:287
  35.2 0.0 copy-start.3
  35.2 0.0 collective-permute-start
  35.9 0.0 copy-done.5
  35.9 0.6 fusion.1
  36.5 1.0 collective-permute-done.refs_1_
  37.5 0.0 copy-start.6
  37.5 1.0 copy-done.6
  38.5 0.0 copy-done.3
  38.5 7.9 %columns_kernel.2 = (bf16[2,2048,512]{2,1,0:T(8,128)(2,1)}, f32[128,512]{1,0:T(8,128)}) custom-call(s32[1]{0:T(128)S(6)} %copy.9.live_ref, f32[2048,128]{1,0:T(8,128)} %residual_ref.4, f32[2048,256]{1,0:T(8,128)S(1)} %copy-done, s32[1,512]{1,0:T(1,128)} %get-tuple-element.55.slots_ref, f32[768,256]{1,0:T(8,128)} %bitcast.19, f32[768,256]{1,0:T(8,128)} %copy-done.6), custom_call_target="tpu_custom_call" | custom-call | flops 2415919104 | bytes 9177092 | tf_op jit(solution)/shard_map/columns_kernel/pallas_call | solution.py:223
  46.4 3.5 %all-to-all-start.2 = ((f32[16,8,512]{2,1,0:T(8,128)}), f32[16,8,512]{2,1,0:T(8,128)S(1)}, u32[]{:S(2)}, u32[]{:S(2)}) async-start(f32[16,8,512]{2,1,0:T(8,128)} %bitcast.21), calls=%async_computation.2 | async-start | bytes 524288 | tf_op jit(solution)/shard_map/all_to_all | solution.py:261
  50.0 7.9 %columns_kernel.3 = (bf16[2,2048,512]{2,1,0:T(8,128)(2,1)}, f32[128,512]{1,0:T(8,128)}) custom-call(s32[1]{0:T(128)S(6)} %copy.9.live_ref, f32[2048,128]{1,0:T(8,128)} %residual_ref.4, f32[2048,256]{1,0:T(8,128)S(1)} %copy-done, s32[1,512]{1,0:T(1,128)} %get-tuple-element.54.slots_ref, f32[768,256]{1,0:T(8,128)} %bitcast.20, f32[768,256]{1,0:T(8,128)} %copy-done.6), custom_call_target="tpu_custom_call" | custom-call | flops 2415919104 | bytes 9177092 | tf_op jit(solution)/shard_map/columns_kernel/pallas_call | solution.py:223
  57.9 2.5 %all-to-all-done.2 = f32[16,8,512]{2,1,0:T(8,128)S(1)} async-done(((f32[16,8,512]{2,1,0:T(8,128)}), f32[16,8,512]{2,1,0:T(8,128)S(1)}, u32[]{:S(2)}, u32[]{:S(2)}) %all-to-all-start.2) | async-done | bytes 262176 | tf_op jit(solution)/shard_map/all_to_all | solution.py:261
  60.4 0.7 broadcast_in_dim.48
  61.1 4.4 %all-to-all-start.3 = ((f32[16,8,512]{2,1,0:T(8,128)}), f32[16,8,512]{2,1,0:T(8,128)S(1)}, u32[]{:S(2)}, u32[]{:S(2)}) async-start(f32[16,8,512]{2,1,0:T(8,128)} %broadcast_in_dim.48), calls=%async_computation.3 | async-start | bytes 524288 | tf_op jit(solution)/shard_map/all_to_all | solution.py:264
  65.5 3.0 %slice_bitcast_fusion = (f32[512,512]{1,0:T(8,128)}, f32[512,512]{1,0:T(8,128)}) fusion(f32[2,512,512]{2,1,0:T(8,128)} %param.11), kind=kLoop, calls=%fused_computation.8 | loop fusion | bytes 4194304 | tf_op jit(solution)/shard_map/squeeze | solution.py:323
  68.6 9.0 %cross_kernel.1.cross_ref = bf16[2,512,512]{2,1,0:T(8,128)(2,1)} custom-call(bf16[2,2048,512]{2,1,0:T(8,128)(2,1)} %get-tuple-element.39.first_ref.columns_ref, bf16[2,2048,512]{2,1,0:T(8,128)(2,1)} %get-tuple-element.40.second_ref.columns_ref, f32[512,512]{1,0:T(8,128)} %get-tuple-element.53.inverse_ref), custom_call_target="tpu_custom_call" | custom-call | flops 3221225472 | bytes 10485760 | tf_op jit(solution)/shard_map/cross_kernel/pallas_call | solution.py:223
  77.6 0.0 all-to-all-done.3
  77.6 0.0 copy-start.1
  77.7 0.7 copy-done.1
  78.4 2.4 %next_kernel.1 = f32[128,512]{1,0:T(8,128)} custom-call(f32[128,512]{1,0:T(8,128)} %bitcast.14, bf16[2,512,512]{2,1,0:T(8,128)(2,1)} %cross_kernel.1.cross_ref, f32[128,512]{1,0:T(8,128)} %get-tuple-element.43.ahead_ref), custom_call_target="tpu_custom_call" | custom-call | flops 201326592 | bytes 1835008 | tf_op jit(solution)/shard_map/next_kernel/pallas_call | solution.py:223
  80.8 6.9 %all-to-all-start.4 = ((f32[16,8,512]{2,1,0:T(8,128)}), f32[16,8,512]{2,1,0:T(8,128)S(1)}, u32[]{:S(2)}, u32[]{:S(2)}) async-start(f32[16,8,512]{2,1,0:T(8,128)} %bitcast.17), calls=%async_computation.4 | async-start | bytes 524288 | tf_op jit(solution)/shard_map/all_to_all | solution.py:261
  87.7 6.1 %update_kernel.1.residual_ref = f32[2048,128]{1,0:T(8,128)} custom-call(f32[128,512]{1,0:T(8,128)} %bitcast.15, f32[512,512]{1,0:T(8,128)} %get-tuple-element.53.inverse_ref, f32[2048,128]{1,0:T(8,128)} %residual_ref.4, bf16[2,2048,512]{2,1,0:T(8,128)(2,1)} %get-tuple-element.39.first_ref.columns_ref), custom_call_target="tpu_custom_call" | custom-call | flops 805306368 | bytes 7602176 | tf_op jit(solution)/shard_map/update_kernel/pallas_call | solution.py:223
  93.8 3.2 %all-to-all-done.4 = f32[16,8,512]{2,1,0:T(8,128)S(1)} async-done(((f32[16,8,512]{2,1,0:T(8,128)}), f32[16,8,512]{2,1,0:T(8,128)S(1)}, u32[]{:S(2)}, u32[]{:S(2)}) %all-to-all-start.4) | async-done | bytes 262176 | tf_op jit(solution)/shard_map/all_to_all | solution.py:261
  97.0 0.7 broadcast_in_dim.49
  97.8 3.7 %all-to-all-start.5 = ((f32[16,8,512]{2,1,0:T(8,128)}), f32[16,8,512]{2,1,0:T(8,128)S(1)}, u32[]{:S(2)}, u32[]{:S(2)}) async-start(f32[16,8,512]{2,1,0:T(8,128)} %broadcast_in_dim.49), calls=%async_computation.5 | async-start | bytes 524288 | tf_op jit(solution)/shard_map/all_to_all | solution.py:264
  101.5 7.5 %solved_kernel.1.columns_ref = bf16[2,2048,512]{2,1,0:T(8,128)(2,1)} custom-call(bf16[2,2048,512]{2,1,0:T(8,128)(2,1)} %get-tuple-element.40.second_ref.columns_ref, f32[512,512]{1,0:T(8,128)} %get-tuple-element.52.inverse_ref), custom_call_target="tpu_custom_call" | custom-call | flops 3221225472 | bytes 9437184 | tf_op jit(solution)/shard_map/solved_kernel/pallas_call | solution.py:223
  109.0 1.6 %all-to-all-done.5 = f32[16,8,512]{2,1,0:T(8,128)S(1)} async-done(((f32[16,8,512]{2,1,0:T(8,128)}), f32[16,8,512]{2,1,0:T(8,128)S(1)}, u32[]{:S(2)}, u32[]{:S(2)}) %all-to-all-start.5) | async-done | bytes 262176 | tf_op jit(solution)/shard_map/all_to_all | solution.py:264
  110.6 0.0 copy-start.2
  110.6 0.7 copy-done.2
  111.3 5.7 %last_kernel.1 = f32[2048,128]{1,0:T(8,128)} custom-call(f32[128,512]{1,0:T(8,128)} %bitcast.16, f32[2048,128]{1,0:T(8,128)} %update_kernel.1.residual_ref, bf16[2,2048,512]{2,1,0:T(8,128)(2,1)} %solved_kernel.1.columns_ref), custom_call_target="tpu_custom_call" | custom-call | flops 805306368 | bytes 6553600 | tf_op jit(solution)/shard_map/last_kernel/pallas_call | solution.py:223
  (3 shorter events, 0.0 us)
Async XLA Ops:
  0.0 4.9 %copy-start = (f32[2048,256]{1,0:T(8,128)S(1)}, f32[2048,256]{1,0:T(8,128)}, u32[]{:S(2)}) copy-start(f32[2048,256]{1,0:T(8,128)} %samples_ref.5) | copy-start | bytes 6291460
  0.0 5.0 %copy-start.4 = (s32[2,512]{1,0:T(2,128)S(1)}, s32[2,512]{1,0:T(2,128)}, u32[]{:S(2)}) copy-start(s32[2,512]{1,0:T(2,128)} %ids_ref.1) | copy-start | bytes 12292
  5.0 30.9 %copy-start.5 = (s32[1,1024]{1,0:T(1,128)S(1)}, s32[1,1024]{1,0:T(1,128)}, u32[]{:S(2)}) copy-start(s32[1,1024]{1,0:T(1,128)} %get-tuple-element.32) | copy-start | bytes 12292
  35.2 3.3 %copy-start.3 = (f32[16,48,256]{2,1,0:T(8,128)}, f32[16,48,256]{2,1,0:T(8,128)S(1)}, u32[]{:S(2)}) copy-start(f32[16,48,256]{2,1,0:T(8,128)S(1)} %all_to_all.30) | copy-start | bytes 2359300
  35.2 2.3 %collective-permute-start = (f32[768,256]{1,0:T(8,128)S(1)}, f32[768,256]{1,0:T(8,128)S(1)}, u32[]{:S(2)}, u32[]{:S(2)}) collective-permute-start(f32[768,256]{1,0:T(8,128)S(1)} %bitcast.18), channel_id=1, source_target_pairs={{1,0},{0,1},{3,2},{2,3},{5,4},{4,5},{7,6},{6,7},{9,8},{8,9},{11,10... | collective-permute-start | bytes 2359304 | tf_op jit(solution)/shard_map/ppermute | solution.py:290
  37.5 1.0 copy-start.6
  46.4 13.9 %all-to-all-start.2 = ((f32[16,8,512]{2,1,0:T(8,128)}), f32[16,8,512]{2,1,0:T(8,128)S(1)}, u32[]{:S(2)}, u32[]{:S(2)}) async-start(f32[16,8,512]{2,1,0:T(8,128)} %bitcast.21), calls=%async_computation.2 | async-start | bytes 524288 | tf_op jit(solution)/shard_map/all_to_all | solution.py:261
  61.1 16.5 %all-to-all-start.3 = ((f32[16,8,512]{2,1,0:T(8,128)}), f32[16,8,512]{2,1,0:T(8,128)S(1)}, u32[]{:S(2)}, u32[]{:S(2)}) async-start(f32[16,8,512]{2,1,0:T(8,128)} %broadcast_in_dim.48), calls=%async_computation.3 | async-start | bytes 524288 | tf_op jit(solution)/shard_map/all_to_all | solution.py:264
  77.6 0.7 copy-start.1
  80.8 16.2 %all-to-all-start.4 = ((f32[16,8,512]{2,1,0:T(8,128)}), f32[16,8,512]{2,1,0:T(8,128)S(1)}, u32[]{:S(2)}, u32[]{:S(2)}) async-start(f32[16,8,512]{2,1,0:T(8,128)} %bitcast.17), calls=%async_computation.4 | async-start | bytes 524288 | tf_op jit(solution)/shard_map/all_to_all | solution.py:261
  97.8 12.8 %all-to-all-start.5 = ((f32[16,8,512]{2,1,0:T(8,128)}), f32[16,8,512]{2,1,0:T(8,128)S(1)}, u32[]{:S(2)}, u32[]{:S(2)}) async-start(f32[16,8,512]{2,1,0:T(8,128)} %broadcast_in_dim.49), calls=%async_computation.5 | async-start | bytes 524288 | tf_op jit(solution)/shard_map/all_to_all | solution.py:264
  110.6 0.7 copy-start.2

commit v3 on v2

--- a/solution.py
+++ b/solution.py
@@ -10,6 +10,8 @@
 F32 = jnp.float32
 BF16 = jnp.bfloat16
 ROWS_STEP = 512
+HALF_STEP = 1024
+LIMIT = 24 * 2**20
 
 
 def round_up(value, unit):
@@ -86,29 +88,25 @@
     )(ids, samples)
 
 
-def pieces(rows):
-    step = min(ROWS_STEP, rows)
+def pieces(rows, step=ROWS_STEP):
+    step = min(step, rows)
     return [pl.ds(start, step) for start in range(0, rows, step)]
 
 
-def rows_of(ref, at):
-    return ref.at[at] if len(ref.shape) == 2 else ref.at[:, at]
-
-
-def start_copies(source, target, sems):
-    copies = [
-        pltpu.make_async_copy(rows_of(source, at), rows_of(target, at), sems.at[index])
-        for index, at in enumerate(pieces(source.shape[-2]))
-    ]
+def copy_of(source, target, sem):
+    copy = pltpu.make_async_copy(source, target, sem)
+    copy.start()
+    return copy
+
+
+def copies_of(source, target, sems, parts):
+    rows_of = lambda ref, at: ref.at[at] if len(ref.shape) == 2 else ref.at[:, at]
+    return [copy_of(rows_of(source, at), rows_of(target, at), sems.at[i]) for i, at in enumerate(parts)]
+
+
+def wait_all(*copies):
     for copy in copies:
-        copy.start()
-    return copies
-
-
-def update(residual, columns, coefs):
-    width = residual.shape[1]
-    both = dot(columns[0], coefs, ((1,), (0,)))
-    return residual - (both[:, :width] + both[:, width:] + dot(columns[1], coefs[:, :width], ((1,), (0,))))
+        copy.wait()
 
 
 def unpack(held, slots_ref):
@@ -127,42 +125,38 @@
 
 def columns_kernel(live_ref, residual_ref, samples_ref, slots_ref, *refs):
     *held, columns_ref, total_ref, residual_v, samples_v, columns_v, sems = refs
-    feat, width = samples_ref.shape[1], residual_ref.shape[1]
-    samples_in = start_copies(samples_ref, samples_v, sems.at[0])
-    residual_in = start_copies(residual_ref, residual_v, sems.at[1])
+    rows, feat = samples_ref.shape
+    width = residual_ref.shape[1]
+    samples_in = copy_of(samples_ref, samples_v, sems.at[0])
+    residual_in = copy_of(residual_ref, residual_v, sems.at[1])
     points = unpack(held, slots_ref)
     scale = 0.5 / feat**0.5
-
-    def add(index, at):
-        residual_in[index].wait()
+    wait_all(samples_in, residual_in)
+    for at in pieces(rows):
+        base = dot3(split(samples_v[at, :]), points, ((1,), (0,))) * scale + 1.0
+        slot = lax.broadcasted_iota(jnp.int32, (at.size, 1), 0) + at.start
+        columns_v[0, at, :], columns_v[1, at, :] = split(jnp.where(slot < live_ref[0], base * base * base, 0.0))
+    columns_out = copy_of(columns_v, columns_ref, sems.at[2])
+    for index, at in enumerate(pieces(rows)):
         high, low = split(residual_v[at, :])
         both = dot(jnp.concatenate([high, low], axis=1), columns_v[0, at, :], ((0,), (0,)))
         term = both[:width] + both[width:] + dot(high, columns_v[1, at, :], ((0,), (0,)))
         total_ref[...] = term if index == 0 else total_ref[...] + term
-
-    parts, columns_out = pieces(samples_ref.shape[0]), []
+    columns_out.wait()
+
+
+def cross_kernel(block, first_ref, second_ref, inverse_ref, out_ref, first_v, second_v, inverse_v, sems):
+    size = first_ref.shape[2]
+    parts = pieces(first_ref.shape[1], HALF_STEP)
+    first_in = copies_of(first_ref, first_v, sems.at[0], parts)
+    second_in = copies_of(second_ref, second_v, sems.at[1], parts)
+    inverse_in = copy_of(inverse_ref.at[block], inverse_v, sems.at[2, 0])
+    cross = None
     for index, at in enumerate(parts):
-        samples_in[index].wait()
-        base = dot3(split(samples_v[at, :]), points, ((1,), (0,))) * scale + 1.0
-        slot = lax.broadcasted_iota(jnp.int32, (at.size, 1), 0) + at.start
-        columns_v[0, at, :], columns_v[1, at, :] = split(jnp.where(slot < live_ref[0], base * base * base, 0.0))
-        columns_out.append(pltpu.make_async_copy(columns_v.at[:, at], columns_ref.at[:, at], sems.at[2, index]))
-        columns_out[-1].start()
-        if index > 0:
-            add(index - 1, parts[index - 1])
-    add(len(parts) - 1, parts[-1])
-    for copy in columns_out:
-        copy.wait()
-
-
-def cross_kernel(first_ref, second_ref, inverse_ref, out_ref, first_v, second_v, inverse_v, sems):
-    first_in = start_copies(first_ref, first_v, sems.at[0])
-    second_in = start_copies(second_ref, second_v, sems.at[1])
-    inverse_in = pltpu.make_async_copy(inverse_ref, inverse_v, sems.at[2, 0])
-    inverse_in.start()
-    for copy in [*first_in, *second_in]:
-        copy.wait()
-    cross = dot3((first_v[0], first_v[1]), (second_v[0], second_v[1]), ((0,), (0,)))
+        wait_all(first_in[index], second_in[index])
+        both = dot(jnp.concatenate([first_v[0, at, :], first_v[1, at, :]], axis=1), second_v[0, at, :], ((0,), (0,)))
+        term = both[:size] + both[size:] + dot(first_v[0, at, :], second_v[1, at, :], ((0,), (0,)))
+        cross = term if cross is None else cross + term
     inverse_in.wait()
     out_ref[0], out_ref[1] = split(dot3(split(inverse_v[...]), split(cross), ((0,), (0,))))
 
@@ -175,82 +169,83 @@
     return jnp.concatenate(split(transposed.T), axis=1)
 
 
-def update_kernel(sums_ref, inverse_ref, residual_ref, columns_ref, out_ref, residual_v, columns_v, sems):
-    columns_in = start_copies(columns_ref, columns_v, sems.at[0])
-    residual_in = start_copies(residual_ref, residual_v, sems.at[1])
-    coefs = side_by_side(dot3(split(sums_ref[...]), split(inverse_ref[...]), ((1,), (1,))))
-    finish_update(coefs, columns_in, residual_in, columns_v, residual_v, out_ref, sems.at[2])
-
-
-def finish_update(coefs, columns_in, residual_in, columns_v, residual_v, out_ref, sems):
+def finish_update(coefs, parts, columns_in, residual_in, columns_v, residual_v, out_ref, sems):
+    width = out_ref.shape[1]
     out = []
-    for index, at in enumerate(pieces(out_ref.shape[0])):
-        columns_in[index].wait()
-        residual_in[index].wait()
-        residual_v[at, :] = update(residual_v[at, :], (columns_v[0, at, :], columns_v[1, at, :]), coefs)
-        out.append(pltpu.make_async_copy(residual_v.at[at], out_ref.at[at], sems.at[index]))
-        out[-1].start()
-    for copy in out:
-        copy.wait()
-
-
-def solved_kernel(columns_ref, inverse_ref, out_ref, columns_v, sems):
-    columns_in = start_copies(columns_ref, columns_v, sems.at[0])
-    inverse = split(inverse_ref[...])
+    for index, at in enumerate(parts):
+        wait_all(columns_in[index], residual_in[index])
+        both = dot(columns_v[0, at, :], coefs, ((1,), (0,)))
+        both = both[:, :width] + both[:, width:] + dot(columns_v[1, at, :], coefs[:, :width], ((1,), (0,)))
+        residual_v[at, :] = residual_v[at, :] - both
+        out.append(copy_of(residual_v.at[at], out_ref.at[at], sems.at[index]))
+    wait_all(*out)
+
+
+def update_kernel(block, sums_ref, inverse_ref, residual_ref, columns_ref, out_ref, residual_v, columns_v, inverse_v, sems):
+    parts = pieces(residual_ref.shape[0])
+    inverse_in = copy_of(inverse_ref.at[block], inverse_v, sems.at[3, 0])
+    columns_in = copies_of(columns_ref, columns_v, sems.at[0], parts)
+    residual_in = copies_of(residual_ref, residual_v, sems.at[1], parts)
+    inverse_in.wait()
+    coefs = side_by_side(dot3(split(sums_ref[...]), split(inverse_v[...]), ((1,), (1,))))
+    finish_update(coefs, parts, columns_in, residual_in, columns_v, residual_v, out_ref, sems.at[2])
+
+
+def solved_kernel(block, columns_ref, inverse_ref, out_ref, columns_v, inverse_v, sems):
+    parts = pieces(columns_ref.shape[1], HALF_STEP)
+    inverse_in = copy_of(inverse_ref.at[block], inverse_v, sems.at[2, 0])
+    columns_in = copies_of(columns_ref, columns_v, sems.at[0], parts)
+    inverse_in.wait()
+    inverse = split(inverse_v[...])
     out = []
-    for index, at in enumerate(pieces(columns_ref.shape[1])):
+    for index, at in enumerate(parts):
         columns_in[index].wait()
         columns_v[0, at, :], columns_v[1, at, :] = split(dot3((columns_v[0, at, :], columns_v[1, at, :]), inverse, ((1,), (0,))))
-        out.append(pltpu.make_async_copy(columns_v.at[:, at], out_ref.at[:, at], sems.at[1, index]))
-        out[-1].start()
-    for copy in out:
-        copy.wait()
+        out.append(copy_of(columns_v.at[:, at], out_ref.at[:, at], sems.at[1, index]))
+    wait_all(*out)
 
 
 def last_kernel(sums_ref, residual_ref, columns_ref, out_ref, residual_v, columns_v, sems):
-    columns_in = start_copies(columns_ref, columns_v, sems.at[0])
-    residual_in = start_copies(residual_ref, residual_v, sems.at[1])
-    finish_update(side_by_side(sums_ref[...]), columns_in, residual_in, columns_v, residual_v, out_ref, sems.at[2])
-
-
-VMEM = pl.BlockSpec(memory_space=pltpu.VMEM)
-HBM = pl.BlockSpec(memory_space=pltpu.HBM)
-SMEM = pl.BlockSpec(memory_space=pltpu.SMEM)
-
-
-def local(kernel, out_shape, args, flops, in_specs, out_specs, scratch_shapes=(), limit=61):
-    moved = sum(a.size * a.dtype.itemsize for a in [*args, *(out_shape if isinstance(out_shape, list) else [out_shape])])
-    return pl.pallas_call(
+    parts = pieces(residual_ref.shape[0])
+    columns_in = copies_of(columns_ref, columns_v, sems.at[0], parts)
+    residual_in = copies_of(residual_ref, residual_v, sems.at[1], parts)
+    finish_update(side_by_side(sums_ref[...]), parts, columns_in, residual_in, columns_v, residual_v, out_ref, sems.at[2])
+
+
+SPACES = {"V": pltpu.VMEM, "H": pltpu.HBM, "S": pltpu.SMEM}
+
+
+def local(kernel, args, places, outs, scratch_shapes, flops, name):
+    args = [pltpu.with_memory_space_constraint(a, SPACES[p]) if p != "S" else a for a, p in zip(args, places)]
+    moved = sum(a.size * a.dtype.itemsize for a in args)
+    made = pl.pallas_call(
         kernel,
-        out_shape=out_shape,
-        in_specs=in_specs,
-        out_specs=out_specs,
+        out_shape=[SPACES[p](shape, dtype) for p, shape, dtype in outs],
+        in_specs=[pl.BlockSpec(memory_space=SPACES[p]) for p in places],
+        out_specs=[pl.BlockSpec(memory_space=SPACES[p]) for p, _, _ in outs],
         scratch_shapes=scratch_shapes,
         cost_estimate=pl.CostEstimate(flops=flops, bytes_accessed=moved, transcendentals=0),
-        compiler_params=pltpu.CompilerParams(vmem_limit_bytes=limit * 2**20),
-        name=kernel.__name__,
+        compiler_params=pltpu.CompilerParams(vmem_limit_bytes=LIMIT),
+        name=name,
     )(*args)
-
-
-def shape_of(*shape, dtype=F32):
-    return jax.ShapeDtypeStruct(shape, dtype)
+    return made if len(outs) > 1 else made[0]
 
 
 def columns_and_sums(live, residual, samples, slots, held):
     (rows, width), feat, size = residual.shape, samples.shape[1], slots.shape[1]
     return local(
         columns_kernel,
-        [shape_of(2, rows, size, dtype=BF16), shape_of(width, size)],
         (live, residual, samples, slots, *held),
-        6 * rows * size * (feat + width),
-        [SMEM, HBM, HBM, VMEM] + [VMEM] * len(held),
-        [HBM, VMEM],
+        "SHHV" + "V" * len(held),
+        [("H", (2, rows, size), BF16), ("V", (width, size), F32)],
         [
             pltpu.VMEM((rows, width), F32),
             pltpu.VMEM((rows, feat), F32),
             pltpu.VMEM((2, rows, size), BF16),
-            pltpu.SemaphoreType.DMA((3, len(pieces(rows)))),
+            pltpu.SemaphoreType.DMA((3,)),
         ],
+        6 * rows * size * (feat + width),
+        "columns",
     )
 
 
@@ -294,37 +289,40 @@
     parts = len(pieces(rows_here))
     columns_v = pltpu.VMEM((2, rows_here, size), BF16)
     residual_v = pltpu.VMEM((rows_here, width), F32)
+    inverse_v = pltpu.VMEM((size, size), F32)
+    sems = pltpu.SemaphoreType.DMA((4, parts))
+
     def cross_of(columns, following, b):
         return local(
-            cross_kernel,
-            shape_of(2, size, size, dtype=BF16),
-            (columns, following, block_inverse[b]),
+            functools.partial(cross_kernel, b),
+            (columns, following, block_inverse),
+            "HHH",
+            [("V", (2, size, size), BF16)],
+            [columns_v, columns_v, inverse_v, sems],
             6 * rows_here * size * size,
-            [HBM, HBM, HBM],
-            VMEM,
-            [columns_v, columns_v, pltpu.VMEM((size, size), F32), pltpu.SemaphoreType.DMA((3, parts))],
+            "cross",
         )
 
     def updated(sums, residual, columns, b):
         return local(
-            update_kernel,
-            shape_of(rows_here, width),
-            (sums, block_inverse[b], residual, columns),
+            functools.partial(update_kernel, b),
+            (sums, block_inverse, residual, columns),
+            "VHHH",
+            [("H", (rows_here, width), F32)],
+            [residual_v, columns_v, inverse_v, sems],
             6 * rows_here * size * width,
-            [VMEM, VMEM, HBM, HBM],
-            HBM,
-            [residual_v, columns_v, pltpu.SemaphoreType.DMA((3, parts))],
+            "update",
         )
 
     def solved_of(columns):
         return local(
-            solved_kernel,
-            shape_of(2, rows_here, size, dtype=BF16),
-            (columns, block_inverse[blocks - 1]),
+            functools.partial(solved_kernel, blocks - 1),
+            (columns, block_inverse),
+            "HH",
+            [("H", (2, rows_here, size), BF16)],
+            [columns_v, inverse_v, sems],
             6 * rows_here * size * size,
-            [HBM, VMEM],
-            HBM,
-            [columns_v, pltpu.SemaphoreType.DMA((2, parts))],
+            "solved",
         )
 
     residual = targets
@@ -342,15 +340,16 @@
         residual, before = made[0], columns
         if b + 1 < blocks:
             _, columns, ahead = made
-            totals = local(next_kernel, shape_of(width, size), (sums, more, ahead), 6 * width * size * size, [VMEM] * 3, VMEM)
+            out = [("V", (width, size), F32)]
+            totals = local(next_kernel, (sums, more, ahead), "VVV", out, [], 6 * width * size * size, "next")
     return local(
         last_kernel,
-        shape_of(rows_here, width),
         (sums, residual, more),
+        "VHH",
+        [("H", (rows_here, width), F32)],
+        [residual_v, columns_v, sems],
         6 * rows_here * size * width,
-        [VMEM, HBM, HBM],
-        HBM,
-        [residual_v, columns_v, pltpu.SemaphoreType.DMA((3, parts))],
+        "last",
     )
 
 

time: 118 us -> 108 us (0.915)
  Pallas kernels: 50.9 us -> 44.6 us
  local copies, waits for them, and re-layouts: 7.57 us -> 1.54 us
  waiting for transfers between devices: 8.28 us -> 13.5 us
  starting transfers between devices: 18.6 us -> 15.4 us
    pallas_call x7, Pallas kernels: 46.6 us -> 40.5 us  [local(): pl.pallas_call(kernel, out_shape=[SPACES[p](shape, dtype) for p, shape, d...]
    squeeze x1 -> x0, local copies, waits for them, and re-layouts: 3.03 us -> none  [solved_of(): block_inverse[blocks - 1]]
    all_to_all x2, waiting for transfers between devices: 1.57 us -> 4.36 us  [sum_over_rows(): lax.all_to_all(jnp.broadcast_to(own[None], (groups, piece, size)), 'rows'...]
    unnamed x14 -> x2, local copies, waits for them, and re-layouts: 2.39 us -> 0.01 us
    all_to_all x2, starting transfers between devices: 10.4 us -> 8.15 us  [sum_over_rows(): got = lax.all_to_all(padded.reshape(groups, piece, size), 'rows', 0, 0)]
    all_to_all x2, waiting for transfers between devices: 5.69 us -> 7.52 us  [sum_over_rows(): got = lax.all_to_all(padded.reshape(groups, piece, size), 'rows', 0, 0)]
  transfers between devices with their start and end apart: 5 -> 5, of which waited for: 4 -> 5; matrix products, arithmetic and copies ran while one was open for 3% -> 0% of each run, Pallas kernels for 26% -> 25%
where the time goes in v3:
time: 108 us; the launch traced here: 107 us
  Pallas kernels  44.6 us (41%)
  blocking collectives  30.1 us (28%)
  starting transfers between devices  15.4 us (14%)
  waiting for transfers between devices  13.5 us (12%)
  between operations  1.63 us (2%)
  local copies, waits for them, and re-layouts  1.54 us (1%)
    pallas_call x7, Pallas kernels, local(): pl.pallas_call(kernel, out_shape=[SPACES[p](shape, dtype) for p, shape, d...  40.5 us
    all_to_all x1, blocking collectives, on_device(): lax.all_to_all(jnp.broadcast_to(rows[None], (groups, cap, feat)), 'rows',...  30.1 us
    all_to_all x2, starting transfers between devices, sum_over_rows(): got = lax.all_to_all(padded.reshape(groups, piece, size), 'rows', 0, 0)  8.15 us
    all_to_all x2, waiting for transfers between devices, sum_over_rows(): got = lax.all_to_all(padded.reshape(groups, piece, size), 'rows', 0, 0)  7.52 us
    all_to_all x2, starting transfers between devices, sum_over_rows(): lax.all_to_all(jnp.broadcast_to(own[None], (groups, piece, size)), 'rows'...  7.27 us
    all_to_all x2, waiting for transfers between devices, sum_over_rows(): lax.all_to_all(jnp.broadcast_to(own[None], (groups, piece, size)), 'rows'...  4.36 us
    pallas_call x1, Pallas kernels, pick(): pl.pallas_call(functools.partial(pick_kernel, groups, cores, cap), out_sh...  4.14 us
  transfers between devices with their start and end apart: 5, of which 5 were waited for; matrix products, arithmetic and copies ran while one was open for 0% of the time, Pallas kernels for 25%

profile of v3, /device:TPU:0, one launch (start us, length us, event | category | flops | bytes accessed | tf_op | source)
XLA Modules:
  0.0 106.9 jit_solution(13083599107613004274)
XLA Ops:
  0.0 4.1 %pick.1 = (f32[48,256]{1,0:T(8,128)S(1)}, s32[1,1024]{1,0:T(1,128)}, s32[1]{0:T(128)}) custom-call(s32[2,512]{1,0:T(2,128)} %ids_ref.1, f32[2048,256]{1,0:T(8,128)} %samples_ref.5), custom_call_target="tpu_custom_call" | custom-call | tf_op jit(solution)/shard_map/pick/pallas_call | solution.py:73
  4.8 0.0 copy-start
  4.9 0.1 broadcast_in_dim.47
  4.9 30.1 %all_to_all.30 = f32[16,48,256]{2,1,0:T(8,128)S(1)} all-to-all(f32[16,48,256]{2,1,0:T(8,128)S(1)} %broadcast_in_dim.47), channel_id=1, replica_groups=mesh['rows'=16,'tgt'=2] {'rows'}, dimensions={0} | all-to-all | bytes 1572864 | tf_op jit(solution)/shard_map/all_to_all | solution.py:282
  35.1 0.0 collective-permute-start
  35.7 0.0 copy-done
  35.8 1.6 %collective-permute-done.refs_1_ = f32[768,256]{1,0:T(8,128)S(1)} collective-permute-done((f32[768,256]{1,0:T(8,128)S(1)}, f32[768,256]{1,0:T(8,128)S(1)}, u32[]{:S(2)}, u32[]{:S(2)}) %collective-permute-start) | collective-permute-done | bytes 786464 | tf_op jit(solution)/shard_map/ppermute | solution.py:285
  37.4 7.8 %columns.2 = (bf16[2,2048,512]{2,1,0:T(8,128)(2,1)}, f32[128,512]{1,0:T(8,128)}) custom-call(s32[1]{0:T(128)S(6)} %copy.9.live_ref, f32[2048,128]{1,0:T(8,128)} %residual_ref.4, f32[2048,256]{1,0:T(8,128)} %samples_ref.5, s32[1,512]{1,0:T(1,128)S(1)} %get-tuple-element.53.slots_ref, f32[768,256]{1,0:T(8,128)S(1)} %bitcast.13, ...), custom_call_target="tpu_custom_call" | custom-call | flops 2415919104 | bytes 4720644 | tf_op jit(solution)/shard_map/columns/pallas_call | solution.py:221
  45.2 3.5 %all-to-all-start.2 = ((f32[16,8,512]{2,1,0:T(8,128)}), f32[16,8,512]{2,1,0:T(8,128)S(1)}, u32[]{:S(2)}, u32[]{:S(2)}) async-start(f32[16,8,512]{2,1,0:T(8,128)} %bitcast.3), calls=%async_computation.2 | async-start | bytes 524288 | tf_op jit(solution)/shard_map/all_to_all | solution.py:256
  48.7 7.0 %columns.3 = (bf16[2,2048,512]{2,1,0:T(8,128)(2,1)}, f32[128,512]{1,0:T(8,128)S(1)}) custom-call(s32[1]{0:T(128)S(6)} %copy.9.live_ref, f32[2048,128]{1,0:T(8,128)} %residual_ref.4, f32[2048,256]{1,0:T(8,128)} %samples_ref.5, s32[1,512]{1,0:T(1,128)S(1)} %get-tuple-element.52.slots_ref, f32[768,256]{1,0:T(8,128)S(1)} %bitcast.14, ...), custom_call_target="tpu_custom_call" | custom-call | flops 2415919104 | bytes 4720644 | tf_op jit(solution)/shard_map/columns/pallas_call | solution.py:221
  55.8 3.3 %all-to-all-done.2 = f32[16,8,512]{2,1,0:T(8,128)S(1)} async-done(((f32[16,8,512]{2,1,0:T(8,128)}), f32[16,8,512]{2,1,0:T(8,128)S(1)}, u32[]{:S(2)}, u32[]{:S(2)}) %all-to-all-start.2) | async-done | bytes 262176 | tf_op jit(solution)/shard_map/all_to_all | solution.py:256
  59.1 0.7 broadcast_in_dim.48
  59.9 3.7 %all-to-all-start.3 = ((f32[16,8,512]{2,1,0:T(8,128)}), f32[16,8,512]{2,1,0:T(8,128)S(1)}, u32[]{:S(2)}, u32[]{:S(2)}) async-start(f32[16,8,512]{2,1,0:T(8,128)} %broadcast_in_dim.48), calls=%async_computation.3 | async-start | bytes 524288 | tf_op jit(solution)/shard_map/all_to_all | solution.py:259
  63.6 7.6 %cross.1.cross_ref = bf16[2,512,512]{2,1,0:T(8,128)(2,1)S(1)} custom-call(bf16[2,2048,512]{2,1,0:T(8,128)(2,1)} %get-tuple-element.39.first_ref.columns_ref, bf16[2,2048,512]{2,1,0:T(8,128)(2,1)} %get-tuple-element.40.second_ref.columns_ref, f32[2,512,512]{2,1,0:T(8,128)} %inverse_ref.5), custom_call_target="tpu_custom_call" | custom-call | flops 3221225472 | bytes 10485760 | tf_op jit(solution)/shard_map/cross/pallas_call | solution.py:221
  71.2 2.1 %all-to-all-done.3 = f32[16,8,512]{2,1,0:T(8,128)S(1)} async-done(((f32[16,8,512]{2,1,0:T(8,128)}), f32[16,8,512]{2,1,0:T(8,128)S(1)}, u32[]{:S(2)}, u32[]{:S(2)}) %all-to-all-start.3) | async-done | bytes 262176 | tf_op jit(solution)/shard_map/all_to_all | solution.py:259
  73.3 1.1 %next.1 = f32[128,512]{1,0:T(8,128)} custom-call(f32[128,512]{1,0:T(8,128)S(1)} %bitcast.9, bf16[2,512,512]{2,1,0:T(8,128)(2,1)S(1)} %cross.1.cross_ref, f32[128,512]{1,0:T(8,128)S(1)} %get-tuple-element.43.ahead_ref), custom_call_target="tpu_custom_call" | custom-call | flops 201326592 | bytes 1572864 | tf_op jit(solution)/shard_map/next/pallas_call | solution.py:221
  74.4 4.6 %all-to-all-start.4 = ((f32[16,8,512]{2,1,0:T(8,128)}), f32[16,8,512]{2,1,0:T(8,128)S(1)}, u32[]{:S(2)}, u32[]{:S(2)}) async-start(f32[16,8,512]{2,1,0:T(8,128)} %bitcast.5), calls=%async_computation.4 | async-start | bytes 524288 | tf_op jit(solution)/shard_map/all_to_all | solution.py:256
  79.0 5.1 %update.1.residual_ref = f32[2048,128]{1,0:T(8,128)} custom-call(f32[128,512]{1,0:T(8,128)S(1)} %bitcast.10, f32[2,512,512]{2,1,0:T(8,128)} %inverse_ref.5, f32[2048,128]{1,0:T(8,128)} %residual_ref.4, bf16[2,2048,512]{2,1,0:T(8,128)(2,1)} %get-tuple-element.39.first_ref.columns_ref), custom_call_target="tpu_custom_call" | custom-call | flops 805306368 | bytes 7602176 | tf_op jit(solution)/shard_map/update/pallas_call | solution.py:221
  84.2 4.2 %all-to-all-done.4 = f32[16,8,512]{2,1,0:T(8,128)S(1)} async-done(((f32[16,8,512]{2,1,0:T(8,128)}), f32[16,8,512]{2,1,0:T(8,128)S(1)}, u32[]{:S(2)}, u32[]{:S(2)}) %all-to-all-start.4) | async-done | bytes 262176 | tf_op jit(solution)/shard_map/all_to_all | solution.py:256
  88.4 0.7 broadcast_in_dim.49
  89.1 3.5 %all-to-all-start.5 = ((f32[16,8,512]{2,1,0:T(8,128)}), f32[16,8,512]{2,1,0:T(8,128)S(1)}, u32[]{:S(2)}, u32[]{:S(2)}) async-start(f32[16,8,512]{2,1,0:T(8,128)} %broadcast_in_dim.49), calls=%async_computation.5 | async-start | bytes 524288 | tf_op jit(solution)/shard_map/all_to_all | solution.py:259
  92.6 7.0 %solved.1.columns_ref = bf16[2,2048,512]{2,1,0:T(8,128)(2,1)} custom-call(bf16[2,2048,512]{2,1,0:T(8,128)(2,1)} %get-tuple-element.40.second_ref.columns_ref, f32[2,512,512]{2,1,0:T(8,128)} %inverse_ref.5), custom_call_target="tpu_custom_call" | custom-call | flops 3221225472 | bytes 6291456 | tf_op jit(solution)/shard_map/solved/pallas_call | solution.py:221
  99.7 2.2 %all-to-all-done.5 = f32[16,8,512]{2,1,0:T(8,128)S(1)} async-done(((f32[16,8,512]{2,1,0:T(8,128)}), f32[16,8,512]{2,1,0:T(8,128)S(1)}, u32[]{:S(2)}, u32[]{:S(2)}) %all-to-all-start.5) | async-done | bytes 262176 | tf_op jit(solution)/shard_map/all_to_all | solution.py:259
  101.9 4.8 %last.1 = f32[2048,128]{1,0:T(8,128)} custom-call(f32[128,512]{1,0:T(8,128)S(1)} %bitcast.11, f32[2048,128]{1,0:T(8,128)} %update.1.residual_ref, bf16[2,2048,512]{2,1,0:T(8,128)(2,1)} %solved.1.columns_ref), custom_call_target="tpu_custom_call" | custom-call | flops 805306368 | bytes 5505024 | tf_op jit(solution)/shard_map/last/pallas_call | solution.py:221
  (4 shorter events, 0.1 us)
Async XLA Ops:
  4.8 30.9 %copy-start = (s32[1,1024]{1,0:T(1,128)S(1)}, s32[1,1024]{1,0:T(1,128)}, u32[]{:S(2)}) copy-start(s32[1,1024]{1,0:T(1,128)} %get-tuple-element.32) | copy-start | bytes 12292
  35.1 2.3 %collective-permute-start = (f32[768,256]{1,0:T(8,128)S(1)}, f32[768,256]{1,0:T(8,128)S(1)}, u32[]{:S(2)}, u32[]{:S(2)}) collective-permute-start(f32[768,256]{1,0:T(8,128)S(1)} %bitcast.12), channel_id=1, source_target_pairs={{1,0},{0,1},{3,2},{2,3},{5,4},{4,5},{7,6},{6,7},{9,8},{8,9},{11,10... | collective-permute-start | bytes 2359304 | tf_op jit(solution)/shard_map/ppermute | solution.py:285
  45.2 14.0 %all-to-all-start.2 = ((f32[16,8,512]{2,1,0:T(8,128)}), f32[16,8,512]{2,1,0:T(8,128)S(1)}, u32[]{:S(2)}, u32[]{:S(2)}) async-start(f32[16,8,512]{2,1,0:T(8,128)} %bitcast.3), calls=%async_computation.2 | async-start | bytes 524288 | tf_op jit(solution)/shard_map/all_to_all | solution.py:256
  59.9 13.4 %all-to-all-start.3 = ((f32[16,8,512]{2,1,0:T(8,128)}), f32[16,8,512]{2,1,0:T(8,128)S(1)}, u32[]{:S(2)}, u32[]{:S(2)}) async-start(f32[16,8,512]{2,1,0:T(8,128)} %broadcast_in_dim.48), calls=%async_computation.3 | async-start | bytes 524288 | tf_op jit(solution)/shard_map/all_to_all | solution.py:259
  74.4 13.9 %all-to-all-start.4 = ((f32[16,8,512]{2,1,0:T(8,128)}), f32[16,8,512]{2,1,0:T(8,128)S(1)}, u32[]{:S(2)}, u32[]{:S(2)}) async-start(f32[16,8,512]{2,1,0:T(8,128)} %bitcast.5), calls=%async_computation.4 | async-start | bytes 524288 | tf_op jit(solution)/shard_map/all_to_all | solution.py:256
  89.1 12.8 %all-to-all-start.5 = ((f32[16,8,512]{2,1,0:T(8,128)}), f32[16,8,512]{2,1,0:T(8,128)S(1)}, u32[]{:S(2)}, u32[]{:S(2)}) async-start(f32[16,8,512]{2,1,0:T(8,128)} %broadcast_in_dim.49), calls=%async_computation.5 | async-start | bytes 524288 | tf_op jit(solution)/shard_map/all_to_all | solution.py:259

commit v4 on v3

v4 whole, which is shorter than its diff:
```python
import functools
import random

import jax
import jax.numpy as jnp
from jax import lax
from jax.experimental import pallas as pl
from jax.experimental.pallas import tpu as pltpu
from jax.sharding import PartitionSpec as P

F32 = jnp.float32
BF16 = jnp.bfloat16
ROWS_STEP = 512
HALF_STEP = 1024
LIMIT = 24 * 2**20
POINTS_SEED = 14
SUMS_SEED = 152


def order_of(groups, seed):
    order = list(range(groups))
    random.Random(seed).shuffle(order)
    return order


def exchange(x, order):
    return lax.all_to_all(x, "rows", 0, 0, axis_index_groups=[order])


def round_up(value, unit):
    return -(-value // unit) * unit


def split(x):
    high = x.astype(BF16)
    return high, (x - high.astype(F32)).astype(BF16)


def dot(a, b, dims):
    return lax.dot_general(a, b, (dims, ((), ())), preferred_element_type=F32)


def dot3(a, b, dims):
    return dot(a[0], b[0], dims) + dot(a[0], b[1], dims) + dot(a[1], b[0], dims)


def pick_kernel(order, cores, cap, ids_ref, samples_ref, rows_ref, slots_ref, most_ref, index_v, index_s, sems):
    rows_here, groups = samples_ref.shape[0], len(order)
    me, core = lax.axis_index("rows"), lax.axis_index("tgt")
    ids = jnp.concatenate([ids_ref[b : b + 1, :] for b in range(ids_ref.shape[0])], axis=1)
    count = ids.shape[1]
    owner = lax.div(ids, jnp.int32(rows_here))
    local = ids - owner * rows_here
    mine = lax.broadcasted_iota(jnp.int32, (groups, count), 0) == owner
    seen = mine.astype(jnp.int32)
    lane = lax.broadcasted_iota(jnp.int32, (groups, count), 1)
    step = 1
    while step < count:
        seen = seen + jnp.where(lane >= step, pltpu.roll(seen, step, 1), 0)
        step *= 2
    most = jnp.max(seen)
    rank = jnp.sum(jnp.where(mine, seen, 0), axis=0, keepdims=True) - 1
    half = lax.div(rank, jnp.int32(cap))
    turn = jnp.zeros_like(owner)
    for index, device in enumerate(order):
        turn = jnp.where(owner == device, index, turn)
    packed = (half * groups + turn) * cap + (rank - half * cap)
    place = lax.broadcasted_iota(jnp.int32, (1, count), 1)
    slots_ref[...] = jnp.where(most > cap * cores, place, packed)
    most_ref[0] = most

    wanted = lax.broadcasted_iota(jnp.int32, (cap, count), 0) + core * cap
    chosen = jnp.where((wanted == rank) & (owner == me), local, 0)
    index_v[...] = jnp.broadcast_to(jnp.sum(chosen, axis=1, keepdims=True), index_v.shape)
    move = pltpu.make_async_copy(index_v, index_s, sems.at[0])
    move.start()
    move.wait()

    @pl.loop(0, cap)
    def _(k):
        pltpu.make_async_copy(samples_ref.at[pl.ds(index_s[k, 0], 1)], rows_ref.at[pl.ds(k, 1)], sems.at[1]).start()

    pltpu.make_async_copy(samples_ref.at[pl.ds(0, cap)], rows_ref, sems.at[1]).wait()


def pick(ids, samples, order, cores, cap):
    count = ids.shape[0] * ids.shape[1]
    vmem = pl.BlockSpec(memory_space=pltpu.VMEM)
    return pl.pallas_call(
        functools.partial(pick_kernel, order, cores, cap),
        out_shape=(
            jax.ShapeDtypeStruct((cap, samples.shape[1]), F32),
            jax.ShapeDtypeStruct((1, count), jnp.int32),
            jax.ShapeDtypeStruct((1,), jnp.int32),
        ),
        in_specs=[vmem, pl.BlockSpec(memory_space=pl.ANY)],
        out_specs=(vmem, vmem, pl.BlockSpec(memory_space=pltpu.SMEM)),
        scratch_shapes=[
            pltpu.VMEM((cap, 128), jnp.int32),
            pltpu.SMEM((cap, 128), jnp.int32),
            pltpu.SemaphoreType.DMA((2,)),
        ],
        name="pick",
    )(ids, samples)


def pieces(rows, step=ROWS_STEP):
    step = min(step, rows)
    return [pl.ds(start, step) for start in range(0, rows, step)]


def copy_of(source, target, sem):
    copy = pltpu.make_async_copy(source, target, sem)
    copy.start()
    return copy


def copies_of(source, target, sems, parts):
    rows_of = lambda ref, at: ref.at[at] if len(ref.shape) == 2 else ref.at[:, at]
    return [copy_of(rows_of(source, at), rows_of(target, at), sems.at[i]) for i, at in enumerate(parts)]


def wait_all(*copies):
    for copy in copies:
        copy.wait()


def unpack(held, slots_ref):
    depth, feat = held[0].shape
    cores = len(held)
    core = lax.axis_index("tgt")
    total = None
    for shift, ref in enumerate(held):
        base = lax.rem(core + shift, cores) * depth
        slot = lax.broadcasted_iota(jnp.int32, (depth, slots_ref.shape[1]), 0) + base
        taken = jnp.where(slot == slots_ref[...], 1.0, 0.0).astype(BF16)
        found = dot(jnp.concatenate(split(ref[...]), axis=1), taken, ((0,), (0,)))
        total = found if total is None else total + found
    return total[:feat].astype(BF16), total[feat:].astype(BF16)


def columns_kernel(resident, live_ref, residual_ref, samples_ref, slots_ref, *refs):
    if resident:
        *held, high_ref, low_ref, total_ref, columns_v, sems = refs
    else:
        *held, high_ref, low_ref, total_ref, columns_v, sems, residual_v, samples_v = refs
        samples_in = copy_of(samples_ref, samples_v, sems.at[2, 0])
        residual_in = copy_of(residual_ref, residual_v, sems.at[3, 0])
    rows, feat = samples_ref.shape
    width = residual_ref.shape[1]
    points = unpack(held, slots_ref)
    scale = 0.5 / feat**0.5
    if not resident:
        wait_all(samples_in, residual_in)
        samples_ref, residual_ref = samples_v, residual_v
    columns_out = []
    for index, half in enumerate(pieces(rows, HALF_STEP)):
        for at in [pl.ds(half.start + part.start, part.size) for part in pieces(half.size)]:
            base = dot3(split(samples_ref[at, :]), points, ((1,), (0,))) * scale + 1.0
            slot = lax.broadcasted_iota(jnp.int32, (at.size, 1), 0) + at.start
            columns_v[0, at, :], columns_v[1, at, :] = split(jnp.where(slot < live_ref[0], base * base * base, 0.0))
        for kind, ref in enumerate((high_ref, low_ref)):
            columns_out.append(copy_of(columns_v.at[kind, half], ref.at[half], sems.at[kind, index]))
    for index, at in enumerate(pieces(rows)):
        high, low = split(residual_ref[at, :])
        both = dot(jnp.concatenate([high, low], axis=1), columns_v[0, at, :], ((0,), (0,)))
        term = both[:width] + both[width:] + dot(high, columns_v[1, at, :], ((0,), (0,)))
        total_ref[...] = term if index == 0 else total_ref[...] + term
    wait_all(*columns_out)


def cross_kernel(block, first_high, first_low, second_high, second_low, inverse_ref, out_ref, first_v, second_v, inverse_v, sems):
    rows, size = first_high.shape
    parts = pieces(rows)
    into = lambda ref, scratch, kind, i, at: copy_of(ref.at[at], scratch.at[kind, at], sems.at[2 * kind + (scratch is second_v), i])
    copies = [
        [into(ref, scratch, kind, i, at) for ref, scratch, kind in zip((first_high, first_low, second_high, second_low), (first_v, first_v, second_v, second_v), (0, 1, 0, 1))]
        for i, at in enumerate(parts)
    ]
    inverse_in = copy_of(inverse_ref.at[block], inverse_v, sems.at[4, 0])
    cross = None
    for index, at in enumerate(parts):
        wait_all(*copies[index])
        both = dot(jnp.concatenate([first_v[0, at, :], first_v[1, at, :]], axis=1), second_v[0, at, :], ((0,), (0,)))
        term = both[:size] + both[size:] + dot(first_v[0, at, :], second_v[1, at, :], ((0,), (0,)))
        cross = term if cross is None else cross + term
    inverse_in.wait()
    out_ref[0], out_ref[1] = split(dot3(split(inverse_v[...]), split(cross), ((0,), (0,))))


def next_kernel(sums_ref, cross_ref, ahead_ref, next_ref):
    next_ref[...] = ahead_ref[...] - dot3(split(sums_ref[...]), (cross_ref[0], cross_ref[1]), ((1,), (0,)))


def coefs_of(sums_ref, inverse):
    return jnp.concatenate(split(dot3(split(sums_ref[...]), split(inverse), ((1,), (1,))).T), axis=1)


def update_kernel(block, sums_ref, inverse_ref, residual_ref, high_ref, low_ref, out_ref, residual_v, columns_v, inverse_v, sems):
    width = residual_ref.shape[1]
    parts = pieces(residual_ref.shape[0], HALF_STEP)
    inverse_in = copy_of(inverse_ref.at[block], inverse_v, sems.at[4, 0])
    copies = [
        [
            copy_of(high_ref.at[at], columns_v.at[0, at], sems.at[0, i]),
            copy_of(low_ref.at[at], columns_v.at[1, at], sems.at[1, i]),
            copy_of(residual_ref.at[at], residual_v.at[at], sems.at[2, i]),
        ]
        for i, at in enumerate(parts)
    ]
    inverse_in.wait()
    coefs = coefs_of(sums_ref, inverse_v[...])
    out = []
    for index, at in enumerate(parts):
        wait_all(*copies[index])
        both = dot(columns_v[0, at, :], coefs, ((1,), (0,)))
        residual_v[at, :] -= both[:, :width] + both[:, width:] + dot(columns_v[1, at, :], coefs[:, :width], ((1,), (0,)))
        out.append(copy_of(residual_v.at[at], out_ref.at[at], sems.at[3, index]))
    wait_all(*out)


def last_kernel(sums_ref, inverse_ref, high_ref, residual_ref, low_ref, out_ref, residual_v, low_v, sems):
    width = residual_ref.shape[1]
    residual_in = copy_of(residual_ref, residual_v, sems.at[0, 0])
    low_in = copy_of(low_ref, low_v, sems.at[1, 0])
    coefs = coefs_of(sums_ref, inverse_ref[0])
    residual_in.wait()
    for at in pieces(residual_ref.shape[0]):
        both = dot(high_ref[at, :], coefs, ((1,), (0,)))
        residual_v[at, :] -= both[:, :width] + both[:, width:]
    low_in.wait()
    out = []
    for index, at in enumerate(pieces(residual_ref.shape[0], HALF_STEP)):
        residual_v[at, :] -= dot(low_v[at, :], coefs[:, :width], ((1,), (0,)))
        out.append(copy_of(residual_v.at[at], out_ref.at[at], sems.at[3, index]))
    wait_all(*out)


SPACES = {"V": pltpu.VMEM, "H": pltpu.HBM, "S": pltpu.SMEM}


def local(kernel, args, places, outs, scratch_shapes, flops, name):
    args = [pltpu.with_memory_space_constraint(a, SPACES[p]) if p != "S" else a for a, p in zip(args, places)]
    moved = sum(a.size * a.dtype.itemsize for a in args)
    made = pl.pallas_call(
        kernel,
        out_shape=[SPACES[p](shape, dtype) for p, shape, dtype in outs],
        in_specs=[pl.BlockSpec(memory_space=SPACES[p]) for p in places],
        out_specs=[pl.BlockSpec(memory_space=SPACES[p]) for p, _, _ in outs],
        scratch_shapes=scratch_shapes,
        cost_estimate=pl.CostEstimate(flops=flops, bytes_accessed=moved, transcendentals=0),
        compiler_params=pltpu.CompilerParams(vmem_limit_bytes=LIMIT),
        name=name,
    )(*args)
    return made if len(outs) > 1 else made[0]


def columns_and_sums(live, residual, samples, slots, held, resident):
    (rows, width), feat, size = residual.shape, samples.shape[1], slots.shape[1]
    scratch = [pltpu.VMEM((2, rows, size), BF16), pltpu.SemaphoreType.DMA((4, len(pieces(rows))))]
    return local(
        functools.partial(columns_kernel, resident),
        (live, residual, samples, slots, *held),
        ("SVVV" if resident else "SHHV") + "V" * len(held),
        [("H", (rows, size), BF16), ("H", (rows, size), BF16), ("V", (width, size), F32)],
        scratch if resident else [*scratch, pltpu.VMEM((rows, width), F32), pltpu.VMEM((rows, feat), F32)],
        6 * rows * size * (feat + width),
        "columns",
    )


def sum_over_rows(totals, groups, during_first, during_second=None):
    order = order_of(groups, SUMS_SEED)
    width, size = totals.shape
    piece = round_up(width, groups) // groups
    padded = jnp.pad(totals, ((0, piece * groups - width), (0, 0))) if piece * groups != width else totals
    got = exchange(padded.reshape(groups, piece, size), order)
    got, made = lax.optimization_barrier((got, during_first()))
    own = jnp.sum(got, axis=0)
    back = exchange(jnp.broadcast_to(own[None], (groups, piece, size)), order)
    more = None
    if during_second is not None:
        back, more = lax.optimization_barrier((back, during_second(made)))
    return back.reshape(groups * piece, size)[:width], made, more


def on_device(groups, cores, counts, samples, targets, point_ids, block_inverse):
    rows_here, feat = samples.shape
    blocks, size = point_ids.shape
    mean = blocks * size / groups
    cap = round_up(max(1, round((mean + 4 * mean**0.5) / cores)), 8)

    order = order_of(groups, POINTS_SEED)
    rows, slots, most = pick(point_ids, samples, order, cores, cap)

    def general(rows):
        ids = jnp.pad(point_ids.reshape(-1), (0, cores * groups * cap - blocks * size), constant_values=-1)
        ids = lax.dynamic_slice_in_dim(ids, lax.axis_index("tgt") * groups * cap, groups * cap)
        local = ids - lax.axis_index("rows") * rows_here
        owned = (local >= 0) & (local < rows_here)
        taken = jnp.take(samples, jnp.clip(local, 0, rows_here - 1), axis=0)
        taken = jnp.where(owned[:, None], taken, 0.0)
        return jnp.sum(exchange(taken.reshape(groups, cap, feat), order), axis=0)

    rows = lax.cond(most[0] > cap * cores, general, lambda rows: rows, rows)
    got = exchange(jnp.broadcast_to(rows[None], (groups, cap, feat)), order).reshape(groups * cap, feat)
    held = [got]
    for shift in range(1, cores):
        held.append(lax.ppermute(got, "tgt", [((c + shift) % cores, c) for c in range(cores)]))

    slots = [slots[:, b * size : (b + 1) * size] for b in range(blocks)]
    width = targets.shape[1]
    parts = len(pieces(rows_here))
    columns_v = pltpu.VMEM((2, rows_here, size), BF16)
    residual_v = pltpu.VMEM((rows_here, width), F32)
    inverse_v = pltpu.VMEM((size, size), F32)
    sems = pltpu.SemaphoreType.DMA((5, parts))

    def cross_of(columns, following, b):
        return local(
            functools.partial(cross_kernel, b),
            (*columns, *following, block_inverse),
            "HHHHH",
            [("V", (2, size, size), BF16)],
            [columns_v, columns_v, inverse_v, sems],
            6 * rows_here * size * size,
            "cross",
        )

    def updated(sums, residual, columns, b):
        return local(
            functools.partial(update_kernel, b),
            (sums, block_inverse, residual, *columns),
            "VHHHH",
            [("H", (rows_here, width), F32)],
            [residual_v, columns_v, inverse_v, sems],
            6 * rows_here * size * width,
            "update",
        )

    residual = targets
    *columns, totals = columns_and_sums(counts, residual, samples, slots[0], held, True)
    sums = before = None
    for b in range(blocks):
        def first(b=b, sums=sums, residual=residual, before=before):
            now = residual if b == 0 else updated(sums, residual, before, b - 1)
            if b + 1 == blocks:
                return now, block_inverse[b : b + 1]
            return (now, *columns_and_sums(counts, now, samples, slots[b + 1], held, False))

        def second(made, b=b, columns=columns):
            return cross_of(columns, made[1:3], b)

        sums, made, cross = sum_over_rows(totals, groups, first, second if b + 1 < blocks else None)
        residual, before = made[0], columns
        if b + 1 < blocks:
            _, *columns, ahead = made
            out = [("V", (width, size), F32)]
            totals = local(next_kernel, (sums, cross, ahead), "VVV", out, [], 6 * width * size * size, "next")
    return local(
        last_kernel,
        (sums, made[1], columns[0], residual, columns[1]),
        "VVVHH",
        [("H", (rows_here, width), F32)],
        [residual_v, pltpu.VMEM((rows_here, size), BF16), sems],
        6 * rows_here * size * width,
        "last",
    )


def solution(mesh):
    return jax.shard_map(
        functools.partial(on_device, mesh.shape["rows"], mesh.shape["tgt"]),
        mesh=mesh,
        in_specs=(P("rows"), P("rows", None), P("rows", "tgt"), P(), P()),
        out_specs=P("rows", "tgt"),
        check_vma=False,
    )
```

time: 108 us -> 99.9 us (0.925)
  waiting for transfers between devices: 13.5 us -> 1.62 us
  Pallas kernels: 44.6 us -> 33 us
  blocking collectives: 30.1 us -> 38.5 us
  starting transfers between devices: 15.4 us -> 18.9 us
  local copies, waits for them, and re-layouts: 1.54 us -> 4.4 us
    all_to_all x4 -> x3, waiting for transfers between devices: 11.9 us -> 0.01 us  [exchange(): return lax.all_to_all(x, 'rows', 0, 0, axis_index_groups=[order])]
    pallas_call x7 -> x6, Pallas kernels: 40.5 us -> 28.8 us  [local(): pl.pallas_call(kernel, out_shape=[SPACES[p](shape, dtype) for p, shape, d...]
    all_to_all x1 -> x2, blocking collectives: 30.1 us -> 38.5 us  [exchange(): return lax.all_to_all(x, 'rows', 0, 0, axis_index_groups=[order])]
    all_to_all x4 -> x3, starting transfers between devices: 15.4 us -> 18.9 us  [exchange(): return lax.all_to_all(x, 'rows', 0, 0, axis_index_groups=[order])]
    unnamed x2 -> x18, local copies, waits for them, and re-layouts: 0.01 us -> 2.29 us
    slice x0 -> x1, local copies, waits for them, and re-layouts: none -> 1.29 us  [first(): return (now, block_inverse[b:b + 1])]
  transfers between devices with their start and end apart: 5 -> 4, of which waited for: 5 -> 1; matrix products, arithmetic and copies ran while one was open for 0% -> 1% of each run, Pallas kernels for 25% -> 18%
where the time goes in v4:
time: 99.9 us; the launch traced here: 99.1 us
  blocking collectives  38.5 us (39%)
  Pallas kernels  33 us (33%)
  starting transfers between devices  18.9 us (19%)
  local copies, waits for them, and re-layouts  4.4 us (4%)
  between operations  1.65 us (2%)
  waiting for transfers between devices  1.62 us (2%)
  other arithmetic  1 us (1%)
    all_to_all x2, blocking collectives, exchange(): return lax.all_to_all(x, 'rows', 0, 0, axis_index_groups=[order])  38.5 us
    pallas_call x6, Pallas kernels, local(): pl.pallas_call(kernel, out_shape=[SPACES[p](shape, dtype) for p, shape, d...  28.8 us
    all_to_all x3, starting transfers between devices, exchange(): return lax.all_to_all(x, 'rows', 0, 0, axis_index_groups=[order])  18.9 us
    pallas_call x1, Pallas kernels, pick(): pl.pallas_call(functools.partial(pick_kernel, order, cores, cap), out_sha...  4.28 us
    unnamed x18, local copies, waits for them, and re-layouts  2.29 us
  transfers between devices with their start and end apart: 4, of which 1 were waited for; matrix products, arithmetic and copies ran while one was open for 1% of the time, Pallas kernels for 18%

profile of v4, /device:TPU:0, one launch (start us, length us, event | category | flops | bytes accessed | tf_op | source)
XLA Modules:
  0.0 99.1 jit_solution(10281096615905047417)
XLA Ops:
  0.0 0.0 copy-start
  0.0 0.0 copy-start.7
  0.0 4.3 %pick.1 = (f32[48,256]{1,0:T(8,128)S(1)}, s32[1,1024]{1,0:T(1,128)}, s32[1]{0:T(128)}) custom-call(s32[2,512]{1,0:T(2,128)} %ids_ref.1, f32[2048,256]{1,0:T(8,128)} %samples_ref.5), custom_call_target="tpu_custom_call" | custom-call | tf_op jit(solution)/shard_map/pick/pallas_call | solution.py:89
  4.9 0.0 copy-done
  5.0 0.0 copy-done.7
  5.0 0.0 copy-start.8
  5.0 0.0 copy-start.2
  5.0 0.1 broadcast_in_dim.47
  5.1 27.9 %all_to_all.30 = f32[16,48,256]{2,1,0:T(8,128)S(1)} all-to-all(f32[16,48,256]{2,1,0:T(8,128)S(1)} %broadcast_in_dim.47), channel_id=1, replica_groups={{14,12,2,28,0,10,4,26,8,30,16,20,24,22,18,6},{15,13,3,29,1,11,5,27,9,31..., dimensions={0} | all-to-all | bytes 1572864 | tf_op jit(solution)/shard_map/all_to_all | solution.py:27
  33.0 0.0 copy-start.3
  33.0 0.0 collective-permute-start
  33.7 0.0 copy-done.8
  33.7 1.6 %collective-permute-done.refs_1_ = f32[768,256]{1,0:T(8,128)S(1)} collective-permute-done((f32[768,256]{1,0:T(8,128)S(1)}, f32[768,256]{1,0:T(8,128)S(1)}, u32[]{:S(2)}, u32[]{:S(2)}) %collective-permute-start) | collective-permute-done | bytes 786464 | tf_op jit(solution)/shard_map/ppermute | solution.py:309
  35.3 0.0 copy-start.5
  35.3 0.0 copy-done.2
  35.3 5.7 %columns.2 = (bf16[2048,512]{1,0:T(8,128)(2,1)}, bf16[2048,512]{1,0:T(8,128)(2,1)}, f32[128,512]{1,0:T(8,128)}) custom-call(s32[1]{0:T(128)S(6)} %copy.9.live_ref, f32[2048,128]{1,0:T(8,128)S(1)} %copy-done.2, f32[2048,256]{1,0:T(8,128)S(1)} %copy-done, s32[1,512]{1,0:T(1,128)S(1)} %get-tuple-element.57.slots_ref, f32[768,256]{1,0:T(8,128)S(1)} %bitcast.13, ...), custom_call_target="tpu_custom_call" | custom-call | flops 2415919104 | bytes 4720644 | tf_op jit(solution)/shard_map/columns/pallas_call | solution.py:245
  41.0 0.0 copy-done.3
  41.0 0.0 copy-done.5
  41.1 6.0 %all-to-all-start.2 = ((f32[16,8,512]{2,1,0:T(8,128)}), f32[16,8,512]{2,1,0:T(8,128)S(1)}, u32[]{:S(2)}, u32[]{:S(2)}) async-start(f32[16,8,512]{2,1,0:T(8,128)} %bitcast.3), calls=%async_computation.2 | async-start | bytes 524288 | tf_op jit(solution)/shard_map/all_to_all | solution.py:27
  47.1 0.0 copy-start.4
  47.1 1.1 %copy-done.4 = f32[16,48,256]{2,1,0:T(8,128)S(1)} copy-done((f32[16,48,256]{2,1,0:T(8,128)S(1)}, f32[16,48,256]{2,1,0:T(8,128)}, u32[]{:S(2)}) %copy-start.4) | copy-done | bytes 786456
  48.2 0.0 copy-start.6
  48.2 1.1 %copy-done.6 = f32[768,256]{1,0:T(8,128)S(1)} copy-done((f32[768,256]{1,0:T(8,128)S(1)}, f32[768,256]{1,0:T(8,128)}, u32[]{:S(2)}) %copy-start.6) | copy-done | bytes 786456
  49.3 6.6 %columns.3 = (bf16[2048,512]{1,0:T(8,128)(2,1)}, bf16[2048,512]{1,0:T(8,128)(2,1)}, f32[128,512]{1,0:T(8,128)S(1)}) custom-call(s32[1]{0:T(128)S(6)} %copy.9.live_ref, f32[2048,128]{1,0:T(8,128)} %residual_ref.4, f32[2048,256]{1,0:T(8,128)} %samples_ref.5, s32[1,512]{1,0:T(1,128)S(1)} %get-tuple-element.56.slots_ref, f32[768,256]{1,0:T(8,128)S(1)} %bitcast.14, ...), custom_call_target="tpu_custom_call" | custom-call | flops 2415919104 | bytes 4720644 | tf_op jit(solution)/shard_map/columns/pallas_call | solution.py:245
  56.0 0.0 all-to-all-done.2
  56.0 0.7 broadcast_in_dim.48
  56.7 6.0 %all-to-all-start.3 = ((f32[16,8,512]{2,1,0:T(8,128)}), f32[16,8,512]{2,1,0:T(8,128)S(1)}, u32[]{:S(2)}, u32[]{:S(2)}) async-start(f32[16,8,512]{2,1,0:T(8,128)} %broadcast_in_dim.48), calls=%async_computation.3 | async-start | bytes 524288 | tf_op jit(solution)/shard_map/all_to_all | solution.py:27
  62.7 6.4 %cross.1.cross_ref = bf16[2,512,512]{2,1,0:T(8,128)(2,1)S(1)} custom-call(bf16[2048,512]{1,0:T(8,128)(2,1)} %get-tuple-element.42.first_high.high_ref, bf16[2048,512]{1,0:T(8,128)(2,1)} %get-tuple-element.43.first_low.low_ref, bf16[2048,512]{1,0:T(8,128)(2,1)} %get-tuple-element.44.second_high.high_ref, ...), custom_call_target="tpu_custom_call" | custom-call | flops 3221225472 | bytes 10485760 | tf_op jit(solution)/shard_map/cross/pallas_call | solution.py:245
  69.2 0.0 all-to-all-done.3
  69.2 1.1 %next.1 = f32[128,512]{1,0:T(8,128)} custom-call(f32[128,512]{1,0:T(8,128)S(1)} %bitcast.9, bf16[2,512,512]{2,1,0:T(8,128)(2,1)S(1)} %cross.1.cross_ref, f32[128,512]{1,0:T(8,128)S(1)} %get-tuple-element.48.ahead_ref), custom_call_target="tpu_custom_call" | custom-call | flops 201326592 | bytes 1572864 | tf_op jit(solution)/shard_map/next/pallas_call | solution.py:245
  70.3 6.9 %all-to-all-start.4 = ((f32[16,8,512]{2,1,0:T(8,128)}), f32[16,8,512]{2,1,0:T(8,128)}, u32[]{:S(2)}, u32[]{:S(2)}) async-start(f32[16,8,512]{2,1,0:T(8,128)} %bitcast.5), calls=%async_computation.4 | async-start | bytes 524288 | tf_op jit(solution)/shard_map/all_to_all | solution.py:27
  77.1 1.3 %slice.11.inverse_ref = f32[1,512,512]{2,1,0:T(8,128)S(1)} slice(f32[2,512,512]{2,1,0:T(8,128)} %inverse_ref.3), slice={[1:2], [0:512], [0:512]} | slice | bytes 2097152 | tf_op jit(solution)/shard_map/slice | solution.py:348
  78.4 0.0 copy-start.1
  78.5 4.6 %update.1.residual_ref = f32[2048,128]{1,0:T(8,128)} custom-call(f32[128,512]{1,0:T(8,128)S(1)} %bitcast.10, f32[2,512,512]{2,1,0:T(8,128)} %inverse_ref.3, f32[2048,128]{1,0:T(8,128)} %residual_ref.4, bf16[2048,512]{1,0:T(8,128)(2,1)} %get-tuple-element.42.first_high.high_ref, bf16[2048,512]{1,0:T(8,128)(2,1)} %get-tuple-element.43.first_low.low_ref), custom_call_target="tpu_custom_call" | custom-call | flops 805306368 | bytes 7602176 | tf_op jit(solution)/shard_map/update/pallas_call | solution.py:245
  83.1 0.0 all-to-all-done.4
  83.1 1.0 reduce_sum.28
  84.1 10.6 %all_to_all.31 = f32[16,8,512]{2,1,0:T(8,128)S(1)} all-to-all(f32[16,8,512]{2,1,0:T(8,128)S(1)} %broadcast_in_dim.49), channel_id=1, replica_groups={{22,8,14,26,30,16,10,28,0,18,2,6,12,4,20,24},{23,9,15,27,31,17,11,29,1,..., dimensions={0} | all-to-all | bytes 524288 | tf_op jit(solution)/shard_map/all_to_all | solution.py:27
  94.7 0.0 copy-done.1
  94.7 4.3 %last.1 = f32[2048,128]{1,0:T(8,128)} custom-call(f32[128,512]{1,0:T(8,128)S(1)} %bitcast.11, f32[1,512,512]{2,1,0:T(8,128)S(1)} %slice.11.inverse_ref, bf16[2048,512]{1,0:T(8,128)(2,1)S(1)} %copy-done.1, f32[2048,128]{1,0:T(8,128)} %update.1.residual_ref, bf16[2048,512]{1,0:T(8,128)(2,1)} %get-tuple-element.45.second_low.low_ref), custom_call_target="tpu_custom_call" | custom-call | flops 805306368 | bytes 6553600 | tf_op jit(solution)/shard_map/last/pallas_call | solution.py:245
  (4 shorter events, 0.1 us)
Async XLA Ops:
  0.0 4.9 %copy-start = (f32[2048,256]{1,0:T(8,128)S(1)}, f32[2048,256]{1,0:T(8,128)}, u32[]{:S(2)}) copy-start(f32[2048,256]{1,0:T(8,128)} %samples_ref.5) | copy-start | bytes 6291460
  0.0 5.0 %copy-start.7 = (s32[2,512]{1,0:T(2,128)S(1)}, s32[2,512]{1,0:T(2,128)}, u32[]{:S(2)}) copy-start(s32[2,512]{1,0:T(2,128)} %ids_ref.1) | copy-start | bytes 12292
  5.0 28.7 %copy-start.8 = (s32[1,1024]{1,0:T(1,128)S(1)}, s32[1,1024]{1,0:T(1,128)}, u32[]{:S(2)}) copy-start(s32[1,1024]{1,0:T(1,128)} %get-tuple-element.34) | copy-start | bytes 12292
  5.0 30.3 %copy-start.2 = (f32[2048,128]{1,0:T(8,128)S(1)}, f32[2048,128]{1,0:T(8,128)}, u32[]{:S(2)}) copy-start(f32[2048,128]{1,0:T(8,128)} %residual_ref.4) | copy-start | bytes 3145732
  33.0 8.0 %copy-start.3 = (f32[16,48,256]{2,1,0:T(8,128)}, f32[16,48,256]{2,1,0:T(8,128)S(1)}, u32[]{:S(2)}) copy-start(f32[16,48,256]{2,1,0:T(8,128)S(1)} %all_to_all.30) | copy-start | bytes 2359300
  33.0 2.3 %collective-permute-start = (f32[768,256]{1,0:T(8,128)S(1)}, f32[768,256]{1,0:T(8,128)S(1)}, u32[]{:S(2)}, u32[]{:S(2)}) collective-permute-start(f32[768,256]{1,0:T(8,128)S(1)} %bitcast.12), channel_id=1, source_target_pairs={{1,0},{0,1},{3,2},{2,3},{5,4},{4,5},{7,6},{6,7},{9,8},{8,9},{11,10... | collective-permute-start | bytes 2359304 | tf_op jit(solution)/shard_map/ppermute | solution.py:309
  35.3 5.7 %copy-start.5 = (f32[768,256]{1,0:T(8,128)}, f32[768,256]{1,0:T(8,128)S(1)}, u32[]{:S(2)}) copy-start(f32[768,256]{1,0:T(8,128)S(1)} %collective-permute-done.refs_1_) | copy-start | bytes 2359300
  41.1 14.9 %all-to-all-start.2 = ((f32[16,8,512]{2,1,0:T(8,128)}), f32[16,8,512]{2,1,0:T(8,128)S(1)}, u32[]{:S(2)}, u32[]{:S(2)}) async-start(f32[16,8,512]{2,1,0:T(8,128)} %bitcast.3), calls=%async_computation.2 | async-start | bytes 524288 | tf_op jit(solution)/shard_map/all_to_all | solution.py:27
  47.1 1.1 %copy-start.4 = (f32[16,48,256]{2,1,0:T(8,128)S(1)}, f32[16,48,256]{2,1,0:T(8,128)}, u32[]{:S(2)}) copy-start(f32[16,48,256]{2,1,0:T(8,128)} %copy-done.3) | copy-start | bytes 2359300
  48.2 1.1 %copy-start.6 = (f32[768,256]{1,0:T(8,128)S(1)}, f32[768,256]{1,0:T(8,128)}, u32[]{:S(2)}) copy-start(f32[768,256]{1,0:T(8,128)} %copy-done.5) | copy-start | bytes 2359300
  56.7 12.5 %all-to-all-start.3 = ((f32[16,8,512]{2,1,0:T(8,128)}), f32[16,8,512]{2,1,0:T(8,128)S(1)}, u32[]{:S(2)}, u32[]{:S(2)}) async-start(f32[16,8,512]{2,1,0:T(8,128)} %broadcast_in_dim.48), calls=%async_computation.3 | async-start | bytes 524288 | tf_op jit(solution)/shard_map/all_to_all | solution.py:27
  70.3 12.8 %all-to-all-start.4 = ((f32[16,8,512]{2,1,0:T(8,128)}), f32[16,8,512]{2,1,0:T(8,128)}, u32[]{:S(2)}, u32[]{:S(2)}) async-start(f32[16,8,512]{2,1,0:T(8,128)} %bitcast.5), calls=%async_computation.4 | async-start | bytes 524288 | tf_op jit(solution)/shard_map/all_to_all | solution.py:27
  78.4 16.2 %copy-start.1 = (bf16[2048,512]{1,0:T(8,128)(2,1)S(1)}, bf16[2048,512]{1,0:T(8,128)(2,1)}, u32[]{:S(2)}) copy-start(bf16[2048,512]{1,0:T(8,128)(2,1)} %get-tuple-element.44.second_high.high_ref) | copy-start | bytes 6291460

commit v5 on v4

v5 whole, which is shorter than its diff:
```python
import functools
import random

import jax
import jax.numpy as jnp
from jax import lax
from jax.experimental import pallas as pl
from jax.experimental.pallas import tpu as pltpu
from jax.sharding import PartitionSpec as P

F32 = jnp.float32
BF16 = jnp.bfloat16
ROWS_STEP = 512
HALF_STEP = 1024
LIMIT = 24 * 2**20
POINTS_SEED = 14
SUMS_SEED = 152


def order_of(groups, seed):
    order = list(range(groups))
    random.Random(seed).shuffle(order)
    return order


def exchange(x, order):
    return lax.all_to_all(x, "rows", 0, 0, axis_index_groups=[order])


def round_up(value, unit):
    return -(-value // unit) * unit


def split(x):
    high = x.astype(BF16)
    return high, (x - high.astype(F32)).astype(BF16)


def dot(a, b, dims):
    return lax.dot_general(a, b, (dims, ((), ())), preferred_element_type=F32)


def dot3(a, b, dims):
    return dot(a[0], b[0], dims) + dot(a[0], b[1], dims) + dot(a[1], b[0], dims)


def pick_kernel(order, cores, cap, ids_ref, samples_ref, rows_ref, slots_ref, most_ref, index_v, index_s, sems):
    rows_here, groups = samples_ref.shape[0], len(order)
    me, core = lax.axis_index("rows"), lax.axis_index("tgt")
    ids = jnp.concatenate([ids_ref[b : b + 1, :] for b in range(ids_ref.shape[0])], axis=1)
    count = ids.shape[1]
    owner = lax.div(ids, jnp.int32(rows_here))
    local = ids - owner * rows_here
    mine = lax.broadcasted_iota(jnp.int32, (groups, count), 0) == owner
    seen = mine.astype(jnp.int32)
    lane = lax.broadcasted_iota(jnp.int32, (groups, count), 1)
    step = 1
    while step < count:
        seen = seen + jnp.where(lane >= step, pltpu.roll(seen, step, 1), 0)
        step *= 2
    most = jnp.max(seen)
    rank = jnp.sum(jnp.where(mine, seen, 0), axis=0, keepdims=True) - 1
    half = lax.div(rank, jnp.int32(cap))
    turn = jnp.zeros_like(owner)
    for index, device in enumerate(order):
        turn = jnp.where(owner == device, index, turn)
    packed = (half * groups + turn) * cap + (rank - half * cap)
    place = lax.broadcasted_iota(jnp.int32, (1, count), 1)
    slots_ref[...] = jnp.where(most > cap * cores, place, packed)
    most_ref[0] = most

    wanted = lax.broadcasted_iota(jnp.int32, (cap, count), 0) + core * cap
    chosen = jnp.where((wanted == rank) & (owner == me), local, 0)
    index_v[...] = jnp.broadcast_to(jnp.sum(chosen, axis=1, keepdims=True), index_v.shape)
    move = pltpu.make_async_copy(index_v, index_s, sems.at[0])
    move.start()
    move.wait()

    @pl.loop(0, cap)
    def _(k):
        pltpu.make_async_copy(samples_ref.at[pl.ds(index_s[k, 0], 1)], rows_ref.at[pl.ds(k, 1)], sems.at[1]).start()

    pltpu.make_async_copy(samples_ref.at[pl.ds(0, cap)], rows_ref, sems.at[1]).wait()


def pick(ids, samples, order, cores, cap):
    count = ids.shape[0] * ids.shape[1]
    vmem = pl.BlockSpec(memory_space=pltpu.VMEM)
    return pl.pallas_call(
        functools.partial(pick_kernel, order, cores, cap),
        out_shape=(
            jax.ShapeDtypeStruct((cap, samples.shape[1]), F32),
            jax.ShapeDtypeStruct((1, count), jnp.int32),
            jax.ShapeDtypeStruct((1,), jnp.int32),
        ),
        in_specs=[vmem, pl.BlockSpec(memory_space=pl.ANY)],
        out_specs=(vmem, vmem, pl.BlockSpec(memory_space=pltpu.SMEM)),
        scratch_shapes=[
            pltpu.VMEM((cap, 128), jnp.int32),
            pltpu.SMEM((cap, 128), jnp.int32),
            pltpu.SemaphoreType.DMA((2,)),
        ],
        name="pick",
    )(ids, samples)


def pieces(rows, step=ROWS_STEP):
    step = min(step, rows)
    return [pl.ds(start, step) for start in range(0, rows, step)]


def copy_of(source, target, sem):
    copy = pltpu.make_async_copy(source, target, sem)
    copy.start()
    return copy


def copies_of(source, target, sems, parts):
    rows_of = lambda ref, at: ref.at[at] if len(ref.shape) == 2 else ref.at[:, at]
    return [copy_of(rows_of(source, at), rows_of(target, at), sems.at[i]) for i, at in enumerate(parts)]


def wait_all(*copies):
    for copy in copies:
        copy.wait()


def unpack(held, slots):
    depth, feat = held[0].shape
    cores = len(held)
    core = lax.axis_index("tgt")
    total = None
    for shift, ref in enumerate(held):
        base = lax.rem(core + shift, cores) * depth
        slot = lax.broadcasted_iota(jnp.int32, (depth, slots.shape[1]), 0) + base
        taken = jnp.where(slot == slots, 1.0, 0.0).astype(BF16)
        found = dot(jnp.concatenate(split(ref[...]), axis=1), taken, ((0,), (0,)))
        total = found if total is None else total + found
    return total[:feat].astype(BF16), total[feat:].astype(BF16)


def make_columns(live_ref, samples_ref, points, columns_v, high_ref, low_ref, sems):
    rows, feat = samples_ref.shape
    scale = 0.5 / feat**0.5
    copies = []
    for index, half in enumerate(pieces(rows, HALF_STEP)):
        for at in [pl.ds(half.start + part.start, part.size) for part in pieces(half.size)]:
            base = dot3(split(samples_ref[at, :]), points, ((1,), (0,))) * scale + 1.0
            slot = lax.broadcasted_iota(jnp.int32, (at.size, 1), 0) + at.start
            columns_v[0, at, :], columns_v[1, at, :] = split(jnp.where(slot < live_ref[0], base * base * base, 0.0))
        for kind, ref in enumerate((high_ref, low_ref)):
            copies.append(copy_of(columns_v.at[kind, half], ref.at[half], sems.at[kind, index]))
    return copies


def sum_high(residual, high):
    width = residual[0].shape[1]
    both = dot(jnp.concatenate(residual, axis=1), high, ((0,), (0,)))
    return both[:width] + both[width:]


def first_kernel(live_ref, residual_ref, samples_ref, slots_ref, *refs):
    *held, high_ref, low_ref, total_ref, points_ref, points_v, columns_v, sems = refs
    others, _, _, size = points_ref.shape
    points = unpack(held, slots_ref[:, :size])
    for b in range(others):
        points_v[b, 0], points_v[b, 1] = unpack(held, slots_ref[:, (b + 1) * size : (b + 2) * size])
    points_out = copy_of(points_v, points_ref, sems.at[3, 0])
    copies = make_columns(live_ref, samples_ref, points, columns_v, high_ref, low_ref, sems)
    for index, at in enumerate(pieces(samples_ref.shape[0])):
        residual = split(residual_ref[at, :])
        term = sum_high(residual, columns_v[0, at, :]) + dot(residual[0], columns_v[1, at, :], ((0,), (0,)))
        total_ref[...] = term if index == 0 else total_ref[...] + term
    wait_all(points_out, *copies)


def beside_kernel(block, live_ref, samples_ref, points_ref, inverse_ref, high_ref, low_ref, inverse_v, points_v, columns_v, sems):
    points_in = copy_of(points_ref.at[block], points_v, sems.at[3, 0])
    inverse_in = copy_of(inverse_ref.at[block], inverse_v, sems.at[2, 0])
    points_in.wait()
    points = (points_v[0], points_v[1])
    wait_all(inverse_in, *make_columns(live_ref, samples_ref, points, columns_v, high_ref, low_ref, sems))


def coefs_of(sums_ref, inverse_ref):
    return jnp.concatenate(split(dot3(split(sums_ref[...]), split(inverse_ref[...]), ((1,), (1,))).T), axis=1)


def halves(source, target, sems):
    return [copy_of(source.at[at], target.at[at], sems.at[i]) for i, at in enumerate(pieces(source.shape[0], HALF_STEP))]


def update(coefs, residual_in, high_in, low_in, residual_v, columns_v, out_ref, sems):
    width = residual_v.shape[1]
    parts = pieces(residual_v.shape[0], HALF_STEP)
    for index, half in enumerate(parts):
        wait_all(residual_in[index], high_in[index])
        both = dot(columns_v[0, half, :], coefs, ((1,), (0,)))
        residual_v[half, :] -= both[:, :width] + both[:, width:]
    out = []
    for index, half in enumerate(parts):
        low_in[index].wait()
        residual_v[half, :] -= dot(columns_v[1, half, :], coefs[:, :width], ((1,), (0,)))
        out.append(copy_of(residual_v.at[half], out_ref.at[half], sems.at[index]))
    return out


def middle_kernel(block, sums_ref, inverse_ref, residual_ref, high_ref, low_ref, next_high, next_low, inverses, *refs):
    out_ref, total_ref, inverse_v, residual_v, columns_v, next_v, sems = refs
    residual_in = halves(residual_ref, residual_v, sems.at[0])
    high_in = halves(high_ref, columns_v.at[0], sems.at[1])
    low_in = halves(low_ref, columns_v.at[1], sems.at[2])
    next_in = [copy_of(ref, next_v.at[kind], sems.at[3, kind]) for kind, ref in enumerate((next_high, next_low))]
    inverse_in = copy_of(inverses.at[block + 1], inverse_v, sems.at[4, 0])
    coefs = coefs_of(sums_ref, inverse_ref)
    out = update(coefs, residual_in, high_in, low_in, residual_v, columns_v, out_ref, sems.at[5])
    next_in[0].wait()
    parts = pieces(residual_v.shape[0])
    for index, at in enumerate(parts):
        term = sum_high(split(residual_v[at, :]), next_v[0, at, :])
        total_ref[...] = term if index == 0 else total_ref[...] + term
    next_in[1].wait()
    for at in parts:
        total_ref[...] += dot(residual_v[at, :].astype(BF16), next_v[1, at, :], ((0,), (0,)))
    wait_all(inverse_in, *out)


def last_kernel(sums_ref, inverse_ref, residual_ref, high_ref, low_ref, out_ref, residual_v, columns_v, sems):
    residual_in = halves(residual_ref, residual_v, sems.at[0])
    high_in = halves(high_ref, columns_v.at[0], sems.at[1])
    low_in = halves(low_ref, columns_v.at[1], sems.at[2])
    coefs = coefs_of(sums_ref, inverse_ref)
    wait_all(*update(coefs, residual_in, high_in, low_in, residual_v, columns_v, out_ref, sems.at[3]))


SPACES = {"V": pltpu.VMEM, "H": pltpu.HBM, "S": pltpu.SMEM}


def local(kernel, args, places, outs, scratch_shapes, flops, name):
    args = [pltpu.with_memory_space_constraint(a, SPACES[p]) if p != "S" else a for a, p in zip(args, places)]
    moved = sum(a.size * a.dtype.itemsize for a in args)
    made = pl.pallas_call(
        kernel,
        out_shape=[SPACES[p](shape, dtype) for p, shape, dtype in outs],
        in_specs=[pl.BlockSpec(memory_space=SPACES[p]) for p in places],
        out_specs=[pl.BlockSpec(memory_space=SPACES[p]) for p, _, _ in outs],
        scratch_shapes=scratch_shapes,
        cost_estimate=pl.CostEstimate(flops=flops, bytes_accessed=moved, transcendentals=0),
        compiler_params=pltpu.CompilerParams(vmem_limit_bytes=LIMIT),
        name=name,
    )(*args)
    return made if len(outs) > 1 else made[0]


def sum_over_rows(totals, groups, beside):
    order = order_of(groups, SUMS_SEED)
    width, size = totals.shape
    piece = round_up(width, groups) // groups
    padded = jnp.pad(totals, ((0, piece * groups - width), (0, 0))) if piece * groups != width else totals
    got = exchange(padded.reshape(groups, piece, size), order)
    made = None
    if beside is not None:
        got, made = lax.optimization_barrier((got, beside()))
    own = jnp.sum(got, axis=0)
    back = exchange(jnp.broadcast_to(own[None], (groups, piece, size)), order)
    return back.reshape(groups * piece, size)[:width], made


def on_device(groups, cores, counts, samples, targets, point_ids, block_inverse):
    rows_here, feat = samples.shape
    blocks, size = point_ids.shape
    mean = blocks * size / groups
    cap = round_up(max(1, round((mean + 4 * mean**0.5) / cores)), 8)

    order = order_of(groups, POINTS_SEED)
    rows, slots, most = pick(point_ids, samples, order, cores, cap)

    def general(rows):
        ids = jnp.pad(point_ids.reshape(-1), (0, cores * groups * cap - blocks * size), constant_values=-1)
        ids = lax.dynamic_slice_in_dim(ids, lax.axis_index("tgt") * groups * cap, groups * cap)
        local = ids - lax.axis_index("rows") * rows_here
        owned = (local >= 0) & (local < rows_here)
        taken = jnp.take(samples, jnp.clip(local, 0, rows_here - 1), axis=0)
        taken = jnp.where(owned[:, None], taken, 0.0)
        return jnp.sum(exchange(taken.reshape(groups, cap, feat), order), axis=0)

    rows = lax.cond(most[0] > cap * cores, general, lambda rows: rows, rows)
    got = exchange(jnp.broadcast_to(rows[None], (groups, cap, feat)), order).reshape(groups * cap, feat)
    held = [got]
    for shift in range(1, cores):
        held.append(lax.ppermute(got, "tgt", [((c + shift) % cores, c) for c in range(cores)]))

    width = targets.shape[1]
    columns_v = pltpu.VMEM((2, rows_here, size), BF16)
    residual_v = pltpu.VMEM((rows_here, width), F32)
    sems = pltpu.SemaphoreType.DMA((6, len(pieces(rows_here, HALF_STEP))))
    columns_out = [("H", (rows_here, size), BF16)] * 2
    inverse_out = ("V", (size, size), F32)
    totals_out = ("V", (width, size), F32)
    work = 6 * rows_here * size

    residual = targets
    *columns, totals, points = local(
        first_kernel,
        (counts, residual, samples, slots, *held),
        "SVVV" + "V" * cores,
        [*columns_out, totals_out, ("H", (blocks - 1, 2, feat, size), BF16)],
        [pltpu.VMEM((blocks - 1, 2, feat, size), BF16), columns_v, sems],
        work * (feat + width),
        "first",
    )
    for b in range(blocks - 1):

        def beside(b=b, points=points):
            args = (counts, samples, points, block_inverse)
            outs = [*columns_out, inverse_out]
            scratch = [pltpu.VMEM((2, feat, size), BF16), columns_v, sems]
            return local(functools.partial(beside_kernel, b), args, "SVHH", outs, scratch, work * feat, "beside")

        sums, (*following, inverse) = sum_over_rows(totals, groups, beside)
        residual, totals, inverse = local(
            functools.partial(middle_kernel, b),
            (sums, inverse, residual, *columns, *following, block_inverse),
            "VVHHHHHH",
            [("H", (rows_here, width), F32), totals_out, inverse_out],
            [residual_v, columns_v, columns_v, sems],
            2 * work * width,
            "middle",
        )
        columns = following
    sums, _ = sum_over_rows(totals, groups, None)
    return local(
        last_kernel,
        (sums, inverse, residual, *columns),
        "VVHHH",
        [("H", (rows_here, width), F32)],
        [residual_v, columns_v, sems],
        work * width,
        "last",
    )


def solution(mesh):
    return jax.shard_map(
        functools.partial(on_device, mesh.shape["rows"], mesh.shape["tgt"]),
        mesh=mesh,
        in_specs=(P("rows"), P("rows", None), P("rows", "tgt"), P(), P()),
        out_specs=P("rows", "tgt"),
        check_vma=False,
    )
```

time: 99.9 us -> 99.7 us (level)
  blocking collectives: 38.5 us -> 61.2 us
  starting transfers between devices: 18.9 us -> 6.03 us
  Pallas kernels: 33 us -> 27.3 us
  local copies, waits for them, and re-layouts: 4.4 us -> 0.13 us
  waiting for transfers between devices: 1.62 us -> 3.24 us
    all_to_all x2 -> x4, blocking collectives: 38.5 us -> 61.2 us  [exchange(): return lax.all_to_all(x, 'rows', 0, 0, axis_index_groups=[order])]
    all_to_all x3 -> x1, starting transfers between devices: 18.9 us -> 6.03 us  [exchange(): return lax.all_to_all(x, 'rows', 0, 0, axis_index_groups=[order])]
    pallas_call x6 -> x4, Pallas kernels: 28.8 us -> 23.1 us  [local(): pl.pallas_call(kernel, out_shape=[SPACES[p](shape, dtype) for p, shape, d...]
    unnamed x18 -> x8, local copies, waits for them, and re-layouts: 2.29 us -> 0.02 us
    all_to_all x3 -> x1, waiting for transfers between devices: 0.01 us -> 1.61 us  [exchange(): return lax.all_to_all(x, 'rows', 0, 0, axis_index_groups=[order])]
    slice x2 -> x0, local copies, waits for them, and re-layouts: 1.3 us -> none  [the longest x1 1.29 us: first(): return (now, block_inverse[b:b + 1])]
  transfers between devices with their start and end apart: 4 -> 2, of which waited for: 1 -> 2; matrix products, arithmetic and copies ran while one was open for 1% -> 0% of each run, Pallas kernels for 18% -> 5%
where the time goes in v5:
time: 99.7 us; the launch traced here: 99.3 us
  blocking collectives  61.2 us (61%)
  Pallas kernels  27.3 us (27%)
  starting transfers between devices  6.03 us (6%)
  waiting for transfers between devices  3.24 us (3%)
  between operations  1.32 us (1%)
    all_to_all x4, blocking collectives, exchange(): return lax.all_to_all(x, 'rows', 0, 0, axis_index_groups=[order])  61.2 us
    pallas_call x4, Pallas kernels, local(): pl.pallas_call(kernel, out_shape=[SPACES[p](shape, dtype) for p, shape, d...  23.1 us
    all_to_all x1, starting transfers between devices, exchange(): return lax.all_to_all(x, 'rows', 0, 0, axis_index_groups=[order])  6.03 us
    pallas_call x1, Pallas kernels, pick(): pl.pallas_call(functools.partial(pick_kernel, order, cores, cap), out_sha...  4.28 us
  transfers between devices with their start and end apart: 2, of which 2 were waited for; matrix products, arithmetic and copies ran while one was open for 0% of the time, Pallas kernels for 5%

profile of v5, /device:TPU:0, one launch (start us, length us, event | category | flops | bytes accessed | tf_op | source)
XLA Modules:
  0.0 99.3 jit_solution(13598110897131770803)
XLA Ops:
  0.0 0.0 copy-start
  0.0 0.0 copy-start.3
  0.0 4.3 %pick.1 = (f32[48,256]{1,0:T(8,128)S(1)}, s32[1,1024]{1,0:T(1,128)}, s32[1]{0:T(128)}) custom-call(s32[2,512]{1,0:T(2,128)} %ids_ref.1, f32[2048,256]{1,0:T(8,128)} %samples_ref.5), custom_call_target="tpu_custom_call" | custom-call | tf_op jit(solution)/shard_map/pick/pallas_call | solution.py:89
  4.9 0.0 copy-done
  4.9 0.0 copy-done.3
  4.9 0.0 copy-start.1
  4.9 0.0 copy-start.2
  4.9 0.1 broadcast_in_dim.47
  5.0 28.1 %all_to_all.30 = f32[16,48,256]{2,1,0:T(8,128)S(1)} all-to-all(f32[16,48,256]{2,1,0:T(8,128)S(1)} %broadcast_in_dim.47), channel_id=1, replica_groups={{14,12,2,28,0,10,4,26,8,30,16,20,24,22,18,6},{15,13,3,29,1,11,5,27,9,31..., dimensions={0} | all-to-all | bytes 1572864 | tf_op jit(solution)/shard_map/all_to_all | solution.py:27
  33.1 0.0 collective-permute-start
  33.7 1.6 %collective-permute-done.refs_1_ = f32[768,256]{1,0:T(8,128)S(1)} collective-permute-done((f32[768,256]{1,0:T(8,128)S(1)}, f32[768,256]{1,0:T(8,128)S(1)}, u32[]{:S(2)}, u32[]{:S(2)}) %collective-permute-start) | collective-permute-done | bytes 786464 | tf_op jit(solution)/shard_map/ppermute | solution.py:291
  35.4 0.0 copy-done.1
  35.4 0.0 copy-done.2
  35.4 6.3 %first.1 = (bf16[2048,512]{1,0:T(8,128)(2,1)}, bf16[2048,512]{1,0:T(8,128)(2,1)}, f32[128,512]{1,0:T(8,128)}, bf16[1,2,256,512]{3,2,1,0:T(8,128)(2,1)}) custom-call(s32[1]{0:T(128)S(6)} %copy.9.live_ref, f32[2048,128]{1,0:T(8,128)S(1)} %copy-done.1, f32[2048,256]{1,0:T(8,128)S(1)} %copy-done, s32[1,1024]{1,0:T(1,128)S(1)} %copy-done.2, ...), custom_call_target="tpu_custom_call" | custom-call | flops 2415919104 | bytes 4722692 | tf_op jit(solution)/shard_map/first/pallas_call | solution.py:242
  41.7 6.0 %all-to-all-start.2 = ((f32[16,8,512]{2,1,0:T(8,128)}), f32[16,8,512]{2,1,0:T(8,128)S(1)}, u32[]{:S(2)}, u32[]{:S(2)}) async-start(f32[16,8,512]{2,1,0:T(8,128)} %bitcast.3), calls=%async_computation.2 | async-start | bytes 524288 | tf_op jit(solution)/shard_map/all_to_all | solution.py:27
  47.7 5.0 %beside.1 = (bf16[2048,512]{1,0:T(8,128)(2,1)}, bf16[2048,512]{1,0:T(8,128)(2,1)}, f32[512,512]{1,0:T(8,128)S(1)}) custom-call(s32[1]{0:T(128)S(6)} %copy.9.live_ref, f32[2048,256]{1,0:T(8,128)S(1)} %copy-done, bf16[1,2,256,512]{3,2,1,0:T(8,128)(2,1)} %get-tuple-element.36.points_ref, f32[2,512,512]{2,1,0:T(8,128)} %inverses.1), custom_call_target="tpu_custom_call" | custom-call | flops 1610612736 | bytes 4718596 | tf_op jit(solution)/shard_map/beside/pallas_call | solution.py:242
  52.7 1.6 %all-to-all-done.2 = f32[16,8,512]{2,1,0:T(8,128)S(1)} async-done(((f32[16,8,512]{2,1,0:T(8,128)}), f32[16,8,512]{2,1,0:T(8,128)S(1)}, u32[]{:S(2)}, u32[]{:S(2)}) %all-to-all-start.2) | async-done | bytes 262176 | tf_op jit(solution)/shard_map/all_to_all | solution.py:27
  54.4 10.9 %all_to_all.31 = f32[16,8,512]{2,1,0:T(8,128)S(1)} all-to-all(f32[16,8,512]{2,1,0:T(8,128)S(1)} %broadcast_in_dim.48), channel_id=1, replica_groups={{22,8,14,26,30,16,10,28,0,18,2,6,12,4,20,24},{23,9,15,27,31,17,11,29,1,..., dimensions={0} | all-to-all | bytes 524288 | tf_op jit(solution)/shard_map/all_to_all | solution.py:27
  65.3 6.0 %middle.1 = (f32[2048,128]{1,0:T(8,128)}, f32[128,512]{1,0:T(8,128)S(1)}, f32[512,512]{1,0:T(8,128)S(1)}) custom-call(f32[128,512]{1,0:T(8,128)S(1)} %bitcast.9, f32[512,512]{1,0:T(8,128)S(1)} %get-tuple-element.41.inverse_ref, f32[2048,128]{1,0:T(8,128)} %residual_ref.3, bf16[2048,512]{1,0:T(8,128)(2,1)} %get-tuple-element.42.high_ref, ...), custom_call_target="tpu_custom_call" | custom-call | flops 1610612736 | bytes 12845056 | tf_op jit(solution)/shard_map/middle/pallas_call | solution.py:242
  71.3 11.1 %all_to_all.32 = f32[16,8,512]{2,1,0:T(8,128)S(1)} all-to-all(f32[16,8,512]{2,1,0:T(8,128)S(1)} %bitcast.13), channel_id=1, replica_groups={{22,8,14,26,30,16,10,28,0,18,2,6,12,4,20,24},{23,9,15,27,31,17,11,29,1,..., dimensions={0} | all-to-all | bytes 524288 | tf_op jit(solution)/shard_map/all_to_all | solution.py:27
  82.4 11.2 %all_to_all.33 = f32[16,8,512]{2,1,0:T(8,128)S(1)} all-to-all(f32[16,8,512]{2,1,0:T(8,128)S(1)} %broadcast_in_dim.49), channel_id=1, replica_groups={{22,8,14,26,30,16,10,28,0,18,2,6,12,4,20,24},{23,9,15,27,31,17,11,29,1,..., dimensions={0} | all-to-all | bytes 524288 | tf_op jit(solution)/shard_map/all_to_all | solution.py:27
  93.6 5.7 %last.1 = f32[2048,128]{1,0:T(8,128)} custom-call(f32[128,512]{1,0:T(8,128)S(1)} %bitcast.10, f32[512,512]{1,0:T(8,128)S(1)} %get-tuple-element.47.inverse_ref, f32[2048,128]{1,0:T(8,128)} %get-tuple-element.48.residual_ref, bf16[2048,512]{1,0:T(8,128)(2,1)} %get-tuple-element.44.next_high.high_ref, bf16[2048,512]{1,0:T(8,128)(2,1)} %get-tuple-element.45.next_low.low_ref), custom_call_target="tpu_custom_call" | custom-call | flops 805306368 | bytes 6553600 | tf_op jit(solution)/shard_map/last/pallas_call | solution.py:242
  (5 shorter events, 0.1 us)
Async XLA Ops:
  0.0 4.9 %copy-start = (f32[2048,256]{1,0:T(8,128)S(1)}, f32[2048,256]{1,0:T(8,128)}, u32[]{:S(2)}) copy-start(f32[2048,256]{1,0:T(8,128)} %samples_ref.5) | copy-start | bytes 6291460
  0.0 4.9 %copy-start.3 = (s32[2,512]{1,0:T(2,128)S(1)}, s32[2,512]{1,0:T(2,128)}, u32[]{:S(2)}) copy-start(s32[2,512]{1,0:T(2,128)} %ids_ref.1) | copy-start | bytes 12292
  4.9 30.5 %copy-start.1 = (f32[2048,128]{1,0:T(8,128)S(1)}, f32[2048,128]{1,0:T(8,128)}, u32[]{:S(2)}) copy-start(f32[2048,128]{1,0:T(8,128)} %residual_ref.3) | copy-start | bytes 3145732
  4.9 30.5 %copy-start.2 = (s32[1,1024]{1,0:T(1,128)S(1)}, s32[1,1024]{1,0:T(1,128)}, u32[]{:S(2)}) copy-start(s32[1,1024]{1,0:T(1,128)} %get-tuple-element.32.slots_ref) | copy-start | bytes 12292
  33.1 2.3 %collective-permute-start = (f32[768,256]{1,0:T(8,128)S(1)}, f32[768,256]{1,0:T(8,128)S(1)}, u32[]{:S(2)}, u32[]{:S(2)}) collective-permute-start(f32[768,256]{1,0:T(8,128)S(1)} %bitcast.11), channel_id=1, source_target_pairs={{1,0},{0,1},{3,2},{2,3},{5,4},{4,5},{7,6},{6,7},{9,8},{8,9},{11,10... | collective-permute-start | bytes 2359304 | tf_op jit(solution)/shard_map/ppermute | solution.py:291
  41.7 12.7 %all-to-all-start.2 = ((f32[16,8,512]{2,1,0:T(8,128)}), f32[16,8,512]{2,1,0:T(8,128)S(1)}, u32[]{:S(2)}, u32[]{:S(2)}) async-start(f32[16,8,512]{2,1,0:T(8,128)} %bitcast.3), calls=%async_computation.2 | async-start | bytes 524288 | tf_op jit(solution)/shard_map/all_to_all | solution.py:27

commit v6 on v5

--- a/solution.py
+++ b/solution.py
@@ -83,27 +83,6 @@
     pltpu.make_async_copy(samples_ref.at[pl.ds(0, cap)], rows_ref, sems.at[1]).wait()
 
 
-def pick(ids, samples, order, cores, cap):
-    count = ids.shape[0] * ids.shape[1]
-    vmem = pl.BlockSpec(memory_space=pltpu.VMEM)
-    return pl.pallas_call(
-        functools.partial(pick_kernel, order, cores, cap),
-        out_shape=(
-            jax.ShapeDtypeStruct((cap, samples.shape[1]), F32),
-            jax.ShapeDtypeStruct((1, count), jnp.int32),
-            jax.ShapeDtypeStruct((1,), jnp.int32),
-        ),
-        in_specs=[vmem, pl.BlockSpec(memory_space=pl.ANY)],
-        out_specs=(vmem, vmem, pl.BlockSpec(memory_space=pltpu.SMEM)),
-        scratch_shapes=[
-            pltpu.VMEM((cap, 128), jnp.int32),
-            pltpu.SMEM((cap, 128), jnp.int32),
-            pltpu.SemaphoreType.DMA((2,)),
-        ],
-        name="pick",
-    )(ids, samples)
-
-
 def pieces(rows, step=ROWS_STEP):
     step = min(step, rows)
     return [pl.ds(start, step) for start in range(0, rows, step)]
@@ -115,9 +94,8 @@
     return copy
 
 
-def copies_of(source, target, sems, parts):
-    rows_of = lambda ref, at: ref.at[at] if len(ref.shape) == 2 else ref.at[:, at]
-    return [copy_of(rows_of(source, at), rows_of(target, at), sems.at[i]) for i, at in enumerate(parts)]
+def halves(source, target, sems):
+    return [copy_of(source.at[at], target.at[at], sems.at[i]) for i, at in enumerate(pieces(source.shape[0], HALF_STEP))]
 
 
 def wait_all(*copies):
@@ -125,21 +103,21 @@
         copy.wait()
 
 
-def unpack(held, slots):
-    depth, feat = held[0].shape
-    cores = len(held)
-    core = lax.axis_index("tgt")
-    total = None
-    for shift, ref in enumerate(held):
-        base = lax.rem(core + shift, cores) * depth
-        slot = lax.broadcasted_iota(jnp.int32, (depth, slots.shape[1]), 0) + base
-        taken = jnp.where(slot == slots, 1.0, 0.0).astype(BF16)
-        found = dot(jnp.concatenate(split(ref[...]), axis=1), taken, ((0,), (0,)))
-        total = found if total is None else total + found
-    return total[:feat].astype(BF16), total[feat:].astype(BF16)
-
-
-def make_columns(live_ref, samples_ref, points, columns_v, high_ref, low_ref, sems):
+def found_in(ref, slots, shift, cores):
+    depth = ref.shape[0]
+    base = lax.rem(lax.axis_index("tgt") + shift, cores) * depth
+    slot = lax.broadcasted_iota(jnp.int32, (depth, slots.shape[1]), 0) + base
+    taken = jnp.where(slot == slots, 1.0, 0.0).astype(BF16)
+    return dot(jnp.concatenate(split(ref[...]), axis=1), taken, ((0,), (0,)))
+
+
+def own_kernel(cores, slots_ref, held_ref, found_ref):
+    blocks, _, size = found_ref.shape
+    for b in range(blocks):
+        found_ref[b] = found_in(held_ref, slots_ref[:, b * size : (b + 1) * size], 0, cores).astype(BF16)
+
+
+def make_columns(live_ref, samples_ref, points, high_v, low_v, high_ref, low_ref, sems):
     rows, feat = samples_ref.shape
     scale = 0.5 / feat**0.5
     copies = []
@@ -147,9 +125,9 @@
         for at in [pl.ds(half.start + part.start, part.size) for part in pieces(half.size)]:
             base = dot3(split(samples_ref[at, :]), points, ((1,), (0,))) * scale + 1.0
             slot = lax.broadcasted_iota(jnp.int32, (at.size, 1), 0) + at.start
-            columns_v[0, at, :], columns_v[1, at, :] = split(jnp.where(slot < live_ref[0], base * base * base, 0.0))
-        for kind, ref in enumerate((high_ref, low_ref)):
-            copies.append(copy_of(columns_v.at[kind, half], ref.at[half], sems.at[kind, index]))
+            high_v[at, :], low_v[at, :] = split(jnp.where(slot < live_ref[0], base * base * base, 0.0))
+        copies.append(copy_of(high_v.at[half], high_ref.at[half], sems.at[0, index]))
+        copies.append(copy_of(low_v.at[half], low_ref.at[half], sems.at[1, index]))
     return copies
 
 
@@ -159,14 +137,18 @@
     return both[:width] + both[width:]
 
 
-def first_kernel(live_ref, residual_ref, samples_ref, slots_ref, *refs):
+def first_kernel(live_ref, residual_ref, samples_ref, slots_ref, found_ref, *refs):
     *held, high_ref, low_ref, total_ref, points_ref, points_v, columns_v, sems = refs
-    others, _, _, size = points_ref.shape
-    points = unpack(held, slots_ref[:, :size])
-    for b in range(others):
-        points_v[b, 0], points_v[b, 1] = unpack(held, slots_ref[:, (b + 1) * size : (b + 2) * size])
+    blocks, _, size = found_ref.shape
+    feat = samples_ref.shape[1]
+    for b in range(blocks):
+        found = found_ref[b].astype(F32)
+        for shift, ref in enumerate(held):
+            found = found + found_in(ref, slots_ref[:, b * size : (b + 1) * size], shift + 1, len(held) + 1)
+        points_v[b, 0], points_v[b, 1] = found[:feat].astype(BF16), found[feat:].astype(BF16)
     points_out = copy_of(points_v, points_ref, sems.at[3, 0])
-    copies = make_columns(live_ref, samples_ref, points, columns_v, high_ref, low_ref, sems)
+    points = (points_v[0, 0], points_v[0, 1])
+    copies = make_columns(live_ref, samples_ref, points, columns_v.at[0], columns_v.at[1], high_ref, low_ref, sems)
     for index, at in enumerate(pieces(samples_ref.shape[0])):
         residual = split(residual_ref[at, :])
         term = sum_high(residual, columns_v[0, at, :]) + dot(residual[0], columns_v[1, at, :], ((0,), (0,)))
@@ -175,34 +157,23 @@
 
 
 def beside_kernel(block, live_ref, samples_ref, points_ref, inverse_ref, high_ref, low_ref, inverse_v, points_v, columns_v, sems):
-    points_in = copy_of(points_ref.at[block], points_v, sems.at[3, 0])
+    points_in = copy_of(points_ref.at[block + 1], points_v, sems.at[3, 0])
     inverse_in = copy_of(inverse_ref.at[block], inverse_v, sems.at[2, 0])
     points_in.wait()
     points = (points_v[0], points_v[1])
-    wait_all(inverse_in, *make_columns(live_ref, samples_ref, points, columns_v, high_ref, low_ref, sems))
+    wait_all(inverse_in, *make_columns(live_ref, samples_ref, points, columns_v.at[0], columns_v.at[1], high_ref, low_ref, sems))
 
 
 def coefs_of(sums_ref, inverse_ref):
     return jnp.concatenate(split(dot3(split(sums_ref[...]), split(inverse_ref[...]), ((1,), (1,))).T), axis=1)
 
 
-def halves(source, target, sems):
-    return [copy_of(source.at[at], target.at[at], sems.at[i]) for i, at in enumerate(pieces(source.shape[0], HALF_STEP))]
-
-
-def update(coefs, residual_in, high_in, low_in, residual_v, columns_v, out_ref, sems):
-    width = residual_v.shape[1]
-    parts = pieces(residual_v.shape[0], HALF_STEP)
-    for index, half in enumerate(parts):
-        wait_all(residual_in[index], high_in[index])
+def update_high(coefs, residual_ref, columns_v, out_ref, waits):
+    width = residual_ref.shape[1]
+    for half, ready in zip(pieces(residual_ref.shape[0], HALF_STEP), waits):
+        wait_all(*ready)
         both = dot(columns_v[0, half, :], coefs, ((1,), (0,)))
-        residual_v[half, :] -= both[:, :width] + both[:, width:]
-    out = []
-    for index, half in enumerate(parts):
-        low_in[index].wait()
-        residual_v[half, :] -= dot(columns_v[1, half, :], coefs[:, :width], ((1,), (0,)))
-        out.append(copy_of(residual_v.at[half], out_ref.at[half], sems.at[index]))
-    return out
+        out_ref[half, :] = residual_ref[half, :] - (both[:, :width] + both[:, width:])
 
 
 def middle_kernel(block, sums_ref, inverse_ref, residual_ref, high_ref, low_ref, next_high, next_low, inverses, *refs):
@@ -213,24 +184,33 @@
     next_in = [copy_of(ref, next_v.at[kind], sems.at[3, kind]) for kind, ref in enumerate((next_high, next_low))]
     inverse_in = copy_of(inverses.at[block + 1], inverse_v, sems.at[4, 0])
     coefs = coefs_of(sums_ref, inverse_ref)
-    out = update(coefs, residual_in, high_in, low_in, residual_v, columns_v, out_ref, sems.at[5])
-    next_in[0].wait()
-    parts = pieces(residual_v.shape[0])
+    width = out_ref.shape[1]
+    update_high(coefs, residual_v, columns_v, out_ref, zip(residual_in, high_in))
+    wait_all(*low_in, next_in[0])
+    parts = pieces(out_ref.shape[0])
     for index, at in enumerate(parts):
-        term = sum_high(split(residual_v[at, :]), next_v[0, at, :])
+        residual = out_ref[at, :] - dot(columns_v[1, at, :], coefs[:, :width], ((1,), (0,)))
+        out_ref[at, :] = residual
+        term = sum_high(split(residual), next_v[0, at, :])
         total_ref[...] = term if index == 0 else total_ref[...] + term
     next_in[1].wait()
     for at in parts:
-        total_ref[...] += dot(residual_v[at, :].astype(BF16), next_v[1, at, :], ((0,), (0,)))
-    wait_all(inverse_in, *out)
+        total_ref[...] += dot(out_ref[at, :].astype(BF16), next_v[1, at, :], ((0,), (0,)))
+    inverse_in.wait()
 
 
 def last_kernel(sums_ref, inverse_ref, residual_ref, high_ref, low_ref, out_ref, residual_v, columns_v, sems):
-    residual_in = halves(residual_ref, residual_v, sems.at[0])
     high_in = halves(high_ref, columns_v.at[0], sems.at[1])
     low_in = halves(low_ref, columns_v.at[1], sems.at[2])
     coefs = coefs_of(sums_ref, inverse_ref)
-    wait_all(*update(coefs, residual_in, high_in, low_in, residual_v, columns_v, out_ref, sems.at[3]))
+    width = residual_ref.shape[1]
+    update_high(coefs, residual_ref, columns_v, residual_v, zip(high_in))
+    out = []
+    for index, half in enumerate(pieces(out_ref.shape[0], HALF_STEP)):
+        low_in[index].wait()
+        residual_v[half, :] -= dot(columns_v[1, half, :], coefs[:, :width], ((1,), (0,)))
+        out.append(copy_of(residual_v.at[half], out_ref.at[half], sems.at[3, index]))
+    wait_all(*out)
 
 
 SPACES = {"V": pltpu.VMEM, "H": pltpu.HBM, "S": pltpu.SMEM}
@@ -273,7 +253,15 @@
     cap = round_up(max(1, round((mean + 4 * mean**0.5) / cores)), 8)
 
     order = order_of(groups, POINTS_SEED)
-    rows, slots, most = pick(point_ids, samples, order, cores, cap)
+    rows, slots, most = local(
+        functools.partial(pick_kernel, order, cores, cap),
+        (point_ids, samples),
+        "VH",
+        [("V", (cap, feat), F32), ("V", (1, blocks * size), jnp.int32), ("S", (1,), jnp.int32)],
+        [pltpu.VMEM((cap, 128), jnp.int32), pltpu.SMEM((cap, 128), jnp.int32), pltpu.SemaphoreType.DMA((2,))],
+        0,
+        "pick",
+    )
 
     def general(rows):
         ids = jnp.pad(point_ids.reshape(-1), (0, cores * groups * cap - blocks * size), constant_values=-1)
@@ -286,9 +274,17 @@
 
     rows = lax.cond(most[0] > cap * cores, general, lambda rows: rows, rows)
     got = exchange(jnp.broadcast_to(rows[None], (groups, cap, feat)), order).reshape(groups * cap, feat)
-    held = [got]
-    for shift in range(1, cores):
-        held.append(lax.ppermute(got, "tgt", [((c + shift) % cores, c) for c in range(cores)]))
+    held = [lax.ppermute(got, "tgt", [((c + shift) % cores, c) for c in range(cores)]) for shift in range(1, cores)]
+    found = local(
+        functools.partial(own_kernel, cores),
+        (slots, got),
+        "VV",
+        [("V", (blocks, 2 * feat, size), BF16)],
+        [],
+        4 * groups * cap * feat * blocks * size,
+        "own",
+    )
+    held, found = lax.optimization_barrier((held, found))
 
     width = targets.shape[1]
     columns_v = pltpu.VMEM((2, rows_here, size), BF16)
@@ -302,10 +298,10 @@
     residual = targets
     *columns, totals, points = local(
         first_kernel,
-        (counts, residual, samples, slots, *held),
-        "SVVV" + "V" * cores,
-        [*columns_out, totals_out, ("H", (blocks - 1, 2, feat, size), BF16)],
-        [pltpu.VMEM((blocks - 1, 2, feat, size), BF16), columns_v, sems],
+        (counts, residual, samples, slots, found, *held),
+        "SVVVV" + "V" * len(held),
+        [*columns_out, totals_out, ("H", (blocks, 2, feat, size), BF16)],
+        [pltpu.VMEM((blocks, 2, feat, size), BF16), columns_v, sems],
         work * (feat + width),
         "first",
     )
@@ -322,7 +318,7 @@
             functools.partial(middle_kernel, b),
             (sums, inverse, residual, *columns, *following, block_inverse),
             "VVHHHHHH",
-            [("H", (rows_here, width), F32), totals_out, inverse_out],
+            [("V", (rows_here, width), F32), totals_out, inverse_out],
             [residual_v, columns_v, columns_v, sems],
             2 * work * width,
             "middle",
@@ -332,7 +328,7 @@
     return local(
         last_kernel,
         (sums, inverse, residual, *columns),
-        "VVHHH",
+        "VVVHH",
         [("H", (rows_here, width), F32)],
         [residual_v, columns_v, sems],
         work * width,

time: 99.7 us -> 97.2 us (0.975)
  waiting for transfers between devices: 3.24 us -> 2.23 us
    pallas_call x1 -> x0, Pallas kernels: 4.28 us -> none  [pick(): pl.pallas_call(functools.partial(pick_kernel, order, cores, cap), out_sha...]
    pallas_call x4 -> x6, Pallas kernels: 23.1 us -> 26.6 us  [local(): pl.pallas_call(kernel, out_shape=[SPACES[p](shape, dtype) for p, shape, d...]
    ppermute x1, waiting for transfers between devices: 1.63 us -> 0.6 us  [on_device(): lax.ppermute(got, 'tgt', [((c + shift) % cores, c) for c in range(cores)])]
  transfers between devices with their start and end apart: 2 -> 2, of which waited for: 2 -> 2; matrix products, arithmetic and copies ran while one was open for 0% -> 0% of each run, Pallas kernels for 5% -> 6%
where the time goes in v6:
time: 97.2 us; the launch traced here: 96.8 us
  blocking collectives  61 us (63%)
  Pallas kernels  26.6 us (27%)
  starting transfers between devices  6.03 us (6%)
  waiting for transfers between devices  2.23 us (2%)
    all_to_all x4, blocking collectives, exchange(): return lax.all_to_all(x, 'rows', 0, 0, axis_index_groups=[order])  61 us
    pallas_call x6, Pallas kernels, local(): pl.pallas_call(kernel, out_shape=[SPACES[p](shape, dtype) for p, shape, d...  26.6 us
    all_to_all x1, starting transfers between devices, exchange(): return lax.all_to_all(x, 'rows', 0, 0, axis_index_groups=[order])  6.03 us
  transfers between devices with their start and end apart: 2, of which 2 were waited for; matrix products, arithmetic and copies ran while one was open for 0% of the time, Pallas kernels for 6%

profile of v6, /device:TPU:0, one launch (start us, length us, event | category | flops | bytes accessed | tf_op | source)
XLA Modules:
  0.0 96.8 jit_solution(7632806249480723546)
XLA Ops:
  0.0 0.0 copy-start
  0.0 3.7 %pick.1 = (f32[48,256]{1,0:T(8,128)S(1)}, s32[1,1024]{1,0:T(1,128)S(1)}, s32[1]{0:T(128)S(4)}) custom-call(s32[2,512]{1,0:T(2,128)} %ids_ref.1, f32[2048,256]{1,0:T(8,128)} %samples_ref.5), custom_call_target="tpu_custom_call" | custom-call | bytes 2101248 | tf_op jit(solution)/shard_map/pick/pallas_call | solution.py:222
  3.7 0.0 copy-done
  3.7 0.1 broadcast_in_dim.47
  3.8 0.0 copy-start.1
  3.8 27.9 %all_to_all.30 = f32[16,48,256]{2,1,0:T(8,128)S(1)} all-to-all(f32[16,48,256]{2,1,0:T(8,128)S(1)} %broadcast_in_dim.47), channel_id=1, replica_groups={{14,12,2,28,0,10,4,26,8,30,16,20,24,22,18,6},{15,13,3,29,1,11,5,27,9,31..., dimensions={0} | all-to-all | bytes 1572864 | tf_op jit(solution)/shard_map/all_to_all | solution.py:27
  31.7 0.0 collective-permute-start
  32.4 1.0 %own.1.found_ref = bf16[2,512,512]{2,1,0:T(8,128)(2,1)S(1)} custom-call(s32[1,1024]{1,0:T(1,128)S(1)} %get-tuple-element.34.slots_ref, f32[768,256]{1,0:T(8,128)S(1)} %bitcast.12), custom_call_target="tpu_custom_call" | custom-call | flops 805306368 | bytes 790528 | tf_op jit(solution)/shard_map/own/pallas_call | solution.py:222
  33.4 0.6 collective-permute-done.refs_0_
  34.0 0.0 copy-done.1
  34.0 5.6 %first.1 = (bf16[2048,512]{1,0:T(8,128)(2,1)}, bf16[2048,512]{1,0:T(8,128)(2,1)}, f32[128,512]{1,0:T(8,128)}, bf16[2,2,256,512]{3,2,1,0:T(8,128)(2,1)}) custom-call(s32[1]{0:T(128)S(6)} %copy.9.live_ref, f32[2048,128]{1,0:T(8,128)S(1)} %copy-done.1, f32[2048,256]{1,0:T(8,128)S(1)} %copy-done, s32[1,1024]{1,0:T(1,128)S(1)} %get-tuple-element.34.slots_ref, ...), custom_call_target="tpu_custom_call" | custom-call | flops 2415919104 | bytes 4984836 | tf_op jit(solution)/shard_map/first/pallas_call | solution.py:222
  39.6 6.0 %all-to-all-start.2 = ((f32[16,8,512]{2,1,0:T(8,128)}), f32[16,8,512]{2,1,0:T(8,128)S(1)}, u32[]{:S(2)}, u32[]{:S(2)}) async-start(f32[16,8,512]{2,1,0:T(8,128)} %bitcast.3), calls=%async_computation.2 | async-start | bytes 524288 | tf_op jit(solution)/shard_map/all_to_all | solution.py:27
  45.6 5.0 %beside.1 = (bf16[2048,512]{1,0:T(8,128)(2,1)}, bf16[2048,512]{1,0:T(8,128)(2,1)}, f32[512,512]{1,0:T(8,128)S(1)}) custom-call(s32[1]{0:T(128)S(6)} %copy.9.live_ref, f32[2048,256]{1,0:T(8,128)S(1)} %copy-done, bf16[2,2,256,512]{3,2,1,0:T(8,128)(2,1)} %get-tuple-element.40.points_ref, f32[2,512,512]{2,1,0:T(8,128)} %inverses.1), custom_call_target="tpu_custom_call" | custom-call | flops 1610612736 | bytes 5242884 | tf_op jit(solution)/shard_map/beside/pallas_call | solution.py:222
  50.6 1.6 %all-to-all-done.2 = f32[16,8,512]{2,1,0:T(8,128)S(1)} async-done(((f32[16,8,512]{2,1,0:T(8,128)}), f32[16,8,512]{2,1,0:T(8,128)S(1)}, u32[]{:S(2)}, u32[]{:S(2)}) %all-to-all-start.2) | async-done | bytes 262176 | tf_op jit(solution)/shard_map/all_to_all | solution.py:27
  52.3 10.9 %all_to_all.31 = f32[16,8,512]{2,1,0:T(8,128)S(1)} all-to-all(f32[16,8,512]{2,1,0:T(8,128)S(1)} %broadcast_in_dim.48), channel_id=1, replica_groups={{22,8,14,26,30,16,10,28,0,18,2,6,12,4,20,24},{23,9,15,27,31,17,11,29,1,..., dimensions={0} | all-to-all | bytes 524288 | tf_op jit(solution)/shard_map/all_to_all | solution.py:27
  63.1 6.0 %middle.1 = (f32[2048,128]{1,0:T(8,128)S(1)}, f32[128,512]{1,0:T(8,128)S(1)}, f32[512,512]{1,0:T(8,128)S(1)}) custom-call(f32[128,512]{1,0:T(8,128)S(1)} %bitcast.9, f32[512,512]{1,0:T(8,128)S(1)} %get-tuple-element.45.inverse_ref, f32[2048,128]{1,0:T(8,128)} %residual_ref.3, bf16[2048,512]{1,0:T(8,128)(2,1)} %get-tuple-element.46.high_ref, ...), custom_call_target="tpu_custom_call" | custom-call | flops 1610612736 | bytes 12845056 | tf_op jit(solution)/shard_map/middle/pallas_call | solution.py:222
  69.1 11.1 %all_to_all.32 = f32[16,8,512]{2,1,0:T(8,128)S(1)} all-to-all(f32[16,8,512]{2,1,0:T(8,128)S(1)} %bitcast.13), channel_id=1, replica_groups={{22,8,14,26,30,16,10,28,0,18,2,6,12,4,20,24},{23,9,15,27,31,17,11,29,1,..., dimensions={0} | all-to-all | bytes 524288 | tf_op jit(solution)/shard_map/all_to_all | solution.py:27
  80.2 11.2 %all_to_all.33 = f32[16,8,512]{2,1,0:T(8,128)S(1)} all-to-all(f32[16,8,512]{2,1,0:T(8,128)S(1)} %broadcast_in_dim.49), channel_id=1, replica_groups={{22,8,14,26,30,16,10,28,0,18,2,6,12,4,20,24},{23,9,15,27,31,17,11,29,1,..., dimensions={0} | all-to-all | bytes 524288 | tf_op jit(solution)/shard_map/all_to_all | solution.py:27
  91.4 5.4 %last.1 = f32[2048,128]{1,0:T(8,128)} custom-call(f32[128,512]{1,0:T(8,128)S(1)} %bitcast.10, f32[512,512]{1,0:T(8,128)S(1)} %get-tuple-element.51.inverse_ref, f32[2048,128]{1,0:T(8,128)S(1)} %get-tuple-element.52.residual_ref, bf16[2048,512]{1,0:T(8,128)(2,1)} %get-tuple-element.48.next_high.high_ref, bf16[2048,512]{1,0:T(8,128)(2,1)} %get-tuple-element.49.next_low.low_ref), custom_call_target="tpu_custom_call" | custom-call | flops 805306368 | bytes 6553600 | tf_op jit(solution)/shard_map/last/pallas_call | solution.py:222
  (5 shorter events, 0.1 us)
Async XLA Ops:
  0.0 3.7 %copy-start = (f32[2048,256]{1,0:T(8,128)S(1)}, f32[2048,256]{1,0:T(8,128)}, u32[]{:S(2)}) copy-start(f32[2048,256]{1,0:T(8,128)} %samples_ref.5) | copy-start | bytes 6291460
  3.8 30.2 %copy-start.1 = (f32[2048,128]{1,0:T(8,128)S(1)}, f32[2048,128]{1,0:T(8,128)}, u32[]{:S(2)}) copy-start(f32[2048,128]{1,0:T(8,128)} %residual_ref.3) | copy-start | bytes 3145732
  31.7 2.3 %collective-permute-start = (f32[768,256]{1,0:T(8,128)S(1)}, f32[768,256]{1,0:T(8,128)S(1)}, u32[]{:S(2)}, u32[]{:S(2)}) collective-permute-start(f32[768,256]{1,0:T(8,128)S(1)} %bitcast.11), channel_id=1, source_target_pairs={{1,0},{0,1},{3,2},{2,3},{5,4},{4,5},{7,6},{6,7},{9,8},{8,9},{11,10... | collective-permute-start | bytes 2359304 | tf_op jit(solution)/shard_map/ppermute | solution.py:277
  39.6 12.7 %all-to-all-start.2 = ((f32[16,8,512]{2,1,0:T(8,128)}), f32[16,8,512]{2,1,0:T(8,128)S(1)}, u32[]{:S(2)}, u32[]{:S(2)}) async-start(f32[16,8,512]{2,1,0:T(8,128)} %bitcast.3), calls=%async_computation.2 | async-start | bytes 524288 | tf_op jit(solution)/shard_map/all_to_all | solution.py:27

commit v7 on v6

--- a/solution.py
+++ b/solution.py
@@ -94,8 +94,8 @@
     return copy
 
 
-def halves(source, target, sems):
-    return [copy_of(source.at[at], target.at[at], sems.at[i]) for i, at in enumerate(pieces(source.shape[0], HALF_STEP))]
+def stage(live_ref):
+    return pl.when(live_ref[0] >= 0)
 
 
 def wait_all(*copies):
@@ -117,24 +117,30 @@
         found_ref[b] = found_in(held_ref, slots_ref[:, b * size : (b + 1) * size], 0, cores).astype(BF16)
 
 
-def make_columns(live_ref, samples_ref, points, high_v, low_v, high_ref, low_ref, sems):
+def make_columns(live_ref, samples_ref, points_of, columns_v, high_ref, low_ref, sems):
     rows, feat = samples_ref.shape
     scale = 0.5 / feat**0.5
     copies = []
     for index, half in enumerate(pieces(rows, HALF_STEP)):
-        for at in [pl.ds(half.start + part.start, part.size) for part in pieces(half.size)]:
-            base = dot3(split(samples_ref[at, :]), points, ((1,), (0,))) * scale + 1.0
-            slot = lax.broadcasted_iota(jnp.int32, (at.size, 1), 0) + at.start
-            high_v[at, :], low_v[at, :] = split(jnp.where(slot < live_ref[0], base * base * base, 0.0))
-        copies.append(copy_of(high_v.at[half], high_ref.at[half], sems.at[0, index]))
-        copies.append(copy_of(low_v.at[half], low_ref.at[half], sems.at[1, index]))
+
+        @stage(live_ref)
+        def _():
+            points = points_of()
+            for at in [pl.ds(half.start + part.start, part.size) for part in pieces(half.size)]:
+                base = dot3(split(samples_ref[at, :]), points, ((1,), (0,))) * scale + 1.0
+                slot = lax.broadcasted_iota(jnp.int32, (at.size, 1), 0) + at.start
+                columns_v[0, at, :], columns_v[1, at, :] = split(jnp.where(slot < live_ref[0], base * base * base, 0.0))
+
+        for kind, ref in enumerate((high_ref, low_ref)):
+            copies.append(copy_of(columns_v.at[kind, half], ref.at[half], sems.at[kind, index]))
     return copies
 
 
-def sum_high(residual, high):
-    width = residual[0].shape[1]
+def sum_of(residual, high, low):
+    width = residual.shape[1]
+    residual = split(residual)
     both = dot(jnp.concatenate(residual, axis=1), high, ((0,), (0,)))
-    return both[:width] + both[width:]
+    return both[:width] + both[width:] + dot(residual[0], low, ((0,), (0,)))
 
 
 def first_kernel(live_ref, residual_ref, samples_ref, slots_ref, found_ref, *refs):
@@ -146,70 +152,95 @@
         for shift, ref in enumerate(held):
             found = found + found_in(ref, slots_ref[:, b * size : (b + 1) * size], shift + 1, len(held) + 1)
         points_v[b, 0], points_v[b, 1] = found[:feat].astype(BF16), found[feat:].astype(BF16)
-    points_out = copy_of(points_v, points_ref, sems.at[3, 0])
-    points = (points_v[0, 0], points_v[0, 1])
-    copies = make_columns(live_ref, samples_ref, points, columns_v.at[0], columns_v.at[1], high_ref, low_ref, sems)
-    for index, at in enumerate(pieces(samples_ref.shape[0])):
-        residual = split(residual_ref[at, :])
-        term = sum_high(residual, columns_v[0, at, :]) + dot(residual[0], columns_v[1, at, :], ((0,), (0,)))
-        total_ref[...] = term if index == 0 else total_ref[...] + term
-    wait_all(points_out, *copies)
+    copies = make_columns(live_ref, samples_ref, lambda: (points_v[0, 0], points_v[0, 1]), columns_v, high_ref, low_ref, sems)
+    copies.append(copy_of(points_v, points_ref, sems.at[3, 0]))
+
+    @stage(live_ref)
+    def _():
+        for index, at in enumerate(pieces(samples_ref.shape[0])):
+            term = sum_of(residual_ref[at, :], columns_v[0, at, :], columns_v[1, at, :])
+            total_ref[...] = term if index == 0 else total_ref[...] + term
+
+    wait_all(*copies)
 
 
 def beside_kernel(block, live_ref, samples_ref, points_ref, inverse_ref, high_ref, low_ref, inverse_v, points_v, columns_v, sems):
     points_in = copy_of(points_ref.at[block + 1], points_v, sems.at[3, 0])
     inverse_in = copy_of(inverse_ref.at[block], inverse_v, sems.at[2, 0])
     points_in.wait()
-    points = (points_v[0], points_v[1])
-    wait_all(inverse_in, *make_columns(live_ref, samples_ref, points, columns_v.at[0], columns_v.at[1], high_ref, low_ref, sems))
+    copies = make_columns(live_ref, samples_ref, lambda: (points_v[0], points_v[1]), columns_v, high_ref, low_ref, sems)
+    wait_all(inverse_in, *copies)
 
 
 def coefs_of(sums_ref, inverse_ref):
     return jnp.concatenate(split(dot3(split(sums_ref[...]), split(inverse_ref[...]), ((1,), (1,))).T), axis=1)
 
 
-def update_high(coefs, residual_ref, columns_v, out_ref, waits):
-    width = residual_ref.shape[1]
-    for half, ready in zip(pieces(residual_ref.shape[0], HALF_STEP), waits):
-        wait_all(*ready)
-        both = dot(columns_v[0, half, :], coefs, ((1,), (0,)))
-        out_ref[half, :] = residual_ref[half, :] - (both[:, :width] + both[:, width:])
-
-
-def middle_kernel(block, sums_ref, inverse_ref, residual_ref, high_ref, low_ref, next_high, next_low, inverses, *refs):
-    out_ref, total_ref, inverse_v, residual_v, columns_v, next_v, sems = refs
-    residual_in = halves(residual_ref, residual_v, sems.at[0])
-    high_in = halves(high_ref, columns_v.at[0], sems.at[1])
-    low_in = halves(low_ref, columns_v.at[1], sems.at[2])
-    next_in = [copy_of(ref, next_v.at[kind], sems.at[3, kind]) for kind, ref in enumerate((next_high, next_low))]
-    inverse_in = copy_of(inverses.at[block + 1], inverse_v, sems.at[4, 0])
-    coefs = coefs_of(sums_ref, inverse_ref)
-    width = out_ref.shape[1]
-    update_high(coefs, residual_v, columns_v, out_ref, zip(residual_in, high_in))
-    wait_all(*low_in, next_in[0])
+def updated(residual, high, low, coefs):
+    width = residual.shape[1]
+    both = dot(high, coefs, ((1,), (0,)))
+    return residual - (both[:, :width] + both[:, width:] + dot(low, coefs[:, :width], ((1,), (0,))))
+
+
+def middle_kernel(block, live_ref, sums_ref, inverse_ref, residual_ref, high_ref, low_ref, next_high, next_low, inverses, *refs):
+    out_ref, total_ref, inverse_v, coefs_v, residual_v, columns_v, next_v, sems = refs
     parts = pieces(out_ref.shape[0])
-    for index, at in enumerate(parts):
-        residual = out_ref[at, :] - dot(columns_v[1, at, :], coefs[:, :width], ((1,), (0,)))
-        out_ref[at, :] = residual
-        term = sum_high(split(residual), next_v[0, at, :])
-        total_ref[...] = term if index == 0 else total_ref[...] + term
-    next_in[1].wait()
-    for at in parts:
-        total_ref[...] += dot(out_ref[at, :].astype(BF16), next_v[1, at, :], ((0,), (0,)))
+    first_in = [
+        [
+            copy_of(residual_ref.at[at], residual_v.at[at], sems.at[0, i]),
+            copy_of(high_ref.at[at], columns_v.at[0, at], sems.at[1, i]),
+            copy_of(low_ref.at[at], columns_v.at[1, at], sems.at[2, i]),
+        ]
+        for i, at in enumerate(parts)
+    ]
+    next_in = [
+        [copy_of(ref.at[at], next_v.at[kind, at], sems.at[3 + kind, i]) for kind, ref in enumerate((next_high, next_low))]
+        for i, at in enumerate(parts)
+    ]
+    inverse_in = copy_of(inverses.at[block + 1], inverse_v, sems.at[5, 0])
+
+    @stage(live_ref)
+    def _():
+        coefs_v[...] = coefs_of(sums_ref, inverse_ref)
+
+    for copies, at in zip(first_in, parts):
+        wait_all(*copies)
+
+        @stage(live_ref)
+        def _():
+            out_ref[at, :] = updated(residual_v[at, :], columns_v[0, at, :], columns_v[1, at, :], coefs_v[...])
+
+    for copies, at in zip(next_in, parts):
+        wait_all(*copies)
+
+        @stage(live_ref)
+        def _():
+            term = sum_of(out_ref[at, :], next_v[0, at, :], next_v[1, at, :])
+            total_ref[...] = term if at.start == 0 else total_ref[...] + term
+
     inverse_in.wait()
 
 
-def last_kernel(sums_ref, inverse_ref, residual_ref, high_ref, low_ref, out_ref, residual_v, columns_v, sems):
-    high_in = halves(high_ref, columns_v.at[0], sems.at[1])
-    low_in = halves(low_ref, columns_v.at[1], sems.at[2])
-    coefs = coefs_of(sums_ref, inverse_ref)
-    width = residual_ref.shape[1]
-    update_high(coefs, residual_ref, columns_v, residual_v, zip(high_in))
+def last_kernel(live_ref, sums_ref, inverse_ref, residual_ref, high_ref, low_ref, out_ref, coefs_v, residual_v, columns_v, sems):
+    parts = pieces(out_ref.shape[0])
+    columns_in = [
+        [copy_of(ref.at[at], columns_v.at[kind, at], sems.at[kind, i]) for kind, ref in enumerate((high_ref, low_ref))]
+        for i, at in enumerate(parts)
+    ]
+
+    @stage(live_ref)
+    def _():
+        coefs_v[...] = coefs_of(sums_ref, inverse_ref)
+
     out = []
-    for index, half in enumerate(pieces(out_ref.shape[0], HALF_STEP)):
-        low_in[index].wait()
-        residual_v[half, :] -= dot(columns_v[1, half, :], coefs[:, :width], ((1,), (0,)))
-        out.append(copy_of(residual_v.at[half], out_ref.at[half], sems.at[3, index]))
+    for copies, at in zip(columns_in, parts):
+        wait_all(*copies)
+
+        @stage(live_ref)
+        def _():
+            residual_v[at, :] = updated(residual_ref[at, :], columns_v[0, at, :], columns_v[1, at, :], coefs_v[...])
+
+        out.append(copy_of(residual_v.at[at], out_ref.at[at], sems.at[2, len(out)]))
     wait_all(*out)
 
 
@@ -289,7 +320,8 @@
     width = targets.shape[1]
     columns_v = pltpu.VMEM((2, rows_here, size), BF16)
     residual_v = pltpu.VMEM((rows_here, width), F32)
-    sems = pltpu.SemaphoreType.DMA((6, len(pieces(rows_here, HALF_STEP))))
+    coefs_v = pltpu.VMEM((size, 2 * width), BF16)
+    sems = pltpu.SemaphoreType.DMA((6, len(pieces(rows_here))))
     columns_out = [("H", (rows_here, size), BF16)] * 2
     inverse_out = ("V", (size, size), F32)
     totals_out = ("V", (width, size), F32)
@@ -316,10 +348,10 @@
         sums, (*following, inverse) = sum_over_rows(totals, groups, beside)
         residual, totals, inverse = local(
             functools.partial(middle_kernel, b),
-            (sums, inverse, residual, *columns, *following, block_inverse),
-            "VVHHHHHH",
+            (counts, sums, inverse, residual, *columns, *following, block_inverse),
+            "SVVHHHHHH",
             [("V", (rows_here, width), F32), totals_out, inverse_out],
-            [residual_v, columns_v, columns_v, sems],
+            [coefs_v, residual_v, columns_v, columns_v, sems],
             2 * work * width,
             "middle",
         )
@@ -327,10 +359,10 @@
     sums, _ = sum_over_rows(totals, groups, None)
     return local(
         last_kernel,
-        (sums, inverse, residual, *columns),
-        "VVVHH",
+        (counts, sums, inverse, residual, *columns),
+        "SVVVHH",
         [("H", (rows_here, width), F32)],
-        [residual_v, columns_v, sems],
+        [coefs_v, residual_v, columns_v, sems],
         work * width,
         "last",
     )

time: 97.2 us -> 95.6 us (0.984)
  Pallas kernels: 26.6 us -> 25 us
    pallas_call x6, Pallas kernels: 26.6 us -> 25 us  [local(): pl.pallas_call(kernel, out_shape=[SPACES[p](shape, dtype) for p, shape, d...]
  transfers between devices with their start and end apart: 2 -> 2, of which waited for: 2 -> 2; matrix products, arithmetic and copies ran while one was open for 0% -> 0% of each run, Pallas kernels for 6% -> 7%
where the time goes in v7:
time: 95.6 us; the launch traced here: 95.1 us
  blocking collectives  61.1 us (64%)
  Pallas kernels  25 us (26%)
  starting transfers between devices  6.03 us (6%)
  waiting for transfers between devices  1.97 us (2%)
    all_to_all x4, blocking collectives, exchange(): return lax.all_to_all(x, 'rows', 0, 0, axis_index_groups=[order])  61.1 us
    pallas_call x6, Pallas kernels, local(): pl.pallas_call(kernel, out_shape=[SPACES[p](shape, dtype) for p, shape, d...  25 us
    all_to_all x1, starting transfers between devices, exchange(): return lax.all_to_all(x, 'rows', 0, 0, axis_index_groups=[order])  6.03 us
  transfers between devices with their start and end apart: 2, of which 2 were waited for; matrix products, arithmetic and copies ran while one was open for 0% of the time, Pallas kernels for 7%

profile of v7, /device:TPU:0, one launch (start us, length us, event | category | flops | bytes accessed | tf_op | source)
XLA Modules:
  0.0 95.1 jit_solution(11231076344877534647)
XLA Ops:
  0.0 0.0 copy-start
  0.0 3.7 %pick.1 = (f32[48,256]{1,0:T(8,128)S(1)}, s32[1,1024]{1,0:T(1,128)S(1)}, s32[1]{0:T(128)S(4)}) custom-call(s32[2,512]{1,0:T(2,128)} %ids_ref.1, f32[2048,256]{1,0:T(8,128)} %samples_ref.5), custom_call_target="tpu_custom_call" | custom-call | bytes 2101248 | tf_op jit(solution)/shard_map/pick/pallas_call | solution.py:253
  3.7 0.0 copy-done
  3.7 0.1 broadcast_in_dim.47
  3.8 0.0 copy-start.1
  3.8 28.1 %all_to_all.30 = f32[16,48,256]{2,1,0:T(8,128)S(1)} all-to-all(f32[16,48,256]{2,1,0:T(8,128)S(1)} %broadcast_in_dim.47), channel_id=1, replica_groups={{14,12,2,28,0,10,4,26,8,30,16,20,24,22,18,6},{15,13,3,29,1,11,5,27,9,31..., dimensions={0} | all-to-all | bytes 1572864 | tf_op jit(solution)/shard_map/all_to_all | solution.py:27
  31.9 0.0 collective-permute-start
  32.5 1.0 %own.1.found_ref = bf16[2,512,512]{2,1,0:T(8,128)(2,1)S(1)} custom-call(s32[1,1024]{1,0:T(1,128)S(1)} %get-tuple-element.34.slots_ref, f32[768,256]{1,0:T(8,128)S(1)} %bitcast.12), custom_call_target="tpu_custom_call" | custom-call | flops 805306368 | bytes 790528 | tf_op jit(solution)/shard_map/own/pallas_call | solution.py:253
  33.6 0.6 collective-permute-done.refs_0_
  34.2 0.0 copy-done.1
  34.2 6.3 %first.1 = (bf16[2048,512]{1,0:T(8,128)(2,1)}, bf16[2048,512]{1,0:T(8,128)(2,1)}, f32[128,512]{1,0:T(8,128)}, bf16[2,2,256,512]{3,2,1,0:T(8,128)(2,1)}) custom-call(s32[1]{0:T(128)S(6)} %copy.9.live_ref, f32[2048,128]{1,0:T(8,128)S(1)} %copy-done.1, f32[2048,256]{1,0:T(8,128)S(1)} %copy-done, s32[1,1024]{1,0:T(1,128)S(1)} %get-tuple-element.34.slots_ref, ...), custom_call_target="tpu_custom_call" | custom-call | flops 2415919104 | bytes 4984836 | tf_op jit(solution)/shard_map/first/pallas_call | solution.py:253
  40.5 6.0 %all-to-all-start.2 = ((f32[16,8,512]{2,1,0:T(8,128)}), f32[16,8,512]{2,1,0:T(8,128)S(1)}, u32[]{:S(2)}, u32[]{:S(2)}) async-start(f32[16,8,512]{2,1,0:T(8,128)} %bitcast.3), calls=%async_computation.2 | async-start | bytes 524288 | tf_op jit(solution)/shard_map/all_to_all | solution.py:27
  46.5 5.3 %beside.1 = (bf16[2048,512]{1,0:T(8,128)(2,1)}, bf16[2048,512]{1,0:T(8,128)(2,1)}, f32[512,512]{1,0:T(8,128)S(1)}) custom-call(s32[1]{0:T(128)S(6)} %copy.9.live_ref, f32[2048,256]{1,0:T(8,128)S(1)} %copy-done, bf16[2,2,256,512]{3,2,1,0:T(8,128)(2,1)} %get-tuple-element.40.points_ref, f32[2,512,512]{2,1,0:T(8,128)} %inverses.1), custom_call_target="tpu_custom_call" | custom-call | flops 1610612736 | bytes 5242884 | tf_op jit(solution)/shard_map/beside/pallas_call | solution.py:253
  51.8 1.4 %all-to-all-done.2 = f32[16,8,512]{2,1,0:T(8,128)S(1)} async-done(((f32[16,8,512]{2,1,0:T(8,128)}), f32[16,8,512]{2,1,0:T(8,128)S(1)}, u32[]{:S(2)}, u32[]{:S(2)}) %all-to-all-start.2) | async-done | bytes 262176 | tf_op jit(solution)/shard_map/all_to_all | solution.py:27
  53.2 10.9 %all_to_all.31 = f32[16,8,512]{2,1,0:T(8,128)S(1)} all-to-all(f32[16,8,512]{2,1,0:T(8,128)S(1)} %broadcast_in_dim.48), channel_id=1, replica_groups={{22,8,14,26,30,16,10,28,0,18,2,6,12,4,20,24},{23,9,15,27,31,17,11,29,1,..., dimensions={0} | all-to-all | bytes 524288 | tf_op jit(solution)/shard_map/all_to_all | solution.py:27
  64.1 4.9 %middle.1 = (f32[2048,128]{1,0:T(8,128)S(1)}, f32[128,512]{1,0:T(8,128)S(1)}, f32[512,512]{1,0:T(8,128)S(1)}) custom-call(s32[1]{0:T(128)S(6)} %copy.9.live_ref, f32[128,512]{1,0:T(8,128)S(1)} %bitcast.9, f32[512,512]{1,0:T(8,128)S(1)} %get-tuple-element.45.inverse_ref, f32[2048,128]{1,0:T(8,128)} %residual_ref.3, ...), custom_call_target="tpu_custom_call" | custom-call | flops 1610612736 | bytes 12845060 | tf_op jit(solution)/shard_map/middle/pallas_call | solution.py:253
  68.9 11.1 %all_to_all.32 = f32[16,8,512]{2,1,0:T(8,128)S(1)} all-to-all(f32[16,8,512]{2,1,0:T(8,128)S(1)} %bitcast.13), channel_id=1, replica_groups={{22,8,14,26,30,16,10,28,0,18,2,6,12,4,20,24},{23,9,15,27,31,17,11,29,1,..., dimensions={0} | all-to-all | bytes 524288 | tf_op jit(solution)/shard_map/all_to_all | solution.py:27
  80.0 11.2 %all_to_all.33 = f32[16,8,512]{2,1,0:T(8,128)S(1)} all-to-all(f32[16,8,512]{2,1,0:T(8,128)S(1)} %broadcast_in_dim.49), channel_id=1, replica_groups={{22,8,14,26,30,16,10,28,0,18,2,6,12,4,20,24},{23,9,15,27,31,17,11,29,1,..., dimensions={0} | all-to-all | bytes 524288 | tf_op jit(solution)/shard_map/all_to_all | solution.py:27
  91.2 3.9 %last.1 = f32[2048,128]{1,0:T(8,128)} custom-call(s32[1]{0:T(128)S(6)} %copy.9.live_ref, f32[128,512]{1,0:T(8,128)S(1)} %bitcast.10, f32[512,512]{1,0:T(8,128)S(1)} %get-tuple-element.51.inverse_ref, f32[2048,128]{1,0:T(8,128)S(1)} %get-tuple-element.52.residual_ref, bf16[2048,512]{1,0:T(8,128)(2,1)} %get-tuple-element.48.next_high.high_ref, ...), custom_call_target="tpu_custom_call" | custom-call | flops 805306368 | bytes 6553604 | tf_op jit(solution)/shard_map/last/pallas_call | solution.py:253
  (5 shorter events, 0.1 us)
Async XLA Ops:
  0.0 3.7 %copy-start = (f32[2048,256]{1,0:T(8,128)S(1)}, f32[2048,256]{1,0:T(8,128)}, u32[]{:S(2)}) copy-start(f32[2048,256]{1,0:T(8,128)} %samples_ref.5) | copy-start | bytes 6291460
  3.8 30.4 %copy-start.1 = (f32[2048,128]{1,0:T(8,128)S(1)}, f32[2048,128]{1,0:T(8,128)}, u32[]{:S(2)}) copy-start(f32[2048,128]{1,0:T(8,128)} %residual_ref.3) | copy-start | bytes 3145732
  31.9 2.3 %collective-permute-start = (f32[768,256]{1,0:T(8,128)S(1)}, f32[768,256]{1,0:T(8,128)S(1)}, u32[]{:S(2)}, u32[]{:S(2)}) collective-permute-start(f32[768,256]{1,0:T(8,128)S(1)} %bitcast.11), channel_id=1, source_target_pairs={{1,0},{0,1},{3,2},{2,3},{5,4},{4,5},{7,6},{6,7},{9,8},{8,9},{11,10... | collective-permute-start | bytes 2359304 | tf_op jit(solution)/shard_map/ppermute | solution.py:308
  40.5 12.7 %all-to-all-start.2 = ((f32[16,8,512]{2,1,0:T(8,128)}), f32[16,8,512]{2,1,0:T(8,128)S(1)}, u32[]{:S(2)}, u32[]{:S(2)}) async-start(f32[16,8,512]{2,1,0:T(8,128)} %bitcast.3), calls=%async_computation.2 | async-start | bytes 524288 | tf_op jit(solution)/shard_map/all_to_all | solution.py:27

commit v8 on v7

--- a/solution.py
+++ b/solution.py
@@ -13,7 +13,8 @@
 ROWS_STEP = 512
 HALF_STEP = 1024
 LIMIT = 24 * 2**20
-POINTS_SEED = 14
+SLOW_SEED = 12
+FAST_SEED = 16
 SUMS_SEED = 152
 
 
@@ -23,8 +24,13 @@
     return order
 
 
-def exchange(x, order):
-    return lax.all_to_all(x, "rows", 0, 0, axis_index_groups=[order])
+def exchange(x, *orders):
+    return lax.all_to_all(x, "rows", 0, 0, axis_index_groups=list(orders))
+
+
+def gather(x, *orders):
+    count = len(orders[0])
+    return exchange(jnp.broadcast_to(x[None], (count, *x.shape)), *orders).reshape(count * x.shape[0], *x.shape[1:])
 
 
 def round_up(value, unit):
@@ -117,20 +123,15 @@
         found_ref[b] = found_in(held_ref, slots_ref[:, b * size : (b + 1) * size], 0, cores).astype(BF16)
 
 
-def make_columns(live_ref, samples_ref, points_of, columns_v, high_ref, low_ref, sems):
+def make_columns(live_ref, samples_ref, points, columns_v, high_ref, low_ref, sems):
     rows, feat = samples_ref.shape
     scale = 0.5 / feat**0.5
     copies = []
     for index, half in enumerate(pieces(rows, HALF_STEP)):
-
-        @stage(live_ref)
-        def _():
-            points = points_of()
-            for at in [pl.ds(half.start + part.start, part.size) for part in pieces(half.size)]:
-                base = dot3(split(samples_ref[at, :]), points, ((1,), (0,))) * scale + 1.0
-                slot = lax.broadcasted_iota(jnp.int32, (at.size, 1), 0) + at.start
-                columns_v[0, at, :], columns_v[1, at, :] = split(jnp.where(slot < live_ref[0], base * base * base, 0.0))
-
+        for at in [pl.ds(half.start + part.start, part.size) for part in pieces(half.size)]:
+            base = dot3(split(samples_ref[at, :]), points, ((1,), (0,))) * scale + 1.0
+            slot = lax.broadcasted_iota(jnp.int32, (at.size, 1), 0) + at.start
+            columns_v[0, at, :], columns_v[1, at, :] = split(jnp.where(slot < live_ref[0], base * base * base, 0.0))
         for kind, ref in enumerate((high_ref, low_ref)):
             copies.append(copy_of(columns_v.at[kind, half], ref.at[half], sems.at[kind, index]))
     return copies
@@ -152,7 +153,7 @@
         for shift, ref in enumerate(held):
             found = found + found_in(ref, slots_ref[:, b * size : (b + 1) * size], shift + 1, len(held) + 1)
         points_v[b, 0], points_v[b, 1] = found[:feat].astype(BF16), found[feat:].astype(BF16)
-    copies = make_columns(live_ref, samples_ref, lambda: (points_v[0, 0], points_v[0, 1]), columns_v, high_ref, low_ref, sems)
+    copies = make_columns(live_ref, samples_ref, (points_v[0, 0], points_v[0, 1]), columns_v, high_ref, low_ref, sems)
     copies.append(copy_of(points_v, points_ref, sems.at[3, 0]))
 
     @stage(live_ref)
@@ -168,7 +169,7 @@
     points_in = copy_of(points_ref.at[block + 1], points_v, sems.at[3, 0])
     inverse_in = copy_of(inverse_ref.at[block], inverse_v, sems.at[2, 0])
     points_in.wait()
-    copies = make_columns(live_ref, samples_ref, lambda: (points_v[0], points_v[1]), columns_v, high_ref, low_ref, sems)
+    copies = make_columns(live_ref, samples_ref, (points_v[0], points_v[1]), columns_v, high_ref, low_ref, sems)
     wait_all(inverse_in, *copies)
 
 
@@ -273,8 +274,7 @@
     if beside is not None:
         got, made = lax.optimization_barrier((got, beside()))
     own = jnp.sum(got, axis=0)
-    back = exchange(jnp.broadcast_to(own[None], (groups, piece, size)), order)
-    return back.reshape(groups * piece, size)[:width], made
+    return gather(own, order)[:width], made
 
 
 def on_device(groups, cores, counts, samples, targets, point_ids, block_inverse):
@@ -283,7 +283,10 @@
     mean = blocks * size / groups
     cap = round_up(max(1, round((mean + 4 * mean**0.5) / cores)), 8)
 
-    order = order_of(groups, POINTS_SEED)
+    fast = max(d for d in range(1, groups + 1) if groups % d == 0 and d * d <= groups)
+    slow = groups // fast
+    slow_order, fast_order = order_of(slow, SLOW_SEED), order_of(fast, FAST_SEED)
+    order = [s * fast + f for f in fast_order for s in slow_order]
     rows, slots, most = local(
         functools.partial(pick_kernel, order, cores, cap),
         (point_ids, samples),
@@ -304,7 +307,8 @@
         return jnp.sum(exchange(taken.reshape(groups, cap, feat), order), axis=0)
 
     rows = lax.cond(most[0] > cap * cores, general, lambda rows: rows, rows)
-    got = exchange(jnp.broadcast_to(rows[None], (groups, cap, feat)), order).reshape(groups * cap, feat)
+    got = gather(rows, *[[s * fast + f for s in slow_order] for f in range(fast)])
+    got = gather(got, *[[s * fast + f for f in fast_order] for s in range(slow)])
     held = [lax.ppermute(got, "tgt", [((c + shift) % cores, c) for c in range(cores)]) for shift in range(1, cores)]
     found = local(
         functools.partial(own_kernel, cores),

time: 95.6 us -> 95.7 us (level)
    all_to_all x4 -> x5, blocking collectives: 61.1 us -> 61.9 us  [exchange(): return lax.all_to_all(x, 'rows', 0, 0, axis_index_groups=list(orders))]
  transfers between devices with their start and end apart: 2 -> 2, of which waited for: 2 -> 2; matrix products, arithmetic and copies ran while one was open for 0% -> 0% of each run, Pallas kernels for 7% -> 6%
where the time goes in v8:
time: 95.7 us; the launch traced here: 95.6 us
  blocking collectives  61.9 us (65%)
  Pallas kernels  24.5 us (26%)
  starting transfers between devices  6.03 us (6%)
  waiting for transfers between devices  2.12 us (2%)
    all_to_all x5, blocking collectives, exchange(): return lax.all_to_all(x, 'rows', 0, 0, axis_index_groups=list(orders))  61.9 us
    pallas_call x6, Pallas kernels, local(): pl.pallas_call(kernel, out_shape=[SPACES[p](shape, dtype) for p, shape, d...  24.5 us
    all_to_all x1, starting transfers between devices, exchange(): return lax.all_to_all(x, 'rows', 0, 0, axis_index_groups=list(orders))  6.03 us
  transfers between devices with their start and end apart: 2, of which 2 were waited for; matrix products, arithmetic and copies ran while one was open for 0% of the time, Pallas kernels for 6%

profile of v8, /device:TPU:0, one launch (start us, length us, event | category | flops | bytes accessed | tf_op | source)
XLA Modules:
  0.0 95.6 jit_solution(4056039294800694598)
XLA Ops:
  0.0 0.0 copy-start
  0.0 3.7 %pick.1 = (f32[48,256]{1,0:T(8,128)S(1)}, s32[1,1024]{1,0:T(1,128)S(1)}, s32[1]{0:T(128)S(4)}) custom-call(s32[2,512]{1,0:T(2,128)} %ids_ref.1, f32[2048,256]{1,0:T(8,128)} %samples_ref.5), custom_call_target="tpu_custom_call" | custom-call | bytes 2101248 | tf_op jit(solution)/shard_map/pick/pallas_call | solution.py:254
  3.7 0.0 copy-done
  3.7 14.2 %all_to_all.35 = f32[4,48,256]{2,1,0:T(8,128)S(1)} all-to-all(f32[4,48,256]{2,1,0:T(8,128)S(1)} %broadcast_in_dim.54), channel_id=1, replica_groups={{0,16,8,24},{2,18,10,26},{4,20,12,28},{6,22,14,30},{1,17,9,25},{3,19,11..., dimensions={0} | all-to-all | bytes 393216 | tf_op jit(solution)/shard_map/all_to_all | solution.py:28
  18.0 0.1 broadcast_in_dim.56
  18.0 0.0 copy-start.1
  18.1 14.6 %all_to_all.36 = f32[4,192,256]{2,1,0:T(8,128)S(1)} all-to-all(f32[4,192,256]{2,1,0:T(8,128)S(1)} %broadcast_in_dim.56), channel_id=1, replica_groups={{0,6,2,4},{8,14,10,12},{16,22,18,20},{24,30,26,28},{1,7,3,5},{9,15,11,1..., dimensions={0} | all-to-all | bytes 1572864 | tf_op jit(solution)/shard_map/all_to_all | solution.py:28
  32.7 0.0 collective-permute-start
  33.3 1.0 %own.1.found_ref = bf16[2,512,512]{2,1,0:T(8,128)(2,1)S(1)} custom-call(s32[1,1024]{1,0:T(1,128)S(1)} %get-tuple-element.34.slots_ref, f32[768,256]{1,0:T(8,128)S(1)} %bitcast.13), custom_call_target="tpu_custom_call" | custom-call | flops 805306368 | bytes 790528 | tf_op jit(solution)/shard_map/own/pallas_call | solution.py:254
  34.3 0.6 collective-permute-done.refs_0_
  34.9 0.0 copy-done.1
  34.9 6.0 %first.1 = (bf16[2048,512]{1,0:T(8,128)(2,1)}, bf16[2048,512]{1,0:T(8,128)(2,1)}, f32[128,512]{1,0:T(8,128)}, bf16[2,2,256,512]{3,2,1,0:T(8,128)(2,1)}) custom-call(s32[1]{0:T(128)S(6)} %copy.9.live_ref, f32[2048,128]{1,0:T(8,128)S(1)} %copy-done.1, f32[2048,256]{1,0:T(8,128)S(1)} %copy-done, s32[1,1024]{1,0:T(1,128)S(1)} %get-tuple-element.34.slots_ref, ...), custom_call_target="tpu_custom_call" | custom-call | flops 2415919104 | bytes 4984836 | tf_op jit(solution)/shard_map/first/pallas_call | solution.py:254
  41.0 6.0 %all-to-all-start.3 = ((f32[16,8,512]{2,1,0:T(8,128)}), f32[16,8,512]{2,1,0:T(8,128)S(1)}, u32[]{:S(2)}, u32[]{:S(2)}) async-start(f32[16,8,512]{2,1,0:T(8,128)} %bitcast.4), calls=%async_computation.3 | async-start | bytes 524288 | tf_op jit(solution)/shard_map/all_to_all | solution.py:28
  47.0 5.1 %beside.1 = (bf16[2048,512]{1,0:T(8,128)(2,1)}, bf16[2048,512]{1,0:T(8,128)(2,1)}, f32[512,512]{1,0:T(8,128)S(1)}) custom-call(s32[1]{0:T(128)S(6)} %copy.9.live_ref, f32[2048,256]{1,0:T(8,128)S(1)} %copy-done, bf16[2,2,256,512]{3,2,1,0:T(8,128)(2,1)} %get-tuple-element.40.points_ref, f32[2,512,512]{2,1,0:T(8,128)} %inverses.1), custom_call_target="tpu_custom_call" | custom-call | flops 1610612736 | bytes 5242884 | tf_op jit(solution)/shard_map/beside/pallas_call | solution.py:254
  52.1 1.5 %all-to-all-done.3 = f32[16,8,512]{2,1,0:T(8,128)S(1)} async-done(((f32[16,8,512]{2,1,0:T(8,128)}), f32[16,8,512]{2,1,0:T(8,128)S(1)}, u32[]{:S(2)}, u32[]{:S(2)}) %all-to-all-start.3) | async-done | bytes 262176 | tf_op jit(solution)/shard_map/all_to_all | solution.py:28
  53.7 10.9 %all_to_all.37 = f32[16,8,512]{2,1,0:T(8,128)S(1)} all-to-all(f32[16,8,512]{2,1,0:T(8,128)S(1)} %broadcast_in_dim.57), channel_id=1, replica_groups={{22,8,14,26,30,16,10,28,0,18,2,6,12,4,20,24},{23,9,15,27,31,17,11,29,1,..., dimensions={0} | all-to-all | bytes 524288 | tf_op jit(solution)/shard_map/all_to_all | solution.py:28
  64.5 4.9 %middle.1 = (f32[2048,128]{1,0:T(8,128)S(1)}, f32[128,512]{1,0:T(8,128)S(1)}, f32[512,512]{1,0:T(8,128)S(1)}) custom-call(s32[1]{0:T(128)S(6)} %copy.9.live_ref, f32[128,512]{1,0:T(8,128)S(1)} %bitcast.10, f32[512,512]{1,0:T(8,128)S(1)} %get-tuple-element.45.inverse_ref, f32[2048,128]{1,0:T(8,128)} %residual_ref.3, ...), custom_call_target="tpu_custom_call" | custom-call | flops 1610612736 | bytes 12845060 | tf_op jit(solution)/shard_map/middle/pallas_call | solution.py:254
  69.4 11.0 %all_to_all.38 = f32[16,8,512]{2,1,0:T(8,128)S(1)} all-to-all(f32[16,8,512]{2,1,0:T(8,128)S(1)} %bitcast.14), channel_id=1, replica_groups={{22,8,14,26,30,16,10,28,0,18,2,6,12,4,20,24},{23,9,15,27,31,17,11,29,1,..., dimensions={0} | all-to-all | bytes 524288 | tf_op jit(solution)/shard_map/all_to_all | solution.py:28
  80.5 11.2 %all_to_all.39 = f32[16,8,512]{2,1,0:T(8,128)S(1)} all-to-all(f32[16,8,512]{2,1,0:T(8,128)S(1)} %broadcast_in_dim.58), channel_id=1, replica_groups={{22,8,14,26,30,16,10,28,0,18,2,6,12,4,20,24},{23,9,15,27,31,17,11,29,1,..., dimensions={0} | all-to-all | bytes 524288 | tf_op jit(solution)/shard_map/all_to_all | solution.py:28
  91.7 3.9 %last.1 = f32[2048,128]{1,0:T(8,128)} custom-call(s32[1]{0:T(128)S(6)} %copy.9.live_ref, f32[128,512]{1,0:T(8,128)S(1)} %bitcast.11, f32[512,512]{1,0:T(8,128)S(1)} %get-tuple-element.51.inverse_ref, f32[2048,128]{1,0:T(8,128)S(1)} %get-tuple-element.52.residual_ref, bf16[2048,512]{1,0:T(8,128)(2,1)} %get-tuple-element.48.next_high.high_ref, ...), custom_call_target="tpu_custom_call" | custom-call | flops 805306368 | bytes 6553604 | tf_op jit(solution)/shard_map/last/pallas_call | solution.py:254
  (6 shorter events, 0.1 us)
Async XLA Ops:
  0.0 3.7 %copy-start = (f32[2048,256]{1,0:T(8,128)S(1)}, f32[2048,256]{1,0:T(8,128)}, u32[]{:S(2)}) copy-start(f32[2048,256]{1,0:T(8,128)} %samples_ref.5) | copy-start | bytes 6291460
  18.0 16.9 %copy-start.1 = (f32[2048,128]{1,0:T(8,128)S(1)}, f32[2048,128]{1,0:T(8,128)}, u32[]{:S(2)}) copy-start(f32[2048,128]{1,0:T(8,128)} %residual_ref.3) | copy-start | bytes 3145732
  32.7 2.3 %collective-permute-start = (f32[768,256]{1,0:T(8,128)S(1)}, f32[768,256]{1,0:T(8,128)S(1)}, u32[]{:S(2)}, u32[]{:S(2)}) collective-permute-start(f32[768,256]{1,0:T(8,128)S(1)} %bitcast.12), channel_id=1, source_target_pairs={{1,0},{0,1},{3,2},{2,3},{5,4},{4,5},{7,6},{6,7},{9,8},{8,9},{11,10... | collective-permute-start | bytes 2359304 | tf_op jit(solution)/shard_map/ppermute | solution.py:312
  41.0 12.7 %all-to-all-start.3 = ((f32[16,8,512]{2,1,0:T(8,128)}), f32[16,8,512]{2,1,0:T(8,128)S(1)}, u32[]{:S(2)}, u32[]{:S(2)}) async-start(f32[16,8,512]{2,1,0:T(8,128)} %bitcast.4), calls=%async_computation.3 | async-start | bytes 524288 | tf_op jit(solution)/shard_map/all_to_all | solution.py:28

commit v9 on v7

--- a/solution.py
+++ b/solution.py
@@ -117,20 +117,15 @@
         found_ref[b] = found_in(held_ref, slots_ref[:, b * size : (b + 1) * size], 0, cores).astype(BF16)
 
 
-def make_columns(live_ref, samples_ref, points_of, columns_v, high_ref, low_ref, sems):
+def make_columns(live_ref, samples_ref, points, columns_v, high_ref, low_ref, sems):
     rows, feat = samples_ref.shape
     scale = 0.5 / feat**0.5
     copies = []
     for index, half in enumerate(pieces(rows, HALF_STEP)):
-
-        @stage(live_ref)
-        def _():
-            points = points_of()
-            for at in [pl.ds(half.start + part.start, part.size) for part in pieces(half.size)]:
-                base = dot3(split(samples_ref[at, :]), points, ((1,), (0,))) * scale + 1.0
-                slot = lax.broadcasted_iota(jnp.int32, (at.size, 1), 0) + at.start
-                columns_v[0, at, :], columns_v[1, at, :] = split(jnp.where(slot < live_ref[0], base * base * base, 0.0))
-
+        for at in [pl.ds(half.start + part.start, part.size) for part in pieces(half.size)]:
+            base = dot3(split(samples_ref[at, :]), points, ((1,), (0,))) * scale + 1.0
+            slot = lax.broadcasted_iota(jnp.int32, (at.size, 1), 0) + at.start
+            columns_v[0, at, :], columns_v[1, at, :] = split(jnp.where(slot < live_ref[0], base * base * base, 0.0))
         for kind, ref in enumerate((high_ref, low_ref)):
             copies.append(copy_of(columns_v.at[kind, half], ref.at[half], sems.at[kind, index]))
     return copies
@@ -152,23 +147,19 @@
         for shift, ref in enumerate(held):
             found = found + found_in(ref, slots_ref[:, b * size : (b + 1) * size], shift + 1, len(held) + 1)
         points_v[b, 0], points_v[b, 1] = found[:feat].astype(BF16), found[feat:].astype(BF16)
-    copies = make_columns(live_ref, samples_ref, lambda: (points_v[0, 0], points_v[0, 1]), columns_v, high_ref, low_ref, sems)
-    copies.append(copy_of(points_v, points_ref, sems.at[3, 0]))
-
-    @stage(live_ref)
-    def _():
-        for index, at in enumerate(pieces(samples_ref.shape[0])):
-            term = sum_of(residual_ref[at, :], columns_v[0, at, :], columns_v[1, at, :])
-            total_ref[...] = term if index == 0 else total_ref[...] + term
-
-    wait_all(*copies)
+    points_out = copy_of(points_v, points_ref, sems.at[3, 0])
+    copies = make_columns(live_ref, samples_ref, (points_v[0, 0], points_v[0, 1]), columns_v, high_ref, low_ref, sems)
+    for index, at in enumerate(pieces(samples_ref.shape[0])):
+        term = sum_of(residual_ref[at, :], columns_v[0, at, :], columns_v[1, at, :])
+        total_ref[...] = term if index == 0 else total_ref[...] + term
+    wait_all(points_out, *copies)
 
 
 def beside_kernel(block, live_ref, samples_ref, points_ref, inverse_ref, high_ref, low_ref, inverse_v, points_v, columns_v, sems):
     points_in = copy_of(points_ref.at[block + 1], points_v, sems.at[3, 0])
     inverse_in = copy_of(inverse_ref.at[block], inverse_v, sems.at[2, 0])
     points_in.wait()
-    copies = make_columns(live_ref, samples_ref, lambda: (points_v[0], points_v[1]), columns_v, high_ref, low_ref, sems)
+    copies = make_columns(live_ref, samples_ref, (points_v[0], points_v[1]), columns_v, high_ref, low_ref, sems)
     wait_all(inverse_in, *copies)
 
 

time: 95.6 us -> 94.7 us (level)
  transfers between devices with their start and end apart: 2 -> 2, of which waited for: 2 -> 2; matrix products, arithmetic and copies ran while one was open for 0% -> 0% of each run, Pallas kernels for 7% -> 6%
where the time goes in v9:
time: 94.7 us; the launch traced here: 94.2 us
  blocking collectives  61 us (64%)
  Pallas kernels  24.2 us (26%)
  starting transfers between devices  6.03 us (6%)
  waiting for transfers between devices  2.12 us (2%)
    all_to_all x4, blocking collectives, exchange(): return lax.all_to_all(x, 'rows', 0, 0, axis_index_groups=[order])  61 us
    pallas_call x6, Pallas kernels, local(): pl.pallas_call(kernel, out_shape=[SPACES[p](shape, dtype) for p, shape, d...  24.2 us
    all_to_all x1, starting transfers between devices, exchange(): return lax.all_to_all(x, 'rows', 0, 0, axis_index_groups=[order])  6.03 us
  transfers between devices with their start and end apart: 2, of which 2 were waited for; matrix products, arithmetic and copies ran while one was open for 0% of the time, Pallas kernels for 6%

profile of v9, /device:TPU:0, one launch (start us, length us, event | category | flops | bytes accessed | tf_op | source)
XLA Modules:
  0.0 94.2 jit_solution(9644466576192776212)
XLA Ops:
  0.0 0.0 copy-start
  0.0 3.7 %pick.1 = (f32[48,256]{1,0:T(8,128)S(1)}, s32[1,1024]{1,0:T(1,128)S(1)}, s32[1]{0:T(128)S(4)}) custom-call(s32[2,512]{1,0:T(2,128)} %ids_ref.1, f32[2048,256]{1,0:T(8,128)} %samples_ref.5), custom_call_target="tpu_custom_call" | custom-call | bytes 2101248 | tf_op jit(solution)/shard_map/pick/pallas_call | solution.py:244
  3.7 0.0 copy-done
  3.7 0.1 broadcast_in_dim.47
  3.8 0.0 copy-start.1
  3.8 27.9 %all_to_all.30 = f32[16,48,256]{2,1,0:T(8,128)S(1)} all-to-all(f32[16,48,256]{2,1,0:T(8,128)S(1)} %broadcast_in_dim.47), channel_id=1, replica_groups={{14,12,2,28,0,10,4,26,8,30,16,20,24,22,18,6},{15,13,3,29,1,11,5,27,9,31..., dimensions={0} | all-to-all | bytes 1572864 | tf_op jit(solution)/shard_map/all_to_all | solution.py:27
  31.7 0.0 collective-permute-start
  32.3 1.0 %own.1.found_ref = bf16[2,512,512]{2,1,0:T(8,128)(2,1)S(1)} custom-call(s32[1,1024]{1,0:T(1,128)S(1)} %get-tuple-element.34.slots_ref, f32[768,256]{1,0:T(8,128)S(1)} %bitcast.12), custom_call_target="tpu_custom_call" | custom-call | flops 805306368 | bytes 790528 | tf_op jit(solution)/shard_map/own/pallas_call | solution.py:244
  33.4 0.6 collective-permute-done.refs_0_
  34.0 0.0 copy-done.1
  34.0 5.7 %first.1 = (bf16[2048,512]{1,0:T(8,128)(2,1)}, bf16[2048,512]{1,0:T(8,128)(2,1)}, f32[128,512]{1,0:T(8,128)}, bf16[2,2,256,512]{3,2,1,0:T(8,128)(2,1)}) custom-call(s32[1]{0:T(128)S(6)} %copy.9.live_ref, f32[2048,128]{1,0:T(8,128)S(1)} %copy-done.1, f32[2048,256]{1,0:T(8,128)S(1)} %copy-done, s32[1,1024]{1,0:T(1,128)S(1)} %get-tuple-element.34.slots_ref, ...), custom_call_target="tpu_custom_call" | custom-call | flops 2415919104 | bytes 4984836 | tf_op jit(solution)/shard_map/first/pallas_call | solution.py:244
  39.6 6.0 %all-to-all-start.2 = ((f32[16,8,512]{2,1,0:T(8,128)}), f32[16,8,512]{2,1,0:T(8,128)S(1)}, u32[]{:S(2)}, u32[]{:S(2)}) async-start(f32[16,8,512]{2,1,0:T(8,128)} %bitcast.3), calls=%async_computation.2 | async-start | bytes 524288 | tf_op jit(solution)/shard_map/all_to_all | solution.py:27
  45.7 5.1 %beside.1 = (bf16[2048,512]{1,0:T(8,128)(2,1)}, bf16[2048,512]{1,0:T(8,128)(2,1)}, f32[512,512]{1,0:T(8,128)S(1)}) custom-call(s32[1]{0:T(128)S(6)} %copy.9.live_ref, f32[2048,256]{1,0:T(8,128)S(1)} %copy-done, bf16[2,2,256,512]{3,2,1,0:T(8,128)(2,1)} %get-tuple-element.40.points_ref, f32[2,512,512]{2,1,0:T(8,128)} %inverses.1), custom_call_target="tpu_custom_call" | custom-call | flops 1610612736 | bytes 5242884 | tf_op jit(solution)/shard_map/beside/pallas_call | solution.py:244
  50.8 1.5 %all-to-all-done.2 = f32[16,8,512]{2,1,0:T(8,128)S(1)} async-done(((f32[16,8,512]{2,1,0:T(8,128)}), f32[16,8,512]{2,1,0:T(8,128)S(1)}, u32[]{:S(2)}, u32[]{:S(2)}) %all-to-all-start.2) | async-done | bytes 262176 | tf_op jit(solution)/shard_map/all_to_all | solution.py:27
  52.3 10.9 %all_to_all.31 = f32[16,8,512]{2,1,0:T(8,128)S(1)} all-to-all(f32[16,8,512]{2,1,0:T(8,128)S(1)} %broadcast_in_dim.48), channel_id=1, replica_groups={{22,8,14,26,30,16,10,28,0,18,2,6,12,4,20,24},{23,9,15,27,31,17,11,29,1,..., dimensions={0} | all-to-all | bytes 524288 | tf_op jit(solution)/shard_map/all_to_all | solution.py:27
  63.2 4.9 %middle.1 = (f32[2048,128]{1,0:T(8,128)S(1)}, f32[128,512]{1,0:T(8,128)S(1)}, f32[512,512]{1,0:T(8,128)S(1)}) custom-call(s32[1]{0:T(128)S(6)} %copy.9.live_ref, f32[128,512]{1,0:T(8,128)S(1)} %bitcast.9, f32[512,512]{1,0:T(8,128)S(1)} %get-tuple-element.45.inverse_ref, f32[2048,128]{1,0:T(8,128)} %residual_ref.3, ...), custom_call_target="tpu_custom_call" | custom-call | flops 1610612736 | bytes 12845060 | tf_op jit(solution)/shard_map/middle/pallas_call | solution.py:244
  68.1 11.1 %all_to_all.32 = f32[16,8,512]{2,1,0:T(8,128)S(1)} all-to-all(f32[16,8,512]{2,1,0:T(8,128)S(1)} %bitcast.13), channel_id=1, replica_groups={{22,8,14,26,30,16,10,28,0,18,2,6,12,4,20,24},{23,9,15,27,31,17,11,29,1,..., dimensions={0} | all-to-all | bytes 524288 | tf_op jit(solution)/shard_map/all_to_all | solution.py:27
  79.2 11.2 %all_to_all.33 = f32[16,8,512]{2,1,0:T(8,128)S(1)} all-to-all(f32[16,8,512]{2,1,0:T(8,128)S(1)} %broadcast_in_dim.49), channel_id=1, replica_groups={{22,8,14,26,30,16,10,28,0,18,2,6,12,4,20,24},{23,9,15,27,31,17,11,29,1,..., dimensions={0} | all-to-all | bytes 524288 | tf_op jit(solution)/shard_map/all_to_all | solution.py:27
  90.4 3.9 %last.1 = f32[2048,128]{1,0:T(8,128)} custom-call(s32[1]{0:T(128)S(6)} %copy.9.live_ref, f32[128,512]{1,0:T(8,128)S(1)} %bitcast.10, f32[512,512]{1,0:T(8,128)S(1)} %get-tuple-element.51.inverse_ref, f32[2048,128]{1,0:T(8,128)S(1)} %get-tuple-element.52.residual_ref, bf16[2048,512]{1,0:T(8,128)(2,1)} %get-tuple-element.48.next_high.high_ref, ...), custom_call_target="tpu_custom_call" | custom-call | flops 805306368 | bytes 6553604 | tf_op jit(solution)/shard_map/last/pallas_call | solution.py:244
  (5 shorter events, 0.1 us)
Async XLA Ops:
  0.0 3.7 %copy-start = (f32[2048,256]{1,0:T(8,128)S(1)}, f32[2048,256]{1,0:T(8,128)}, u32[]{:S(2)}) copy-start(f32[2048,256]{1,0:T(8,128)} %samples_ref.5) | copy-start | bytes 6291460
  3.8 30.2 %copy-start.1 = (f32[2048,128]{1,0:T(8,128)S(1)}, f32[2048,128]{1,0:T(8,128)}, u32[]{:S(2)}) copy-start(f32[2048,128]{1,0:T(8,128)} %residual_ref.3) | copy-start | bytes 3145732
  31.7 2.3 %collective-permute-start = (f32[768,256]{1,0:T(8,128)S(1)}, f32[768,256]{1,0:T(8,128)S(1)}, u32[]{:S(2)}, u32[]{:S(2)}) collective-permute-start(f32[768,256]{1,0:T(8,128)S(1)} %bitcast.11), channel_id=1, source_target_pairs={{1,0},{0,1},{3,2},{2,3},{5,4},{4,5},{7,6},{6,7},{9,8},{8,9},{11,10... | collective-permute-start | bytes 2359304 | tf_op jit(solution)/shard_map/ppermute | solution.py:299
  39.6 12.7 %all-to-all-start.2 = ((f32[16,8,512]{2,1,0:T(8,128)}), f32[16,8,512]{2,1,0:T(8,128)S(1)}, u32[]{:S(2)}, u32[]{:S(2)}) async-start(f32[16,8,512]{2,1,0:T(8,128)} %bitcast.3), calls=%async_computation.2 | async-start | bytes 524288 | tf_op jit(solution)/shard_map/all_to_all | solution.py:27

commit v10 on v9

--- a/solution.py
+++ b/solution.py
@@ -44,45 +44,6 @@
     return dot(a[0], b[0], dims) + dot(a[0], b[1], dims) + dot(a[1], b[0], dims)
 
 
-def pick_kernel(order, cores, cap, ids_ref, samples_ref, rows_ref, slots_ref, most_ref, index_v, index_s, sems):
-    rows_here, groups = samples_ref.shape[0], len(order)
-    me, core = lax.axis_index("rows"), lax.axis_index("tgt")
-    ids = jnp.concatenate([ids_ref[b : b + 1, :] for b in range(ids_ref.shape[0])], axis=1)
-    count = ids.shape[1]
-    owner = lax.div(ids, jnp.int32(rows_here))
-    local = ids - owner * rows_here
-    mine = lax.broadcasted_iota(jnp.int32, (groups, count), 0) == owner
-    seen = mine.astype(jnp.int32)
-    lane = lax.broadcasted_iota(jnp.int32, (groups, count), 1)
-    step = 1
-    while step < count:
-        seen = seen + jnp.where(lane >= step, pltpu.roll(seen, step, 1), 0)
-        step *= 2
-    most = jnp.max(seen)
-    rank = jnp.sum(jnp.where(mine, seen, 0), axis=0, keepdims=True) - 1
-    half = lax.div(rank, jnp.int32(cap))
-    turn = jnp.zeros_like(owner)
-    for index, device in enumerate(order):
-        turn = jnp.where(owner == device, index, turn)
-    packed = (half * groups + turn) * cap + (rank - half * cap)
-    place = lax.broadcasted_iota(jnp.int32, (1, count), 1)
-    slots_ref[...] = jnp.where(most > cap * cores, place, packed)
-    most_ref[0] = most
-
-    wanted = lax.broadcasted_iota(jnp.int32, (cap, count), 0) + core * cap
-    chosen = jnp.where((wanted == rank) & (owner == me), local, 0)
-    index_v[...] = jnp.broadcast_to(jnp.sum(chosen, axis=1, keepdims=True), index_v.shape)
-    move = pltpu.make_async_copy(index_v, index_s, sems.at[0])
-    move.start()
-    move.wait()
-
-    @pl.loop(0, cap)
-    def _(k):
-        pltpu.make_async_copy(samples_ref.at[pl.ds(index_s[k, 0], 1)], rows_ref.at[pl.ds(k, 1)], sems.at[1]).start()
-
-    pltpu.make_async_copy(samples_ref.at[pl.ds(0, cap)], rows_ref, sems.at[1]).wait()
-
-
 def pieces(rows, step=ROWS_STEP):
     step = min(step, rows)
     return [pl.ds(start, step) for start in range(0, rows, step)]
@@ -101,6 +62,51 @@
 def wait_all(*copies):
     for copy in copies:
         copy.wait()
+
+
+def pick_kernel(order, cores, cap, live_ref, ids_ref, samples_ref, rows_ref, slots_ref, most_ref, parts_ref, samples_v, chosen_v, sems):
+    (rows_here, feat), groups = samples_ref.shape, len(order)
+    parts = pieces(rows_here, HALF_STEP)
+    copies = [copy_of(samples_ref.at[at], samples_v.at[at], sems.at[i]) for i, at in enumerate(parts)]
+    me, core = lax.axis_index("rows"), lax.axis_index("tgt")
+
+    @stage(live_ref)
+    def _():
+        ids = jnp.concatenate([ids_ref[b : b + 1, :] for b in range(ids_ref.shape[0])], axis=1)
+        count = ids.shape[1]
+        owner = lax.div(ids, jnp.int32(rows_here))
+        local = ids - owner * rows_here
+        mine = lax.broadcasted_iota(jnp.int32, (groups, count), 0) == owner
+        seen = mine.astype(jnp.int32)
+        lane = lax.broadcasted_iota(jnp.int32, (groups, count), 1)
+        step = 1
+        while step < count:
+            seen = seen + jnp.where(lane >= step, pltpu.roll(seen, step, 1), 0)
+            step *= 2
+        most = jnp.max(seen)
+        rank = jnp.sum(jnp.where(mine, seen, 0), axis=0, keepdims=True) - 1
+        half = lax.div(rank, jnp.int32(cap))
+        turn = jnp.zeros_like(owner)
+        for index, device in enumerate(order):
+            turn = jnp.where(owner == device, index, turn)
+        packed = (half * groups + turn) * cap + (rank - half * cap)
+        place = lax.broadcasted_iota(jnp.int32, (1, count), 1)
+        slots_ref[...] = jnp.where(most > cap * cores, place, packed)
+        most_ref[0] = most
+
+        wanted = lax.broadcasted_iota(jnp.int32, (cap, count), 0) + core * cap
+        sent = jnp.sum(jnp.where((wanted == rank) & (owner == me), local, 0), axis=1, keepdims=True)
+        chosen_v[...] = jnp.where(lax.broadcasted_iota(jnp.int32, (cap, rows_here), 1) == sent, 1.0, 0.0).astype(BF16)
+
+    for copy, at in zip(copies, parts):
+        copy.wait()
+
+        @stage(live_ref)
+        def _():
+            parts_ref[at, :] = jnp.concatenate(split(samples_v[at, :]), axis=1)
+            both = dot(chosen_v[:, at], parts_ref[at, :], ((1,), (0,)))
+            found = both[:, :feat] + both[:, feat:]
+            rows_ref[...] = found if at.start == 0 else rows_ref[...] + found
 
 
 def found_in(ref, slots, shift, cores):
@@ -118,12 +124,12 @@
 
 
 def make_columns(live_ref, samples_ref, points, columns_v, high_ref, low_ref, sems):
-    rows, feat = samples_ref.shape
+    rows, feat = samples_ref.shape[0], samples_ref.shape[1] // 2
     scale = 0.5 / feat**0.5
     copies = []
     for index, half in enumerate(pieces(rows, HALF_STEP)):
         for at in [pl.ds(half.start + part.start, part.size) for part in pieces(half.size)]:
-            base = dot3(split(samples_ref[at, :]), points, ((1,), (0,))) * scale + 1.0
+            base = dot3((samples_ref[at, :feat], samples_ref[at, feat:]), points, ((1,), (0,))) * scale + 1.0
             slot = lax.broadcasted_iota(jnp.int32, (at.size, 1), 0) + at.start
             columns_v[0, at, :], columns_v[1, at, :] = split(jnp.where(slot < live_ref[0], base * base * base, 0.0))
         for kind, ref in enumerate((high_ref, low_ref)):
@@ -141,7 +147,7 @@
 def first_kernel(live_ref, residual_ref, samples_ref, slots_ref, found_ref, *refs):
     *held, high_ref, low_ref, total_ref, points_ref, points_v, columns_v, sems = refs
     blocks, _, size = found_ref.shape
-    feat = samples_ref.shape[1]
+    feat = samples_ref.shape[1] // 2
     for b in range(blocks):
         found = found_ref[b].astype(F32)
         for shift, ref in enumerate(held):
@@ -275,13 +281,17 @@
     cap = round_up(max(1, round((mean + 4 * mean**0.5) / cores)), 8)
 
     order = order_of(groups, POINTS_SEED)
-    rows, slots, most = local(
+    rows, slots, most, samples_split = local(
         functools.partial(pick_kernel, order, cores, cap),
-        (point_ids, samples),
-        "VH",
-        [("V", (cap, feat), F32), ("V", (1, blocks * size), jnp.int32), ("S", (1,), jnp.int32)],
-        [pltpu.VMEM((cap, 128), jnp.int32), pltpu.SMEM((cap, 128), jnp.int32), pltpu.SemaphoreType.DMA((2,))],
-        0,
+        (counts, point_ids, samples),
+        "SVH",
+        [("V", (cap, feat), F32), ("V", (1, blocks * size), jnp.int32), ("S", (1,), jnp.int32), ("V", (rows_here, 2 * feat), BF16)],
+        [
+            pltpu.VMEM(samples.shape, F32),
+            pltpu.VMEM((cap, rows_here), BF16),
+            pltpu.SemaphoreType.DMA((len(pieces(rows_here, HALF_STEP)),)),
+        ],
+        4 * cap * rows_here * feat,
         "pick",
     )
 
@@ -321,7 +331,7 @@
     residual = targets
     *columns, totals, points = local(
         first_kernel,
-        (counts, residual, samples, slots, found, *held),
+        (counts, residual, samples_split, slots, found, *held),
         "SVVVV" + "V" * len(held),
         [*columns_out, totals_out, ("H", (blocks, 2, feat, size), BF16)],
         [pltpu.VMEM((blocks, 2, feat, size), BF16), columns_v, sems],
@@ -331,7 +341,7 @@
     for b in range(blocks - 1):
 
         def beside(b=b, points=points):
-            args = (counts, samples, points, block_inverse)
+            args = (counts, samples_split, points, block_inverse)
             outs = [*columns_out, inverse_out]
             scratch = [pltpu.VMEM((2, feat, size), BF16), columns_v, sems]
             return local(functools.partial(beside_kernel, b), args, "SVHH", outs, scratch, work * feat, "beside")

time: 94.7 us -> 93.1 us (0.983)
  Pallas kernels: 24.2 us -> 22.6 us
    pallas_call x6, Pallas kernels: 24.2 us -> 22.6 us  [local(): pl.pallas_call(kernel, out_shape=[SPACES[p](shape, dtype) for p, shape, d...]
where the time goes in v10:
time: 93.1 us; the launch traced here: 92.7 us
  blocking collectives  60.1 us (65%)
  Pallas kernels  22.6 us (24%)
  starting transfers between devices  6.05 us (6%)
  waiting for transfers between devices  3.01 us (3%)
    all_to_all x4, blocking collectives, exchange(): return lax.all_to_all(x, 'rows', 0, 0, axis_index_groups=[order])  60.1 us
    pallas_call x6, Pallas kernels, local(): pl.pallas_call(kernel, out_shape=[SPACES[p](shape, dtype) for p, shape, d...  22.6 us
    all_to_all x1, starting transfers between devices, exchange(): return lax.all_to_all(x, 'rows', 0, 0, axis_index_groups=[order])  6.05 us
  transfers between devices with their start and end apart: 2, of which 2 were waited for; matrix products, arithmetic and copies ran while one was open for 0% of the time, Pallas kernels for 6%

profile of v10, /device:TPU:0, one launch (start us, length us, event | category | flops | bytes accessed | tf_op | source)
XLA Modules:
  0.0 92.7 jit_solution(1932747728768378095)
XLA Ops:
  0.7 2.5 %pick.1 = (f32[48,256]{1,0:T(8,128)S(1)}, s32[1,1024]{1,0:T(1,128)S(1)}, s32[1]{0:T(128)S(4)}, bf16[2048,512]{1,0:T(8,128)(2,1)S(1)}) custom-call(s32[1]{0:T(128)S(6)} %copy.9.live_ref, s32[2,512]{1,0:T(2,128)} %ids_ref.1, f32[2048,256]{1,0:T(8,128)} %samples_ref.1), custom_call_target="tpu_custom_call" | custom-call | flops 100663296 | bytes 2101252 | tf_op jit(solution)/shard_map/pick/pallas_call | solution.py:250
  3.2 0.1 broadcast_in_dim.47
  3.3 0.0 copy-start
  3.3 27.0 %all_to_all.30 = f32[16,48,256]{2,1,0:T(8,128)S(1)} all-to-all(f32[16,48,256]{2,1,0:T(8,128)S(1)} %broadcast_in_dim.47), channel_id=1, replica_groups={{14,12,2,28,0,10,4,26,8,30,16,20,24,22,18,6},{15,13,3,29,1,11,5,27,9,31..., dimensions={0} | all-to-all | bytes 1572864 | tf_op jit(solution)/shard_map/all_to_all | solution.py:27
  30.3 0.0 collective-permute-start
  30.4 1.0 %own.1.found_ref = bf16[2,512,512]{2,1,0:T(8,128)(2,1)S(1)} custom-call(s32[1,1024]{1,0:T(1,128)S(1)} %get-tuple-element.36.slots_ref, f32[768,256]{1,0:T(8,128)S(1)} %bitcast.12), custom_call_target="tpu_custom_call" | custom-call | flops 805306368 | bytes 790528 | tf_op jit(solution)/shard_map/own/pallas_call | solution.py:250
  31.4 1.3 %collective-permute-done.refs_0_ = f32[768,256]{1,0:T(8,128)S(1)} collective-permute-done((f32[768,256]{1,0:T(8,128)S(1)}, f32[768,256]{1,0:T(8,128)S(1)}, u32[]{:S(2)}, u32[]{:S(2)}) %collective-permute-start) | collective-permute-done | bytes 786464 | tf_op jit(solution)/shard_map/ppermute | solution.py:309
  32.6 0.0 copy-done
  32.6 5.4 %first.1 = (bf16[2048,512]{1,0:T(8,128)(2,1)}, bf16[2048,512]{1,0:T(8,128)(2,1)}, f32[128,512]{1,0:T(8,128)}, bf16[2,2,256,512]{3,2,1,0:T(8,128)(2,1)}) custom-call(s32[1]{0:T(128)S(6)} %copy.9.live_ref, f32[2048,128]{1,0:T(8,128)S(1)} %copy-done, bf16[2048,512]{1,0:T(8,128)(2,1)S(1)} %get-tuple-element.35.samples_ref, ...), custom_call_target="tpu_custom_call" | custom-call | flops 2415919104 | bytes 4984836 | tf_op jit(solution)/shard_map/first/pallas_call | solution.py:250
  38.1 6.0 %all-to-all-start.2 = ((f32[16,8,512]{2,1,0:T(8,128)}), f32[16,8,512]{2,1,0:T(8,128)S(1)}, u32[]{:S(2)}, u32[]{:S(2)}) async-start(f32[16,8,512]{2,1,0:T(8,128)} %bitcast.3), calls=%async_computation.2 | async-start | bytes 524288 | tf_op jit(solution)/shard_map/all_to_all | solution.py:27
  44.1 4.9 %beside.1 = (bf16[2048,512]{1,0:T(8,128)(2,1)}, bf16[2048,512]{1,0:T(8,128)(2,1)}, f32[512,512]{1,0:T(8,128)S(1)}) custom-call(s32[1]{0:T(128)S(6)} %copy.9.live_ref, bf16[2048,512]{1,0:T(8,128)(2,1)S(1)} %get-tuple-element.35.samples_ref, bf16[2,2,256,512]{3,2,1,0:T(8,128)(2,1)} %get-tuple-element.42.points_ref, f32[2,512,512]{2,1,0:T(8,128)} %inverses.1), custom_call_target="tpu_custom_call" | custom-call | flops 1610612736 | bytes 5242884 | tf_op jit(solution)/shard_map/beside/pallas_call | solution.py:250
  49.0 1.7 %all-to-all-done.2 = f32[16,8,512]{2,1,0:T(8,128)S(1)} async-done(((f32[16,8,512]{2,1,0:T(8,128)}), f32[16,8,512]{2,1,0:T(8,128)S(1)}, u32[]{:S(2)}, u32[]{:S(2)}) %all-to-all-start.2) | async-done | bytes 262176 | tf_op jit(solution)/shard_map/all_to_all | solution.py:27
  50.8 10.9 %all_to_all.31 = f32[16,8,512]{2,1,0:T(8,128)S(1)} all-to-all(f32[16,8,512]{2,1,0:T(8,128)S(1)} %broadcast_in_dim.48), channel_id=1, replica_groups={{22,8,14,26,30,16,10,28,0,18,2,6,12,4,20,24},{23,9,15,27,31,17,11,29,1,..., dimensions={0} | all-to-all | bytes 524288 | tf_op jit(solution)/shard_map/all_to_all | solution.py:27
  61.7 4.9 %middle.1 = (f32[2048,128]{1,0:T(8,128)S(1)}, f32[128,512]{1,0:T(8,128)S(1)}, f32[512,512]{1,0:T(8,128)S(1)}) custom-call(s32[1]{0:T(128)S(6)} %copy.9.live_ref, f32[128,512]{1,0:T(8,128)S(1)} %bitcast.9, f32[512,512]{1,0:T(8,128)S(1)} %get-tuple-element.47.inverse_ref, f32[2048,128]{1,0:T(8,128)} %residual_ref.3, ...), custom_call_target="tpu_custom_call" | custom-call | flops 1610612736 | bytes 12845060 | tf_op jit(solution)/shard_map/middle/pallas_call | solution.py:250
  66.5 11.1 %all_to_all.32 = f32[16,8,512]{2,1,0:T(8,128)S(1)} all-to-all(f32[16,8,512]{2,1,0:T(8,128)S(1)} %bitcast.13), channel_id=1, replica_groups={{22,8,14,26,30,16,10,28,0,18,2,6,12,4,20,24},{23,9,15,27,31,17,11,29,1,..., dimensions={0} | all-to-all | bytes 524288 | tf_op jit(solution)/shard_map/all_to_all | solution.py:27
  77.6 11.2 %all_to_all.33 = f32[16,8,512]{2,1,0:T(8,128)S(1)} all-to-all(f32[16,8,512]{2,1,0:T(8,128)S(1)} %broadcast_in_dim.49), channel_id=1, replica_groups={{22,8,14,26,30,16,10,28,0,18,2,6,12,4,20,24},{23,9,15,27,31,17,11,29,1,..., dimensions={0} | all-to-all | bytes 524288 | tf_op jit(solution)/shard_map/all_to_all | solution.py:27
  88.8 3.9 %last.1 = f32[2048,128]{1,0:T(8,128)} custom-call(s32[1]{0:T(128)S(6)} %copy.9.live_ref, f32[128,512]{1,0:T(8,128)S(1)} %bitcast.10, f32[512,512]{1,0:T(8,128)S(1)} %get-tuple-element.53.inverse_ref, f32[2048,128]{1,0:T(8,128)S(1)} %get-tuple-element.54.residual_ref, bf16[2048,512]{1,0:T(8,128)(2,1)} %get-tuple-element.50.next_high.high_ref, ...), custom_call_target="tpu_custom_call" | custom-call | flops 805306368 | bytes 6553604 | tf_op jit(solution)/shard_map/last/pallas_call | solution.py:250
  (5 shorter events, 0.1 us)
Async XLA Ops:
  3.3 29.3 %copy-start = (f32[2048,128]{1,0:T(8,128)S(1)}, f32[2048,128]{1,0:T(8,128)}, u32[]{:S(2)}) copy-start(f32[2048,128]{1,0:T(8,128)} %residual_ref.3) | copy-start | bytes 3145732
  30.3 2.3 %collective-permute-start = (f32[768,256]{1,0:T(8,128)S(1)}, f32[768,256]{1,0:T(8,128)S(1)}, u32[]{:S(2)}, u32[]{:S(2)}) collective-permute-start(f32[768,256]{1,0:T(8,128)S(1)} %bitcast.11), channel_id=1, source_target_pairs={{1,0},{0,1},{3,2},{2,3},{5,4},{4,5},{7,6},{6,7},{9,8},{8,9},{11,10... | collective-permute-start | bytes 2359304 | tf_op jit(solution)/shard_map/ppermute | solution.py:309
  38.1 12.7 %all-to-all-start.2 = ((f32[16,8,512]{2,1,0:T(8,128)}), f32[16,8,512]{2,1,0:T(8,128)S(1)}, u32[]{:S(2)}, u32[]{:S(2)}) async-start(f32[16,8,512]{2,1,0:T(8,128)} %bitcast.3), calls=%async_computation.2 | async-start | bytes 524288 | tf_op jit(solution)/shard_map/all_to_all | solution.py:27

commit v11 on v10

--- a/solution.py
+++ b/solution.py
@@ -144,27 +144,37 @@
     return both[:width] + both[width:] + dot(residual[0], low, ((0,), (0,)))
 
 
-def first_kernel(live_ref, residual_ref, samples_ref, slots_ref, found_ref, *refs):
-    *held, high_ref, low_ref, total_ref, points_ref, points_v, columns_v, sems = refs
+def points_of(found, held, slots):
+    total = found.astype(F32)
+    for shift, ref in enumerate(held):
+        total = total + found_in(ref, slots, shift + 1, len(held) + 1)
+    feat = total.shape[0] // 2
+    return total[:feat].astype(BF16), total[feat:].astype(BF16)
+
+
+def first_kernel(cores, live_ref, residual_ref, samples_ref, slots_ref, found_ref, *refs):
+    held, refs = refs[: cores - 1], refs[cores - 1 :]
+    high_ref, low_ref, total_ref, slots_out, found_out, *held_out, points_v, columns_v, sems = refs
     blocks, _, size = found_ref.shape
-    feat = samples_ref.shape[1] // 2
-    for b in range(blocks):
-        found = found_ref[b].astype(F32)
-        for shift, ref in enumerate(held):
-            found = found + found_in(ref, slots_ref[:, b * size : (b + 1) * size], shift + 1, len(held) + 1)
-        points_v[b, 0], points_v[b, 1] = found[:feat].astype(BF16), found[feat:].astype(BF16)
-    points_out = copy_of(points_v, points_ref, sems.at[3, 0])
-    copies = make_columns(live_ref, samples_ref, (points_v[0, 0], points_v[0, 1]), columns_v, high_ref, low_ref, sems)
+    copies = [copy_of(found_ref.at[pl.ds(1, blocks - 1)], found_out, sems.at[3, 0]), copy_of(slots_ref, slots_out, sems.at[3, 1])]
+    copies += [copy_of(ref, out, sems.at[4, i]) for i, (ref, out) in enumerate(zip(held, held_out))]
+    points_v[0], points_v[1] = points_of(found_ref[0], held, slots_ref[:, :size])
+    copies += make_columns(live_ref, samples_ref, (points_v[0], points_v[1]), columns_v, high_ref, low_ref, sems)
     for index, at in enumerate(pieces(samples_ref.shape[0])):
         term = sum_of(residual_ref[at, :], columns_v[0, at, :], columns_v[1, at, :])
         total_ref[...] = term if index == 0 else total_ref[...] + term
-    wait_all(points_out, *copies)
-
-
-def beside_kernel(block, live_ref, samples_ref, points_ref, inverse_ref, high_ref, low_ref, inverse_v, points_v, columns_v, sems):
-    points_in = copy_of(points_ref.at[block + 1], points_v, sems.at[3, 0])
+    wait_all(*copies)
+
+
+def beside_kernel(block, cores, live_ref, samples_ref, slots_ref, found_ref, inverse_ref, *refs):
+    held, refs = refs[: cores - 1], refs[cores - 1 :]
+    high_ref, low_ref, inverse_v, points_v, slots_v, found_v, *held_v, columns_v, sems = refs
+    size = found_v.shape[1]
+    in_flight = [copy_of(found_ref.at[block], found_v, sems.at[3, 0]), copy_of(slots_ref, slots_v, sems.at[3, 1])]
+    in_flight += [copy_of(ref, v, sems.at[4, i]) for i, (ref, v) in enumerate(zip(held, held_v))]
     inverse_in = copy_of(inverse_ref.at[block], inverse_v, sems.at[2, 0])
-    points_in.wait()
+    wait_all(*in_flight)
+    points_v[0], points_v[1] = points_of(found_v[...], held_v, slots_v[:, (block + 1) * size : (block + 2) * size])
     copies = make_columns(live_ref, samples_ref, (points_v[0], points_v[1]), columns_v, high_ref, low_ref, sems)
     wait_all(inverse_in, *copies)
 
@@ -322,29 +332,49 @@
     columns_v = pltpu.VMEM((2, rows_here, size), BF16)
     residual_v = pltpu.VMEM((rows_here, width), F32)
     coefs_v = pltpu.VMEM((size, 2 * width), BF16)
-    sems = pltpu.SemaphoreType.DMA((6, len(pieces(rows_here))))
+    sems = pltpu.SemaphoreType.DMA((6, max(cores, len(pieces(rows_here)))))
     columns_out = [("H", (rows_here, size), BF16)] * 2
     inverse_out = ("V", (size, size), F32)
     totals_out = ("V", (width, size), F32)
     work = 6 * rows_here * size
 
     residual = targets
-    *columns, totals, points = local(
-        first_kernel,
+    points_v = pltpu.VMEM((2, feat, size), BF16)
+    high, low, totals, slots_out, found, *held = local(
+        functools.partial(first_kernel, cores),
         (counts, residual, samples_split, slots, found, *held),
         "SVVVV" + "V" * len(held),
-        [*columns_out, totals_out, ("H", (blocks, 2, feat, size), BF16)],
-        [pltpu.VMEM((blocks, 2, feat, size), BF16), columns_v, sems],
+        [
+            *columns_out,
+            totals_out,
+            ("H", slots.shape, jnp.int32),
+            ("H", (blocks - 1, 2 * feat, size), BF16),
+            *[("H", h.shape, F32) for h in held],
+        ],
+        [points_v, columns_v, sems],
         work * (feat + width),
         "first",
     )
+    columns = [high, low]
     for b in range(blocks - 1):
 
-        def beside(b=b, points=points):
-            args = (counts, samples_split, points, block_inverse)
-            outs = [*columns_out, inverse_out]
-            scratch = [pltpu.VMEM((2, feat, size), BF16), columns_v, sems]
-            return local(functools.partial(beside_kernel, b), args, "SVHH", outs, scratch, work * feat, "beside")
+        def beside(b=b):
+            return local(
+                functools.partial(beside_kernel, b, cores),
+                (counts, samples_split, slots_out, found, block_inverse, *held),
+                "SVHHH" + "H" * len(held),
+                [*columns_out, inverse_out],
+                [
+                    points_v,
+                    pltpu.VMEM(slots.shape, jnp.int32),
+                    pltpu.VMEM((2 * feat, size), BF16),
+                    *[pltpu.VMEM(h.shape, F32) for h in held],
+                    columns_v,
+                    sems,
+                ],
+                work * feat,
+                "beside",
+            )
 
         sums, (*following, inverse) = sum_over_rows(totals, groups, beside)
         residual, totals, inverse = local(

time: 93.1 us -> 92.8 us (level)
  transfers between devices with their start and end apart: 2 -> 2, of which waited for: 2 -> 2; matrix products, arithmetic and copies ran while one was open for 0% -> 0% of each run, Pallas kernels for 6% -> 7%
where the time goes in v11:
time: 92.8 us; the launch traced here: 92.3 us
  blocking collectives  60.1 us (65%)
  Pallas kernels  23.1 us (25%)
  starting transfers between devices  6.04 us (7%)
  waiting for transfers between devices  2.18 us (2%)
    all_to_all x4, blocking collectives, exchange(): return lax.all_to_all(x, 'rows', 0, 0, axis_index_groups=[order])  60.1 us
    pallas_call x6, Pallas kernels, local(): pl.pallas_call(kernel, out_shape=[SPACES[p](shape, dtype) for p, shape, d...  23.1 us
    all_to_all x1, starting transfers between devices, exchange(): return lax.all_to_all(x, 'rows', 0, 0, axis_index_groups=[order])  6.04 us
  transfers between devices with their start and end apart: 2, of which 2 were waited for; matrix products, arithmetic and copies ran while one was open for 0% of the time, Pallas kernels for 7%

profile of v11, /device:TPU:0, one launch (start us, length us, event | category | flops | bytes accessed | tf_op | source)
XLA Modules:
  0.0 92.3 jit_solution(13035732786371952774)
XLA Ops:
  0.7 2.5 %pick.1 = (f32[48,256]{1,0:T(8,128)S(1)}, s32[1,1024]{1,0:T(1,128)S(1)}, s32[1]{0:T(128)S(4)}, bf16[2048,512]{1,0:T(8,128)(2,1)S(1)}) custom-call(s32[1]{0:T(128)S(6)} %copy.9.live_ref, s32[2,512]{1,0:T(2,128)} %ids_ref.1, f32[2048,256]{1,0:T(8,128)} %samples_ref.1), custom_call_target="tpu_custom_call" | custom-call | flops 100663296 | bytes 2101252 | tf_op jit(solution)/shard_map/pick/pallas_call | solution.py:260
  3.2 0.1 broadcast_in_dim.47
  3.3 0.0 copy-start
  3.3 27.0 %all_to_all.30 = f32[16,48,256]{2,1,0:T(8,128)S(1)} all-to-all(f32[16,48,256]{2,1,0:T(8,128)S(1)} %broadcast_in_dim.47), channel_id=1, replica_groups={{14,12,2,28,0,10,4,26,8,30,16,20,24,22,18,6},{15,13,3,29,1,11,5,27,9,31..., dimensions={0} | all-to-all | bytes 1572864 | tf_op jit(solution)/shard_map/all_to_all | solution.py:27
  30.3 0.0 collective-permute-start
  30.4 1.0 %own.1.found_ref = bf16[2,512,512]{2,1,0:T(8,128)(2,1)S(1)} custom-call(s32[1,1024]{1,0:T(1,128)S(1)} %get-tuple-element.38.slots_ref, f32[768,256]{1,0:T(8,128)S(1)} %bitcast.12), custom_call_target="tpu_custom_call" | custom-call | flops 805306368 | bytes 790528 | tf_op jit(solution)/shard_map/own/pallas_call | solution.py:260
  31.4 1.3 %collective-permute-done.refs_0_ = f32[768,256]{1,0:T(8,128)S(1)} collective-permute-done((f32[768,256]{1,0:T(8,128)S(1)}, f32[768,256]{1,0:T(8,128)S(1)}, u32[]{:S(2)}, u32[]{:S(2)}) %collective-permute-start) | collective-permute-done | bytes 786464 | tf_op jit(solution)/shard_map/ppermute | solution.py:319
  32.6 0.0 copy-done
  32.6 5.1 %first.1 = (bf16[2048,512]{1,0:T(8,128)(2,1)}, bf16[2048,512]{1,0:T(8,128)(2,1)}, f32[128,512]{1,0:T(8,128)}, s32[1,1024]{1,0:T(1,128)}, bf16[1,512,512]{2,1,0:T(8,128)(2,1)}, /*index=5*/f32[768,256]{1,0:T(8,128)}) custom-call(s32[1]{0:T(128)S(6)} %copy.9.live_ref, f32[2048,128]{1,0:T(8,128)S(1)} %copy-done, ...), custom_call_target="tpu_custom_call" | custom-call | flops 2415919104 | bytes 4984836 | tf_op jit(solution)/shard_map/first/pallas_call | solution.py:260
  37.7 6.0 %all-to-all-start.2 = ((f32[16,8,512]{2,1,0:T(8,128)}), f32[16,8,512]{2,1,0:T(8,128)S(1)}, u32[]{:S(2)}, u32[]{:S(2)}) async-start(f32[16,8,512]{2,1,0:T(8,128)} %bitcast.3), calls=%async_computation.2 | async-start | bytes 524288 | tf_op jit(solution)/shard_map/all_to_all | solution.py:27
  43.8 5.7 %beside.1 = (bf16[2048,512]{1,0:T(8,128)(2,1)}, bf16[2048,512]{1,0:T(8,128)(2,1)}, f32[512,512]{1,0:T(8,128)S(1)}) custom-call(s32[1]{0:T(128)S(6)} %copy.9.live_ref, bf16[2048,512]{1,0:T(8,128)(2,1)S(1)} %get-tuple-element.37.samples_ref, s32[1,1024]{1,0:T(1,128)} %get-tuple-element.44.slots_ref, bf16[1,512,512]{2,1,0:T(8,128)(2,1)} %get-tuple-element.45.found_ref, ...), custom_call_target="tpu_custom_call" | custom-call | flops 1610612736 | bytes 5509124 | tf_op jit(solution)/shard_map/beside/pallas_call | solution.py:260
  49.5 0.9 all-to-all-done.2
  50.4 10.9 %all_to_all.31 = f32[16,8,512]{2,1,0:T(8,128)S(1)} all-to-all(f32[16,8,512]{2,1,0:T(8,128)S(1)} %broadcast_in_dim.48), channel_id=1, replica_groups={{22,8,14,26,30,16,10,28,0,18,2,6,12,4,20,24},{23,9,15,27,31,17,11,29,1,..., dimensions={0} | all-to-all | bytes 524288 | tf_op jit(solution)/shard_map/all_to_all | solution.py:27
  61.3 4.9 %middle.1 = (f32[2048,128]{1,0:T(8,128)S(1)}, f32[128,512]{1,0:T(8,128)S(1)}, f32[512,512]{1,0:T(8,128)S(1)}) custom-call(s32[1]{0:T(128)S(6)} %copy.9.live_ref, f32[128,512]{1,0:T(8,128)S(1)} %bitcast.9, f32[512,512]{1,0:T(8,128)S(1)} %get-tuple-element.51.inverse_ref, f32[2048,128]{1,0:T(8,128)} %residual_ref.3, ...), custom_call_target="tpu_custom_call" | custom-call | flops 1610612736 | bytes 12845060 | tf_op jit(solution)/shard_map/middle/pallas_call | solution.py:260
  66.2 11.1 %all_to_all.32 = f32[16,8,512]{2,1,0:T(8,128)S(1)} all-to-all(f32[16,8,512]{2,1,0:T(8,128)S(1)} %bitcast.13), channel_id=1, replica_groups={{22,8,14,26,30,16,10,28,0,18,2,6,12,4,20,24},{23,9,15,27,31,17,11,29,1,..., dimensions={0} | all-to-all | bytes 524288 | tf_op jit(solution)/shard_map/all_to_all | solution.py:27
  77.3 11.2 %all_to_all.33 = f32[16,8,512]{2,1,0:T(8,128)S(1)} all-to-all(f32[16,8,512]{2,1,0:T(8,128)S(1)} %broadcast_in_dim.49), channel_id=1, replica_groups={{22,8,14,26,30,16,10,28,0,18,2,6,12,4,20,24},{23,9,15,27,31,17,11,29,1,..., dimensions={0} | all-to-all | bytes 524288 | tf_op jit(solution)/shard_map/all_to_all | solution.py:27
  88.4 3.9 %last.1 = f32[2048,128]{1,0:T(8,128)} custom-call(s32[1]{0:T(128)S(6)} %copy.9.live_ref, f32[128,512]{1,0:T(8,128)S(1)} %bitcast.10, f32[512,512]{1,0:T(8,128)S(1)} %get-tuple-element.57.inverse_ref, f32[2048,128]{1,0:T(8,128)S(1)} %get-tuple-element.58.residual_ref, bf16[2048,512]{1,0:T(8,128)(2,1)} %get-tuple-element.54.next_high.high_ref, ...), custom_call_target="tpu_custom_call" | custom-call | flops 805306368 | bytes 6553604 | tf_op jit(solution)/shard_map/last/pallas_call | solution.py:260
  (5 shorter events, 0.1 us)
Async XLA Ops:
  3.3 29.3 %copy-start = (f32[2048,128]{1,0:T(8,128)S(1)}, f32[2048,128]{1,0:T(8,128)}, u32[]{:S(2)}) copy-start(f32[2048,128]{1,0:T(8,128)} %residual_ref.3) | copy-start | bytes 3145732
  30.3 2.3 %collective-permute-start = (f32[768,256]{1,0:T(8,128)S(1)}, f32[768,256]{1,0:T(8,128)S(1)}, u32[]{:S(2)}, u32[]{:S(2)}) collective-permute-start(f32[768,256]{1,0:T(8,128)S(1)} %bitcast.11), channel_id=1, source_target_pairs={{1,0},{0,1},{3,2},{2,3},{5,4},{4,5},{7,6},{6,7},{9,8},{8,9},{11,10... | collective-permute-start | bytes 2359304 | tf_op jit(solution)/shard_map/ppermute | solution.py:319
  37.7 12.7 %all-to-all-start.2 = ((f32[16,8,512]{2,1,0:T(8,128)}), f32[16,8,512]{2,1,0:T(8,128)S(1)}, u32[]{:S(2)}, u32[]{:S(2)}) async-start(f32[16,8,512]{2,1,0:T(8,128)} %bitcast.3), calls=%async_computation.2 | async-start | bytes 524288 | tf_op jit(solution)/shard_map/all_to_all | solution.py:27

commit v12 on v11

--- a/solution.py
+++ b/solution.py
@@ -64,7 +64,7 @@
         copy.wait()
 
 
-def pick_kernel(order, cores, cap, live_ref, ids_ref, samples_ref, rows_ref, slots_ref, most_ref, parts_ref, samples_v, chosen_v, sems):
+def pick_kernel(order, cores, caps, live_ref, ids_ref, samples_ref, rows_ref, slots_ref, most_ref, samples_v, chosen_v, sems):
     (rows_here, feat), groups = samples_ref.shape, len(order)
     parts = pieces(rows_here, HALF_STEP)
     copies = [copy_of(samples_ref.at[at], samples_v.at[at], sems.at[i]) for i, at in enumerate(parts)]
@@ -85,28 +85,40 @@
             step *= 2
         most = jnp.max(seen)
         rank = jnp.sum(jnp.where(mine, seen, 0), axis=0, keepdims=True) - 1
-        half = lax.div(rank, jnp.int32(cap))
+        cap = jnp.int32(caps[-1])
+        for less in caps[-2::-1]:
+            cap = jnp.where(most <= less * cores, less, cap)
+        half = lax.div(rank, cap)
         turn = jnp.zeros_like(owner)
         for index, device in enumerate(order):
             turn = jnp.where(owner == device, index, turn)
-        packed = (half * groups + turn) * cap + (rank - half * cap)
+        packed = half * (groups * caps[-1]) + turn * cap + (rank - half * cap)
         place = lax.broadcasted_iota(jnp.int32, (1, count), 1)
-        slots_ref[...] = jnp.where(most > cap * cores, place, packed)
+        slots_ref[...] = jnp.where(most > caps[-1] * cores, place, packed)
         most_ref[0] = most
 
-        wanted = lax.broadcasted_iota(jnp.int32, (cap, count), 0) + core * cap
+        wanted = lax.broadcasted_iota(jnp.int32, (caps[-1], count), 0) + core * cap
         sent = jnp.sum(jnp.where((wanted == rank) & (owner == me), local, 0), axis=1, keepdims=True)
-        chosen_v[...] = jnp.where(lax.broadcasted_iota(jnp.int32, (cap, rows_here), 1) == sent, 1.0, 0.0).astype(BF16)
+        chosen_v[...] = jnp.where(lax.broadcasted_iota(jnp.int32, (caps[-1], rows_here), 1) == sent, 1.0, 0.0).astype(BF16)
 
     for copy, at in zip(copies, parts):
         copy.wait()
 
         @stage(live_ref)
         def _():
-            parts_ref[at, :] = jnp.concatenate(split(samples_v[at, :]), axis=1)
-            both = dot(chosen_v[:, at], parts_ref[at, :], ((1,), (0,)))
+            both = dot(chosen_v[:, at], jnp.concatenate(split(samples_v[at, :]), axis=1), ((1,), (0,)))
             found = both[:, :feat] + both[:, feat:]
             rows_ref[...] = found if at.start == 0 else rows_ref[...] + found
+
+
+def owned_kernel(local_ref, samples_ref, out_ref, samples_v, sems):
+    copy_of(samples_ref, samples_v, sems.at[0]).wait()
+    rows, feat = samples_v.shape
+    parts = jnp.concatenate(split(samples_v[...]), axis=1)
+    for at in pieces(local_ref.shape[0], 128):
+        chosen = lax.broadcasted_iota(jnp.int32, (at.size, rows), 1) == local_ref[at, :]
+        both = dot(jnp.where(chosen, 1.0, 0.0).astype(BF16), parts, ((1,), (0,)))
+        out_ref[at, :] = both[:, :feat] + both[:, feat:]
 
 
 def found_in(ref, slots, shift, cores):
@@ -117,19 +129,25 @@
     return dot(jnp.concatenate(split(ref[...]), axis=1), taken, ((0,), (0,)))
 
 
-def own_kernel(cores, slots_ref, held_ref, found_ref):
+def own_kernel(cores, live_ref, slots_ref, held_ref, samples_ref, found_ref, samples_v, sems):
     blocks, _, size = found_ref.shape
-    for b in range(blocks):
-        found_ref[b] = found_in(held_ref, slots_ref[:, b * size : (b + 1) * size], 0, cores).astype(BF16)
+    samples_in = copy_of(samples_ref, samples_v, sems.at[0])
+
+    @stage(live_ref)
+    def _():
+        for b in range(blocks):
+            found_ref[b] = found_in(held_ref, slots_ref[:, b * size : (b + 1) * size], 0, cores).astype(BF16)
+
+    samples_in.wait()
 
 
 def make_columns(live_ref, samples_ref, points, columns_v, high_ref, low_ref, sems):
-    rows, feat = samples_ref.shape[0], samples_ref.shape[1] // 2
+    rows, feat = samples_ref.shape
     scale = 0.5 / feat**0.5
     copies = []
     for index, half in enumerate(pieces(rows, HALF_STEP)):
         for at in [pl.ds(half.start + part.start, part.size) for part in pieces(half.size)]:
-            base = dot3((samples_ref[at, :feat], samples_ref[at, feat:]), points, ((1,), (0,))) * scale + 1.0
+            base = dot3(split(samples_ref[at, :]), points, ((1,), (0,))) * scale + 1.0
             slot = lax.broadcasted_iota(jnp.int32, (at.size, 1), 0) + at.start
             columns_v[0, at, :], columns_v[1, at, :] = split(jnp.where(slot < live_ref[0], base * base * base, 0.0))
         for kind, ref in enumerate((high_ref, low_ref)):
@@ -168,14 +186,15 @@
 
 def beside_kernel(block, cores, live_ref, samples_ref, slots_ref, found_ref, inverse_ref, *refs):
     held, refs = refs[: cores - 1], refs[cores - 1 :]
-    high_ref, low_ref, inverse_v, points_v, slots_v, found_v, *held_v, columns_v, sems = refs
+    high_ref, low_ref, inverse_v, samples_v, points_v, slots_v, found_v, *held_v, columns_v, sems = refs
     size = found_v.shape[1]
     in_flight = [copy_of(found_ref.at[block], found_v, sems.at[3, 0]), copy_of(slots_ref, slots_v, sems.at[3, 1])]
     in_flight += [copy_of(ref, v, sems.at[4, i]) for i, (ref, v) in enumerate(zip(held, held_v))]
+    samples_in = copy_of(samples_ref, samples_v, sems.at[2, 1])
     inverse_in = copy_of(inverse_ref.at[block], inverse_v, sems.at[2, 0])
-    wait_all(*in_flight)
+    wait_all(*in_flight, samples_in)
     points_v[0], points_v[1] = points_of(found_v[...], held_v, slots_v[:, (block + 1) * size : (block + 2) * size])
-    copies = make_columns(live_ref, samples_ref, (points_v[0], points_v[1]), columns_v, high_ref, low_ref, sems)
+    copies = make_columns(live_ref, samples_v, (points_v[0], points_v[1]), columns_v, high_ref, low_ref, sems)
     wait_all(inverse_in, *copies)
 
 
@@ -288,14 +307,15 @@
     rows_here, feat = samples.shape
     blocks, size = point_ids.shape
     mean = blocks * size / groups
-    cap = round_up(max(1, round((mean + 4 * mean**0.5) / cores)), 8)
+    caps = sorted({round_up(max(1, round((mean + spread * mean**0.5) / cores)), 8) for spread in (2, 4)})
+    cap = caps[-1]
 
     order = order_of(groups, POINTS_SEED)
-    rows, slots, most, samples_split = local(
-        functools.partial(pick_kernel, order, cores, cap),
+    rows, slots, most = local(
+        functools.partial(pick_kernel, order, cores, caps),
         (counts, point_ids, samples),
         "SVH",
-        [("V", (cap, feat), F32), ("V", (1, blocks * size), jnp.int32), ("S", (1,), jnp.int32), ("V", (rows_here, 2 * feat), BF16)],
+        [("V", (cap, feat), F32), ("V", (1, blocks * size), jnp.int32), ("S", (1,), jnp.int32)],
         [
             pltpu.VMEM(samples.shape, F32),
             pltpu.VMEM((cap, rows_here), BF16),
@@ -308,21 +328,32 @@
     def general(rows):
         ids = jnp.pad(point_ids.reshape(-1), (0, cores * groups * cap - blocks * size), constant_values=-1)
         ids = lax.dynamic_slice_in_dim(ids, lax.axis_index("tgt") * groups * cap, groups * cap)
-        local = ids - lax.axis_index("rows") * rows_here
-        owned = (local >= 0) & (local < rows_here)
-        taken = jnp.take(samples, jnp.clip(local, 0, rows_here - 1), axis=0)
-        taken = jnp.where(owned[:, None], taken, 0.0)
+        here = ids - lax.axis_index("rows") * rows_here
+        taken = local(
+            owned_kernel,
+            (here[:, None], samples),
+            "VH",
+            [("V", (groups * cap, feat), F32)],
+            [pltpu.VMEM(samples.shape, F32), pltpu.SemaphoreType.DMA((1,))],
+            4 * groups * cap * rows_here * feat,
+            "owned",
+        )
         return jnp.sum(exchange(taken.reshape(groups, cap, feat), order), axis=0)
 
-    rows = lax.cond(most[0] > cap * cores, general, lambda rows: rows, rows)
-    got = exchange(jnp.broadcast_to(rows[None], (groups, cap, feat)), order).reshape(groups * cap, feat)
+    def gather(rows, count=cap):
+        sent = jnp.broadcast_to(rows[None, :count], (groups, count, feat))
+        got = exchange(sent, order).reshape(groups * count, feat)
+        return got if count == cap else jnp.pad(got, ((0, groups * (cap - count)), (0, 0)))
+
+    choices = [functools.partial(gather, count=count) for count in caps] + [lambda rows: gather(general(rows))]
+    got = lax.switch(sum((most[0] > count * cores).astype(jnp.int32) for count in caps), choices, rows)
     held = [lax.ppermute(got, "tgt", [((c + shift) % cores, c) for c in range(cores)]) for shift in range(1, cores)]
-    found = local(
+    found, samples_v = local(
         functools.partial(own_kernel, cores),
-        (slots, got),
-        "VV",
-        [("V", (blocks, 2 * feat, size), BF16)],
-        [],
+        (counts, slots, got, samples),
+        "SVVH",
+        [("V", (blocks, 2 * feat, size), BF16), ("V", samples.shape, F32)],
+        [pltpu.SemaphoreType.DMA((1,))],
         4 * groups * cap * feat * blocks * size,
         "own",
     )
@@ -342,7 +373,7 @@
     points_v = pltpu.VMEM((2, feat, size), BF16)
     high, low, totals, slots_out, found, *held = local(
         functools.partial(first_kernel, cores),
-        (counts, residual, samples_split, slots, found, *held),
+        (counts, residual, samples_v, slots, found, *held),
         "SVVVV" + "V" * len(held),
         [
             *columns_out,
@@ -361,10 +392,11 @@
         def beside(b=b):
             return local(
                 functools.partial(beside_kernel, b, cores),
-                (counts, samples_split, slots_out, found, block_inverse, *held),
-                "SVHHH" + "H" * len(held),
+                (counts, samples, slots_out, found, block_inverse, *held),
+                "SHHHH" + "H" * len(held),
                 [*columns_out, inverse_out],
                 [
+                    pltpu.VMEM(samples.shape, F32),
                     points_v,
                     pltpu.VMEM(slots.shape, jnp.int32),
                     pltpu.VMEM((2 * feat, size), BF16),

time: 92.8 us -> 92.6 us (level); the launches traced: 92.3 us -> 90.9 us
  blocking collectives: 60.1 us -> 58.1 us
  Pallas kernels: 23.1 us -> 25 us
  waiting for transfers between devices: 2.18 us -> 0.59 us
    all_to_all x4, blocking collectives: 60.1 us -> 58.1 us  [exchange(): return lax.all_to_all(x, 'rows', 0, 0, axis_index_groups=[order])]
    pallas_call x6, Pallas kernels: 23.1 us -> 25 us  [local(): pl.pallas_call(kernel, out_shape=[SPACES[p](shape, dtype) for p, shape, d...]
  transfers between devices with their start and end apart: 2 -> 2, of which waited for: 2 -> 1; matrix products, arithmetic and copies ran while one was open for 0% -> 0% of each run, Pallas kernels for 7% -> 9%
where the time goes in v12:
time: 92.6 us; the launch traced here: 90.9 us
  blocking collectives  58.1 us (63%)
  Pallas kernels  25 us (27%)
  starting transfers between devices  6.1 us (7%)
  between operations  0.93 us (1%)
    all_to_all x4, blocking collectives, exchange(): return lax.all_to_all(x, 'rows', 0, 0, axis_index_groups=[order])  58.1 us
    pallas_call x6, Pallas kernels, local(): pl.pallas_call(kernel, out_shape=[SPACES[p](shape, dtype) for p, shape, d...  25 us
    all_to_all x1, starting transfers between devices, exchange(): return lax.all_to_all(x, 'rows', 0, 0, axis_index_groups=[order])  6.03 us
  transfers between devices with their start and end apart: 2, of which 1 were waited for; matrix products, arithmetic and copies ran while one was open for 0% of the time, Pallas kernels for 9%

profile of v12, /device:TPU:0, one launch (start us, length us, event | category | flops | bytes accessed | tf_op | source)
XLA Modules:
  0.0 90.9 jit_solution(6288129964185247129)
XLA Ops:
  0.7 2.6 %pick.1 = (f32[48,256]{1,0:T(8,128)S(1)}, s32[1,1024]{1,0:T(1,128)S(1)}, s32[1]{0:T(128)S(4)}) custom-call(s32[1]{0:T(128)S(6)} %copy.11.live_ref, s32[2,512]{1,0:T(2,128)} %ids_ref.1, f32[2048,256]{1,0:T(8,128)} %samples_ref.5), custom_call_target="tpu_custom_call" | custom-call | flops 100663296 | bytes 2101252 | tf_op jit(solution)/shard_map/pick/pallas_call | solution.py:279
  3.2 24.4 %conditional.1 = (f32[768,256]{1,0:T(8,128)S(1)}) conditional(s32[]{:T(128)} %bitcast.4, f32[48,256]{1,0:T(8,128)S(1)} %get-tuple-element.42, f32[48,256]{1,0:T(8,128)S(1)} %get-tuple-element.42, (s32[2,512]{1,0:T(2,128)}, f32[2048,256]{1,0:T(8,128)}) %tuple.16), branch_computations={%region_0.1_spmd, %region_1.2_spmd, %region_2.4_spmd} | conditional | flops 1610797824 | bytes 6938754 | solution.py:349
  3.3 24.3 %all_to_all.36 = f32[16,40,256]{2,1,0:T(8,128)S(1)} all-to-all(f32[16,40,256]{2,1,0:T(8,128)S(1)} %broadcast_in_dim.8), channel_id=1, replica_groups={{14,12,2,28,0,10,4,26,8,30,16,20,24,22,18,6},{15,13,3,29,1,11,5,27,9,31..., dimensions={0} | all-to-all | bytes 1310720 | tf_op jit(solution)/shard_map/cond/branch_0_fun/all_to_all | solution.py:27
  27.6 0.1 pad.6
  27.6 0.0 copy-start
  27.7 0.1 collective-permute-start
  27.7 1.7 %own.1 = (bf16[2,512,512]{2,1,0:T(8,128)(2,1)S(1)}, f32[2048,256]{1,0:T(8,128)S(1)}) custom-call(s32[1]{0:T(128)S(6)} %copy.11.live_ref, s32[1,1024]{1,0:T(1,128)S(1)} %get-tuple-element.40.slots_ref, f32[768,256]{1,0:T(8,128)S(1)} %get-tuple-element.63.held_ref, f32[2048,256]{1,0:T(8,128)} %samples_ref.5), custom_call_target="tpu_custom_call" | custom-call | flops 805306368 | bytes 2887684 | tf_op jit(solution)/shard_map/own/pallas_call | solution.py:279
  29.4 0.6 collective-permute-done.refs_0_
  30.0 0.0 copy-done
  30.0 5.4 %first.1 = (bf16[2048,512]{1,0:T(8,128)(2,1)}, bf16[2048,512]{1,0:T(8,128)(2,1)}, f32[128,512]{1,0:T(8,128)}, s32[1,1024]{1,0:T(1,128)}, bf16[1,512,512]{2,1,0:T(8,128)(2,1)}, /*index=5*/f32[768,256]{1,0:T(8,128)}) custom-call(s32[1]{0:T(128)S(6)} %copy.11.live_ref, f32[2048,128]{1,0:T(8,128)S(1)} %copy-done, f32[2048,256]{1,0:T(8,128)S(1)} %get-tuple-element.43.samples_ref, ...), custom_call_target="tpu_custom_call" | custom-call | flops 2415919104 | bytes 4984836 | tf_op jit(solution)/shard_map/first/pallas_call | solution.py:279
  35.4 6.0 %all-to-all-start.4 = ((f32[16,8,512]{2,1,0:T(8,128)}), f32[16,8,512]{2,1,0:T(8,128)S(1)}, u32[]{:S(2)}, u32[]{:S(2)}) async-start(f32[16,8,512]{2,1,0:T(8,128)} %bitcast.5), calls=%async_computation.4 | async-start | bytes 524288 | tf_op jit(solution)/shard_map/all_to_all | solution.py:27
  41.4 6.6 %beside.1 = (bf16[2048,512]{1,0:T(8,128)(2,1)}, bf16[2048,512]{1,0:T(8,128)(2,1)}, f32[512,512]{1,0:T(8,128)S(1)}) custom-call(s32[1]{0:T(128)S(6)} %copy.11.live_ref, f32[2048,256]{1,0:T(8,128)} %samples_ref.5, s32[1,1024]{1,0:T(1,128)} %get-tuple-element.48.slots_ref, bf16[1,512,512]{2,1,0:T(8,128)(2,1)} %get-tuple-element.49.found_ref, ...), custom_call_target="tpu_custom_call" | custom-call | flops 1610612736 | bytes 5509124 | tf_op jit(solution)/shard_map/beside/pallas_call | solution.py:279
  48.1 0.0 all-to-all-done.4
  48.1 11.9 %all_to_all.40 = f32[16,8,512]{2,1,0:T(8,128)S(1)} all-to-all(f32[16,8,512]{2,1,0:T(8,128)S(1)} %broadcast_in_dim.20), channel_id=1, replica_groups={{22,8,14,26,30,16,10,28,0,18,2,6,12,4,20,24},{23,9,15,27,31,17,11,29,1,..., dimensions={0} | all-to-all | bytes 524288 | tf_op jit(solution)/shard_map/all_to_all | solution.py:27
  60.0 4.9 %middle.1 = (f32[2048,128]{1,0:T(8,128)S(1)}, f32[128,512]{1,0:T(8,128)S(1)}, f32[512,512]{1,0:T(8,128)S(1)}) custom-call(s32[1]{0:T(128)S(6)} %copy.11.live_ref, f32[128,512]{1,0:T(8,128)S(1)} %bitcast.11, f32[512,512]{1,0:T(8,128)S(1)} %get-tuple-element.55.inverse_ref, f32[2048,128]{1,0:T(8,128)} %residual_ref.3, ...), custom_call_target="tpu_custom_call" | custom-call | flops 1610612736 | bytes 12845060 | tf_op jit(solution)/shard_map/middle/pallas_call | solution.py:279
  64.9 10.7 %all_to_all.41 = f32[16,8,512]{2,1,0:T(8,128)S(1)} all-to-all(f32[16,8,512]{2,1,0:T(8,128)S(1)} %bitcast.16), channel_id=1, replica_groups={{22,8,14,26,30,16,10,28,0,18,2,6,12,4,20,24},{23,9,15,27,31,17,11,29,1,..., dimensions={0} | all-to-all | bytes 524288 | tf_op jit(solution)/shard_map/all_to_all | solution.py:27
  75.7 11.2 %all_to_all.42 = f32[16,8,512]{2,1,0:T(8,128)S(1)} all-to-all(f32[16,8,512]{2,1,0:T(8,128)S(1)} %broadcast_in_dim.26), channel_id=1, replica_groups={{22,8,14,26,30,16,10,28,0,18,2,6,12,4,20,24},{23,9,15,27,31,17,11,29,1,..., dimensions={0} | all-to-all | bytes 524288 | tf_op jit(solution)/shard_map/all_to_all | solution.py:27
  86.9 3.9 %last.1 = f32[2048,128]{1,0:T(8,128)} custom-call(s32[1]{0:T(128)S(6)} %copy.11.live_ref, f32[128,512]{1,0:T(8,128)S(1)} %bitcast.12, f32[512,512]{1,0:T(8,128)S(1)} %get-tuple-element.61.inverse_ref, f32[2048,128]{1,0:T(8,128)S(1)} %get-tuple-element.62.residual_ref, bf16[2048,512]{1,0:T(8,128)(2,1)} %get-tuple-element.58.next_high.high_ref, ...), custom_call_target="tpu_custom_call" | custom-call | flops 805306368 | bytes 6553604 | tf_op jit(solution)/shard_map/last/pallas_call | solution.py:279
  (6 shorter events, 0.1 us)
Async XLA Ops:
  27.6 2.4 %copy-start = (f32[2048,128]{1,0:T(8,128)S(1)}, f32[2048,128]{1,0:T(8,128)}, u32[]{:S(2)}) copy-start(f32[2048,128]{1,0:T(8,128)} %residual_ref.3) | copy-start | bytes 3145732
  27.7 2.4 %collective-permute-start = (f32[768,256]{1,0:T(8,128)S(1)}, f32[768,256]{1,0:T(8,128)S(1)}, u32[]{:S(2)}, u32[]{:S(2)}) collective-permute-start(f32[768,256]{1,0:T(8,128)S(1)} %get-tuple-element.63.held_ref), channel_id=1, source_target_pairs={{1,0},{0,1},{3,2},{2,3},{5,4},{4,5},{7,6},{6,7},{9,8},{8,9},{11,10... | collective-permute-start | bytes 2359304 | tf_op jit(solution)/shard_map/ppermute | solution.py:350
  35.4 12.7 %all-to-all-start.4 = ((f32[16,8,512]{2,1,0:T(8,128)}), f32[16,8,512]{2,1,0:T(8,128)S(1)}, u32[]{:S(2)}, u32[]{:S(2)}) async-start(f32[16,8,512]{2,1,0:T(8,128)} %bitcast.5), calls=%async_computation.4 | async-start | bytes 524288 | tf_op jit(solution)/shard_map/all_to_all | solution.py:27

commit v13 on v12

--- a/solution.py
+++ b/solution.py
@@ -129,7 +129,7 @@
     return dot(jnp.concatenate(split(ref[...]), axis=1), taken, ((0,), (0,)))
 
 
-def own_kernel(cores, live_ref, slots_ref, held_ref, samples_ref, found_ref, samples_v, sems):
+def own_kernel(cores, live_ref, slots_ref, held_ref, samples_ref, found_ref, parts_ref, samples_v, sems):
     blocks, _, size = found_ref.shape
     samples_in = copy_of(samples_ref, samples_v, sems.at[0])
 
@@ -139,15 +139,16 @@
             found_ref[b] = found_in(held_ref, slots_ref[:, b * size : (b + 1) * size], 0, cores).astype(BF16)
 
     samples_in.wait()
+    parts_ref[...] = jnp.concatenate(split(samples_v[...]), axis=1)
 
 
 def make_columns(live_ref, samples_ref, points, columns_v, high_ref, low_ref, sems):
-    rows, feat = samples_ref.shape
+    rows, feat = samples_ref.shape[0], samples_ref.shape[1] // 2
     scale = 0.5 / feat**0.5
     copies = []
     for index, half in enumerate(pieces(rows, HALF_STEP)):
         for at in [pl.ds(half.start + part.start, part.size) for part in pieces(half.size)]:
-            base = dot3(split(samples_ref[at, :]), points, ((1,), (0,))) * scale + 1.0
+            base = dot3((samples_ref[at, :feat], samples_ref[at, feat:]), points, ((1,), (0,))) * scale + 1.0
             slot = lax.broadcasted_iota(jnp.int32, (at.size, 1), 0) + at.start
             columns_v[0, at, :], columns_v[1, at, :] = split(jnp.where(slot < live_ref[0], base * base * base, 0.0))
         for kind, ref in enumerate((high_ref, low_ref)):
@@ -190,9 +191,9 @@
     size = found_v.shape[1]
     in_flight = [copy_of(found_ref.at[block], found_v, sems.at[3, 0]), copy_of(slots_ref, slots_v, sems.at[3, 1])]
     in_flight += [copy_of(ref, v, sems.at[4, i]) for i, (ref, v) in enumerate(zip(held, held_v))]
-    samples_in = copy_of(samples_ref, samples_v, sems.at[2, 1])
+    in_flight.append(copy_of(samples_ref, samples_v, sems.at[2, 1]))
     inverse_in = copy_of(inverse_ref.at[block], inverse_v, sems.at[2, 0])
-    wait_all(*in_flight, samples_in)
+    wait_all(*in_flight)
     points_v[0], points_v[1] = points_of(found_v[...], held_v, slots_v[:, (block + 1) * size : (block + 2) * size])
     copies = make_columns(live_ref, samples_v, (points_v[0], points_v[1]), columns_v, high_ref, low_ref, sems)
     wait_all(inverse_in, *copies)
@@ -348,12 +349,12 @@
     choices = [functools.partial(gather, count=count) for count in caps] + [lambda rows: gather(general(rows))]
     got = lax.switch(sum((most[0] > count * cores).astype(jnp.int32) for count in caps), choices, rows)
     held = [lax.ppermute(got, "tgt", [((c + shift) % cores, c) for c in range(cores)]) for shift in range(1, cores)]
-    found, samples_v = local(
+    found, samples_split = local(
         functools.partial(own_kernel, cores),
         (counts, slots, got, samples),
         "SVVH",
-        [("V", (blocks, 2 * feat, size), BF16), ("V", samples.shape, F32)],
-        [pltpu.SemaphoreType.DMA((1,))],
+        [("V", (blocks, 2 * feat, size), BF16), ("V", (rows_here, 2 * feat), BF16)],
+        [pltpu.VMEM(samples.shape, F32), pltpu.SemaphoreType.DMA((1,))],
         4 * groups * cap * feat * blocks * size,
         "own",
     )
@@ -373,7 +374,7 @@
     points_v = pltpu.VMEM((2, feat, size), BF16)
     high, low, totals, slots_out, found, *held = local(
         functools.partial(first_kernel, cores),
-        (counts, residual, samples_v, slots, found, *held),
+        (counts, residual, samples_split, slots, found, *held),
         "SVVVV" + "V" * len(held),
         [
             *columns_out,
@@ -392,11 +393,11 @@
         def beside(b=b):
             return local(
                 functools.partial(beside_kernel, b, cores),
-                (counts, samples, slots_out, found, block_inverse, *held),
+                (counts, samples_split, slots_out, found, block_inverse, *held),
                 "SHHHH" + "H" * len(held),
                 [*columns_out, inverse_out],
                 [
-                    pltpu.VMEM(samples.shape, F32),
+                    pltpu.VMEM((rows_here, 2 * feat), BF16),
                     points_v,
                     pltpu.VMEM(slots.shape, jnp.int32),
                     pltpu.VMEM((2 * feat, size), BF16),

time: 92.6 us -> 90.9 us (0.982); the launches traced: 90.9 us -> 90.5 us
  transfers between devices with their start and end apart: 2 -> 2, of which waited for: 1 -> 2; matrix products, arithmetic and copies ran while one was open for 0% -> 0% of each run, Pallas kernels for 9% -> 9%
where the time goes in v13:
time: 90.9 us; the launch traced here: 90.5 us
  blocking collectives  57.9 us (64%)
  Pallas kernels  24.8 us (27%)
  starting transfers between devices  6.1 us (7%)
  between operations  0.93 us (1%)
    all_to_all x4, blocking collectives, exchange(): return lax.all_to_all(x, 'rows', 0, 0, axis_index_groups=[order])  57.9 us
    pallas_call x6, Pallas kernels, local(): pl.pallas_call(kernel, out_shape=[SPACES[p](shape, dtype) for p, shape, d...  24.8 us
    all_to_all x1, starting transfers between devices, exchange(): return lax.all_to_all(x, 'rows', 0, 0, axis_index_groups=[order])  6.03 us
  transfers between devices with their start and end apart: 2, of which 2 were waited for; matrix products, arithmetic and copies ran while one was open for 0% of the time, Pallas kernels for 9%

profile of v13, /device:TPU:0, one launch (start us, length us, event | category | flops | bytes accessed | tf_op | source)
XLA Modules:
  0.0 90.5 jit_solution(5042198230270115035)
XLA Ops:
  0.7 2.6 %pick.1 = (f32[48,256]{1,0:T(8,128)S(1)}, s32[1,1024]{1,0:T(1,128)S(1)}, s32[1]{0:T(128)S(4)}) custom-call(s32[1]{0:T(128)S(6)} %copy.11.live_ref, s32[2,512]{1,0:T(2,128)} %ids_ref.1, f32[2048,256]{1,0:T(8,128)} %samples_ref.3), custom_call_target="tpu_custom_call" | custom-call | flops 100663296 | bytes 2101252 | tf_op jit(solution)/shard_map/pick/pallas_call | solution.py:280
  3.2 24.4 %conditional.1 = (f32[768,256]{1,0:T(8,128)S(1)}) conditional(s32[]{:T(128)} %bitcast.4, f32[48,256]{1,0:T(8,128)S(1)} %get-tuple-element.42, f32[48,256]{1,0:T(8,128)S(1)} %get-tuple-element.42, (s32[2,512]{1,0:T(2,128)}, f32[2048,256]{1,0:T(8,128)}) %tuple.16), branch_computations={%region_0.1_spmd, %region_1.2_spmd, %region_2.4_spmd} | conditional | flops 1610797824 | bytes 6938754 | solution.py:350
  3.3 24.3 %all_to_all.36 = f32[16,40,256]{2,1,0:T(8,128)S(1)} all-to-all(f32[16,40,256]{2,1,0:T(8,128)S(1)} %broadcast_in_dim.8), channel_id=1, replica_groups={{14,12,2,28,0,10,4,26,8,30,16,20,24,22,18,6},{15,13,3,29,1,11,5,27,9,31..., dimensions={0} | all-to-all | bytes 1310720 | tf_op jit(solution)/shard_map/cond/branch_0_fun/all_to_all | solution.py:27
  27.6 0.1 pad.6
  27.6 0.0 copy-start
  27.7 0.1 collective-permute-start
  27.7 1.9 %own.1 = (bf16[2,512,512]{2,1,0:T(8,128)(2,1)S(1)}, bf16[2048,512]{1,0:T(8,128)(2,1)S(1)}) custom-call(s32[1]{0:T(128)S(6)} %copy.11.live_ref, s32[1,1024]{1,0:T(1,128)S(1)} %get-tuple-element.40.slots_ref, f32[768,256]{1,0:T(8,128)S(1)} %get-tuple-element.63.held_ref, f32[2048,256]{1,0:T(8,128)} %samples_ref.3), custom_call_target="tpu_custom_call" | custom-call | flops 805306368 | bytes 2887684 | tf_op jit(solution)/shard_map/own/pallas_call | solution.py:280
  29.7 0.0 copy-start.1
  29.7 0.3 collective-permute-done.refs_0_
  30.0 0.0 copy-done
  30.0 5.1 %first.1 = (bf16[2048,512]{1,0:T(8,128)(2,1)}, bf16[2048,512]{1,0:T(8,128)(2,1)}, f32[128,512]{1,0:T(8,128)}, s32[1,1024]{1,0:T(1,128)}, bf16[1,512,512]{2,1,0:T(8,128)(2,1)}, /*index=5*/f32[768,256]{1,0:T(8,128)}) custom-call(s32[1]{0:T(128)S(6)} %copy.11.live_ref, f32[2048,128]{1,0:T(8,128)S(1)} %copy-done, ...), custom_call_target="tpu_custom_call" | custom-call | flops 2415919104 | bytes 4984836 | tf_op jit(solution)/shard_map/first/pallas_call | solution.py:280
  35.2 0.0 copy-done.1
  35.2 6.0 %all-to-all-start.4 = ((f32[16,8,512]{2,1,0:T(8,128)}), f32[16,8,512]{2,1,0:T(8,128)S(1)}, u32[]{:S(2)}, u32[]{:S(2)}) async-start(f32[16,8,512]{2,1,0:T(8,128)} %bitcast.5), calls=%async_computation.4 | async-start | bytes 524288 | tf_op jit(solution)/shard_map/all_to_all | solution.py:27
  41.2 6.4 %beside.1 = (bf16[2048,512]{1,0:T(8,128)(2,1)}, bf16[2048,512]{1,0:T(8,128)(2,1)}, f32[512,512]{1,0:T(8,128)S(1)}) custom-call(s32[1]{0:T(128)S(6)} %copy.11.live_ref, bf16[2048,512]{1,0:T(8,128)(2,1)} %copy-done.1, s32[1,1024]{1,0:T(1,128)} %get-tuple-element.48.slots_ref, bf16[1,512,512]{2,1,0:T(8,128)(2,1)} %get-tuple-element.49.found_ref, ...), custom_call_target="tpu_custom_call" | custom-call | flops 1610612736 | bytes 5509124 | tf_op jit(solution)/shard_map/beside/pallas_call | solution.py:280
  47.6 0.2 all-to-all-done.4
  47.9 11.7 %all_to_all.40 = f32[16,8,512]{2,1,0:T(8,128)S(1)} all-to-all(f32[16,8,512]{2,1,0:T(8,128)S(1)} %broadcast_in_dim.20), channel_id=1, replica_groups={{22,8,14,26,30,16,10,28,0,18,2,6,12,4,20,24},{23,9,15,27,31,17,11,29,1,..., dimensions={0} | all-to-all | bytes 524288 | tf_op jit(solution)/shard_map/all_to_all | solution.py:27
  59.6 4.9 %middle.1 = (f32[2048,128]{1,0:T(8,128)S(1)}, f32[128,512]{1,0:T(8,128)S(1)}, f32[512,512]{1,0:T(8,128)S(1)}) custom-call(s32[1]{0:T(128)S(6)} %copy.11.live_ref, f32[128,512]{1,0:T(8,128)S(1)} %bitcast.11, f32[512,512]{1,0:T(8,128)S(1)} %get-tuple-element.55.inverse_ref, f32[2048,128]{1,0:T(8,128)} %residual_ref.3, ...), custom_call_target="tpu_custom_call" | custom-call | flops 1610612736 | bytes 12845060 | tf_op jit(solution)/shard_map/middle/pallas_call | solution.py:280
  64.4 10.8 %all_to_all.41 = f32[16,8,512]{2,1,0:T(8,128)S(1)} all-to-all(f32[16,8,512]{2,1,0:T(8,128)S(1)} %bitcast.16), channel_id=1, replica_groups={{22,8,14,26,30,16,10,28,0,18,2,6,12,4,20,24},{23,9,15,27,31,17,11,29,1,..., dimensions={0} | all-to-all | bytes 524288 | tf_op jit(solution)/shard_map/all_to_all | solution.py:27
  75.3 11.2 %all_to_all.42 = f32[16,8,512]{2,1,0:T(8,128)S(1)} all-to-all(f32[16,8,512]{2,1,0:T(8,128)S(1)} %broadcast_in_dim.26), channel_id=1, replica_groups={{22,8,14,26,30,16,10,28,0,18,2,6,12,4,20,24},{23,9,15,27,31,17,11,29,1,..., dimensions={0} | all-to-all | bytes 524288 | tf_op jit(solution)/shard_map/all_to_all | solution.py:27
  86.4 3.9 %last.1 = f32[2048,128]{1,0:T(8,128)} custom-call(s32[1]{0:T(128)S(6)} %copy.11.live_ref, f32[128,512]{1,0:T(8,128)S(1)} %bitcast.12, f32[512,512]{1,0:T(8,128)S(1)} %get-tuple-element.61.inverse_ref, f32[2048,128]{1,0:T(8,128)S(1)} %get-tuple-element.62.residual_ref, bf16[2048,512]{1,0:T(8,128)(2,1)} %get-tuple-element.58.next_high.high_ref, ...), custom_call_target="tpu_custom_call" | custom-call | flops 805306368 | bytes 6553604 | tf_op jit(solution)/shard_map/last/pallas_call | solution.py:280
  (6 shorter events, 0.1 us)
Async XLA Ops:
  27.6 2.4 %copy-start = (f32[2048,128]{1,0:T(8,128)S(1)}, f32[2048,128]{1,0:T(8,128)}, u32[]{:S(2)}) copy-start(f32[2048,128]{1,0:T(8,128)} %residual_ref.3) | copy-start | bytes 3145732
  27.7 2.4 %collective-permute-start = (f32[768,256]{1,0:T(8,128)S(1)}, f32[768,256]{1,0:T(8,128)S(1)}, u32[]{:S(2)}, u32[]{:S(2)}) collective-permute-start(f32[768,256]{1,0:T(8,128)S(1)} %get-tuple-element.63.held_ref), channel_id=1, source_target_pairs={{1,0},{0,1},{3,2},{2,3},{5,4},{4,5},{7,6},{6,7},{9,8},{8,9},{11,10... | collective-permute-start | bytes 2359304 | tf_op jit(solution)/shard_map/ppermute | solution.py:351
  29.7 5.5 %copy-start.1 = (bf16[2048,512]{1,0:T(8,128)(2,1)}, bf16[2048,512]{1,0:T(8,128)(2,1)S(1)}, u32[]{:S(2)}) copy-start(bf16[2048,512]{1,0:T(8,128)(2,1)S(1)} %get-tuple-element.43.samples_ref) | copy-start | bytes 6291460
  35.2 12.6 %all-to-all-start.4 = ((f32[16,8,512]{2,1,0:T(8,128)}), f32[16,8,512]{2,1,0:T(8,128)S(1)}, u32[]{:S(2)}, u32[]{:S(2)}) async-start(f32[16,8,512]{2,1,0:T(8,128)} %bitcast.5), calls=%async_computation.4 | async-start | bytes 524288 | tf_op jit(solution)/shard_map/all_to_all | solution.py:27

commit v14 on v13

--- a/solution.py
+++ b/solution.py
@@ -191,10 +191,15 @@
     size = found_v.shape[1]
     in_flight = [copy_of(found_ref.at[block], found_v, sems.at[3, 0]), copy_of(slots_ref, slots_v, sems.at[3, 1])]
     in_flight += [copy_of(ref, v, sems.at[4, i]) for i, (ref, v) in enumerate(zip(held, held_v))]
-    in_flight.append(copy_of(samples_ref, samples_v, sems.at[2, 1]))
+    samples_in = copy_of(samples_ref, samples_v, sems.at[2, 1])
     inverse_in = copy_of(inverse_ref.at[block], inverse_v, sems.at[2, 0])
     wait_all(*in_flight)
-    points_v[0], points_v[1] = points_of(found_v[...], held_v, slots_v[:, (block + 1) * size : (block + 2) * size])
+
+    @stage(live_ref)
+    def _():
+        points_v[0], points_v[1] = points_of(found_v[...], held_v, slots_v[:, (block + 1) * size : (block + 2) * size])
+
+    samples_in.wait()
     copies = make_columns(live_ref, samples_v, (points_v[0], points_v[1]), columns_v, high_ref, low_ref, sems)
     wait_all(inverse_in, *copies)
 

time: 90.9 us -> 90.5 us (level)
  no operation moved by 1% of the time
where the time goes in v14:
time: 90.5 us; the launch traced here: 90.1 us
  blocking collectives  57.5 us (64%)
  Pallas kernels  24.2 us (27%)
  starting transfers between devices  6.1 us (7%)
  waiting for transfers between devices  1.13 us (1%)
  between operations  0.93 us (1%)
    all_to_all x4, blocking collectives, exchange(): return lax.all_to_all(x, 'rows', 0, 0, axis_index_groups=[order])  57.5 us
    pallas_call x6, Pallas kernels, local(): pl.pallas_call(kernel, out_shape=[SPACES[p](shape, dtype) for p, shape, d...  24.2 us
    all_to_all x1, starting transfers between devices, exchange(): return lax.all_to_all(x, 'rows', 0, 0, axis_index_groups=[order])  6.03 us
  transfers between devices with their start and end apart: 2, of which 2 were waited for; matrix products, arithmetic and copies ran while one was open for 0% of the time, Pallas kernels for 9%

profile of v14, /device:TPU:0, one launch (start us, length us, event | category | flops | bytes accessed | tf_op | source)
XLA Modules:
  0.0 90.1 jit_solution(9356502458033821167)
XLA Ops:
  0.7 2.6 %pick.1 = (f32[48,256]{1,0:T(8,128)S(1)}, s32[1,1024]{1,0:T(1,128)S(1)}, s32[1]{0:T(128)S(4)}) custom-call(s32[1]{0:T(128)S(6)} %copy.11.live_ref, s32[2,512]{1,0:T(2,128)} %ids_ref.1, f32[2048,256]{1,0:T(8,128)} %samples_ref.3), custom_call_target="tpu_custom_call" | custom-call | flops 100663296 | bytes 2101252 | tf_op jit(solution)/shard_map/pick/pallas_call | solution.py:285
  3.2 24.4 %conditional.1 = (f32[768,256]{1,0:T(8,128)S(1)}) conditional(s32[]{:T(128)} %bitcast.4, f32[48,256]{1,0:T(8,128)S(1)} %get-tuple-element.42, f32[48,256]{1,0:T(8,128)S(1)} %get-tuple-element.42, (s32[2,512]{1,0:T(2,128)}, f32[2048,256]{1,0:T(8,128)}) %tuple.16), branch_computations={%region_0.1_spmd, %region_1.2_spmd, %region_2.4_spmd} | conditional | flops 1610797824 | bytes 6938754 | solution.py:355
  3.3 24.3 %all_to_all.36 = f32[16,40,256]{2,1,0:T(8,128)S(1)} all-to-all(f32[16,40,256]{2,1,0:T(8,128)S(1)} %broadcast_in_dim.8), channel_id=1, replica_groups={{14,12,2,28,0,10,4,26,8,30,16,20,24,22,18,6},{15,13,3,29,1,11,5,27,9,31..., dimensions={0} | all-to-all | bytes 1310720 | tf_op jit(solution)/shard_map/cond/branch_0_fun/all_to_all | solution.py:27
  27.6 0.1 pad.6
  27.6 0.0 copy-start
  27.7 0.1 collective-permute-start
  27.7 1.9 %own.1 = (bf16[2,512,512]{2,1,0:T(8,128)(2,1)S(1)}, bf16[2048,512]{1,0:T(8,128)(2,1)S(1)}) custom-call(s32[1]{0:T(128)S(6)} %copy.11.live_ref, s32[1,1024]{1,0:T(1,128)S(1)} %get-tuple-element.40.slots_ref, f32[768,256]{1,0:T(8,128)S(1)} %get-tuple-element.63.held_ref, f32[2048,256]{1,0:T(8,128)} %samples_ref.3), custom_call_target="tpu_custom_call" | custom-call | flops 805306368 | bytes 2887684 | tf_op jit(solution)/shard_map/own/pallas_call | solution.py:285
  29.7 0.0 copy-start.1
  29.7 0.3 collective-permute-done.refs_0_
  30.0 0.0 copy-done
  30.0 5.1 %first.1 = (bf16[2048,512]{1,0:T(8,128)(2,1)}, bf16[2048,512]{1,0:T(8,128)(2,1)}, f32[128,512]{1,0:T(8,128)}, s32[1,1024]{1,0:T(1,128)}, bf16[1,512,512]{2,1,0:T(8,128)(2,1)}, /*index=5*/f32[768,256]{1,0:T(8,128)}) custom-call(s32[1]{0:T(128)S(6)} %copy.11.live_ref, f32[2048,128]{1,0:T(8,128)S(1)} %copy-done, ...), custom_call_target="tpu_custom_call" | custom-call | flops 2415919104 | bytes 4984836 | tf_op jit(solution)/shard_map/first/pallas_call | solution.py:285
  35.2 0.0 copy-done.1
  35.2 6.0 %all-to-all-start.4 = ((f32[16,8,512]{2,1,0:T(8,128)}), f32[16,8,512]{2,1,0:T(8,128)S(1)}, u32[]{:S(2)}, u32[]{:S(2)}) async-start(f32[16,8,512]{2,1,0:T(8,128)} %bitcast.5), calls=%async_computation.4 | async-start | bytes 524288 | tf_op jit(solution)/shard_map/all_to_all | solution.py:27
  41.2 5.8 %beside.1 = (bf16[2048,512]{1,0:T(8,128)(2,1)}, bf16[2048,512]{1,0:T(8,128)(2,1)}, f32[512,512]{1,0:T(8,128)S(1)}) custom-call(s32[1]{0:T(128)S(6)} %copy.11.live_ref, bf16[2048,512]{1,0:T(8,128)(2,1)} %copy-done.1, s32[1,1024]{1,0:T(1,128)} %get-tuple-element.48.slots_ref, bf16[1,512,512]{2,1,0:T(8,128)(2,1)} %get-tuple-element.49.found_ref, ...), custom_call_target="tpu_custom_call" | custom-call | flops 1610612736 | bytes 5509124 | tf_op jit(solution)/shard_map/beside/pallas_call | solution.py:285
  47.0 0.8 all-to-all-done.4
  47.9 10.9 %all_to_all.40 = f32[16,8,512]{2,1,0:T(8,128)S(1)} all-to-all(f32[16,8,512]{2,1,0:T(8,128)S(1)} %broadcast_in_dim.20), channel_id=1, replica_groups={{22,8,14,26,30,16,10,28,0,18,2,6,12,4,20,24},{23,9,15,27,31,17,11,29,1,..., dimensions={0} | all-to-all | bytes 524288 | tf_op jit(solution)/shard_map/all_to_all | solution.py:27
  58.8 4.9 %middle.1 = (f32[2048,128]{1,0:T(8,128)S(1)}, f32[128,512]{1,0:T(8,128)S(1)}, f32[512,512]{1,0:T(8,128)S(1)}) custom-call(s32[1]{0:T(128)S(6)} %copy.11.live_ref, f32[128,512]{1,0:T(8,128)S(1)} %bitcast.11, f32[512,512]{1,0:T(8,128)S(1)} %get-tuple-element.55.inverse_ref, f32[2048,128]{1,0:T(8,128)} %residual_ref.3, ...), custom_call_target="tpu_custom_call" | custom-call | flops 1610612736 | bytes 12845060 | tf_op jit(solution)/shard_map/middle/pallas_call | solution.py:285
  63.7 11.1 %all_to_all.41 = f32[16,8,512]{2,1,0:T(8,128)S(1)} all-to-all(f32[16,8,512]{2,1,0:T(8,128)S(1)} %bitcast.16), channel_id=1, replica_groups={{22,8,14,26,30,16,10,28,0,18,2,6,12,4,20,24},{23,9,15,27,31,17,11,29,1,..., dimensions={0} | all-to-all | bytes 524288 | tf_op jit(solution)/shard_map/all_to_all | solution.py:27
  74.8 11.2 %all_to_all.42 = f32[16,8,512]{2,1,0:T(8,128)S(1)} all-to-all(f32[16,8,512]{2,1,0:T(8,128)S(1)} %broadcast_in_dim.26), channel_id=1, replica_groups={{22,8,14,26,30,16,10,28,0,18,2,6,12,4,20,24},{23,9,15,27,31,17,11,29,1,..., dimensions={0} | all-to-all | bytes 524288 | tf_op jit(solution)/shard_map/all_to_all | solution.py:27
  86.0 3.9 %last.1 = f32[2048,128]{1,0:T(8,128)} custom-call(s32[1]{0:T(128)S(6)} %copy.11.live_ref, f32[128,512]{1,0:T(8,128)S(1)} %bitcast.12, f32[512,512]{1,0:T(8,128)S(1)} %get-tuple-element.61.inverse_ref, f32[2048,128]{1,0:T(8,128)S(1)} %get-tuple-element.62.residual_ref, bf16[2048,512]{1,0:T(8,128)(2,1)} %get-tuple-element.58.next_high.high_ref, ...), custom_call_target="tpu_custom_call" | custom-call | flops 805306368 | bytes 6553604 | tf_op jit(solution)/shard_map/last/pallas_call | solution.py:285
  (6 shorter events, 0.1 us)
Async XLA Ops:
  27.6 2.4 %copy-start = (f32[2048,128]{1,0:T(8,128)S(1)}, f32[2048,128]{1,0:T(8,128)}, u32[]{:S(2)}) copy-start(f32[2048,128]{1,0:T(8,128)} %residual_ref.3) | copy-start | bytes 3145732
  27.7 2.4 %collective-permute-start = (f32[768,256]{1,0:T(8,128)S(1)}, f32[768,256]{1,0:T(8,128)S(1)}, u32[]{:S(2)}, u32[]{:S(2)}) collective-permute-start(f32[768,256]{1,0:T(8,128)S(1)} %get-tuple-element.63.held_ref), channel_id=1, source_target_pairs={{1,0},{0,1},{3,2},{2,3},{5,4},{4,5},{7,6},{6,7},{9,8},{8,9},{11,10... | collective-permute-start | bytes 2359304 | tf_op jit(solution)/shard_map/ppermute | solution.py:356
  29.7 5.5 %copy-start.1 = (bf16[2048,512]{1,0:T(8,128)(2,1)}, bf16[2048,512]{1,0:T(8,128)(2,1)S(1)}, u32[]{:S(2)}) copy-start(bf16[2048,512]{1,0:T(8,128)(2,1)S(1)} %get-tuple-element.43.samples_ref) | copy-start | bytes 6291460
  35.2 12.6 %all-to-all-start.4 = ((f32[16,8,512]{2,1,0:T(8,128)}), f32[16,8,512]{2,1,0:T(8,128)S(1)}, u32[]{:S(2)}, u32[]{:S(2)}) async-start(f32[16,8,512]{2,1,0:T(8,128)} %bitcast.5), calls=%async_computation.4 | async-start | bytes 524288 | tf_op jit(solution)/shard_map/all_to_all | solution.py:27

commit v15 on v14

--- a/solution.py
+++ b/solution.py
@@ -255,6 +255,8 @@
 
 def last_kernel(live_ref, sums_ref, inverse_ref, residual_ref, high_ref, low_ref, out_ref, coefs_v, residual_v, columns_v, sems):
     parts = pieces(out_ref.shape[0])
+    end = parts.pop()
+    parts += [pl.ds(end.start + part.start, part.size) for part in pieces(end.size, end.size // 2)]
     columns_in = [
         [copy_of(ref.at[at], columns_v.at[kind, at], sems.at[kind, i]) for kind, ref in enumerate((high_ref, low_ref))]
         for i, at in enumerate(parts)
@@ -369,7 +371,7 @@
     columns_v = pltpu.VMEM((2, rows_here, size), BF16)
     residual_v = pltpu.VMEM((rows_here, width), F32)
     coefs_v = pltpu.VMEM((size, 2 * width), BF16)
-    sems = pltpu.SemaphoreType.DMA((6, max(cores, len(pieces(rows_here)))))
+    sems = pltpu.SemaphoreType.DMA((6, max(cores, len(pieces(rows_here)) + 1)))
     columns_out = [("H", (rows_here, size), BF16)] * 2
     inverse_out = ("V", (size, size), F32)
     totals_out = ("V", (width, size), F32)

time: 90.5 us -> 92.1 us (1.018); the launches traced: 90.1 us -> 90.4 us
  no operation moved by 1% of the time
where the time goes in v15:
time: 92.1 us; the launch traced here: 90.4 us
  blocking collectives  57.5 us (62%)
  Pallas kernels  24.5 us (27%)
  starting transfers between devices  6.1 us (7%)
  waiting for transfers between devices  1.07 us (1%)
  between operations  0.93 us (1%)
    all_to_all x4, blocking collectives, exchange(): return lax.all_to_all(x, 'rows', 0, 0, axis_index_groups=[order])  57.5 us
    pallas_call x6, Pallas kernels, local(): pl.pallas_call(kernel, out_shape=[SPACES[p](shape, dtype) for p, shape, d...  24.5 us
    all_to_all x1, starting transfers between devices, exchange(): return lax.all_to_all(x, 'rows', 0, 0, axis_index_groups=[order])  6.03 us
  transfers between devices with their start and end apart: 2, of which 2 were waited for; matrix products, arithmetic and copies ran while one was open for 0% of the time, Pallas kernels for 9%

profile of v15, /device:TPU:0, one launch (start us, length us, event | category | flops | bytes accessed | tf_op | source)
XLA Modules:
  0.0 90.4 jit_solution(8162912098421716258)
XLA Ops:
  0.7 2.6 %pick.1 = (f32[48,256]{1,0:T(8,128)S(1)}, s32[1,1024]{1,0:T(1,128)S(1)}, s32[1]{0:T(128)S(4)}) custom-call(s32[1]{0:T(128)S(6)} %copy.11.live_ref, s32[2,512]{1,0:T(2,128)} %ids_ref.1, f32[2048,256]{1,0:T(8,128)} %samples_ref.3), custom_call_target="tpu_custom_call" | custom-call | flops 100663296 | bytes 2101252 | tf_op jit(solution)/shard_map/pick/pallas_call | solution.py:287
  3.2 24.4 %conditional.1 = (f32[768,256]{1,0:T(8,128)S(1)}) conditional(s32[]{:T(128)} %bitcast.4, f32[48,256]{1,0:T(8,128)S(1)} %get-tuple-element.42, f32[48,256]{1,0:T(8,128)S(1)} %get-tuple-element.42, (s32[2,512]{1,0:T(2,128)}, f32[2048,256]{1,0:T(8,128)}) %tuple.16), branch_computations={%region_0.1_spmd, %region_1.2_spmd, %region_2.4_spmd} | conditional | flops 1610797824 | bytes 6938754 | solution.py:357
  3.3 24.3 %all_to_all.36 = f32[16,40,256]{2,1,0:T(8,128)S(1)} all-to-all(f32[16,40,256]{2,1,0:T(8,128)S(1)} %broadcast_in_dim.8), channel_id=1, replica_groups={{14,12,2,28,0,10,4,26,8,30,16,20,24,22,18,6},{15,13,3,29,1,11,5,27,9,31..., dimensions={0} | all-to-all | bytes 1310720 | tf_op jit(solution)/shard_map/cond/branch_0_fun/all_to_all | solution.py:27
  27.6 0.1 pad.6
  27.6 0.0 copy-start
  27.7 0.1 collective-permute-start
  27.7 1.9 %own.1 = (bf16[2,512,512]{2,1,0:T(8,128)(2,1)S(1)}, bf16[2048,512]{1,0:T(8,128)(2,1)S(1)}) custom-call(s32[1]{0:T(128)S(6)} %copy.11.live_ref, s32[1,1024]{1,0:T(1,128)S(1)} %get-tuple-element.40.slots_ref, f32[768,256]{1,0:T(8,128)S(1)} %get-tuple-element.63.held_ref, f32[2048,256]{1,0:T(8,128)} %samples_ref.3), custom_call_target="tpu_custom_call" | custom-call | flops 805306368 | bytes 2887684 | tf_op jit(solution)/shard_map/own/pallas_call | solution.py:287
  29.7 0.0 copy-start.1
  29.7 0.3 collective-permute-done.refs_0_
  30.0 0.0 copy-done
  30.0 5.2 %first.1 = (bf16[2048,512]{1,0:T(8,128)(2,1)}, bf16[2048,512]{1,0:T(8,128)(2,1)}, f32[128,512]{1,0:T(8,128)}, s32[1,1024]{1,0:T(1,128)}, bf16[1,512,512]{2,1,0:T(8,128)(2,1)}, /*index=5*/f32[768,256]{1,0:T(8,128)}) custom-call(s32[1]{0:T(128)S(6)} %copy.11.live_ref, f32[2048,128]{1,0:T(8,128)S(1)} %copy-done, ...), custom_call_target="tpu_custom_call" | custom-call | flops 2415919104 | bytes 4984836 | tf_op jit(solution)/shard_map/first/pallas_call | solution.py:287
  35.2 0.0 copy-done.1
  35.2 6.0 %all-to-all-start.4 = ((f32[16,8,512]{2,1,0:T(8,128)}), f32[16,8,512]{2,1,0:T(8,128)S(1)}, u32[]{:S(2)}, u32[]{:S(2)}) async-start(f32[16,8,512]{2,1,0:T(8,128)} %bitcast.5), calls=%async_computation.4 | async-start | bytes 524288 | tf_op jit(solution)/shard_map/all_to_all | solution.py:27
  41.2 5.9 %beside.1 = (bf16[2048,512]{1,0:T(8,128)(2,1)}, bf16[2048,512]{1,0:T(8,128)(2,1)}, f32[512,512]{1,0:T(8,128)S(1)}) custom-call(s32[1]{0:T(128)S(6)} %copy.11.live_ref, bf16[2048,512]{1,0:T(8,128)(2,1)} %copy-done.1, s32[1,1024]{1,0:T(1,128)} %get-tuple-element.48.slots_ref, bf16[1,512,512]{2,1,0:T(8,128)(2,1)} %get-tuple-element.49.found_ref, ...), custom_call_target="tpu_custom_call" | custom-call | flops 1610612736 | bytes 5509124 | tf_op jit(solution)/shard_map/beside/pallas_call | solution.py:287
  47.1 0.7 all-to-all-done.4
  47.9 11.0 %all_to_all.40 = f32[16,8,512]{2,1,0:T(8,128)S(1)} all-to-all(f32[16,8,512]{2,1,0:T(8,128)S(1)} %broadcast_in_dim.20), channel_id=1, replica_groups={{22,8,14,26,30,16,10,28,0,18,2,6,12,4,20,24},{23,9,15,27,31,17,11,29,1,..., dimensions={0} | all-to-all | bytes 524288 | tf_op jit(solution)/shard_map/all_to_all | solution.py:27
  58.9 4.9 %middle.1 = (f32[2048,128]{1,0:T(8,128)S(1)}, f32[128,512]{1,0:T(8,128)S(1)}, f32[512,512]{1,0:T(8,128)S(1)}) custom-call(s32[1]{0:T(128)S(6)} %copy.11.live_ref, f32[128,512]{1,0:T(8,128)S(1)} %bitcast.11, f32[512,512]{1,0:T(8,128)S(1)} %get-tuple-element.55.inverse_ref, f32[2048,128]{1,0:T(8,128)} %residual_ref.3, ...), custom_call_target="tpu_custom_call" | custom-call | flops 1610612736 | bytes 12845060 | tf_op jit(solution)/shard_map/middle/pallas_call | solution.py:287
  63.8 11.1 %all_to_all.41 = f32[16,8,512]{2,1,0:T(8,128)S(1)} all-to-all(f32[16,8,512]{2,1,0:T(8,128)S(1)} %bitcast.16), channel_id=1, replica_groups={{22,8,14,26,30,16,10,28,0,18,2,6,12,4,20,24},{23,9,15,27,31,17,11,29,1,..., dimensions={0} | all-to-all | bytes 524288 | tf_op jit(solution)/shard_map/all_to_all | solution.py:27
  75.0 11.2 %all_to_all.42 = f32[16,8,512]{2,1,0:T(8,128)S(1)} all-to-all(f32[16,8,512]{2,1,0:T(8,128)S(1)} %broadcast_in_dim.26), channel_id=1, replica_groups={{22,8,14,26,30,16,10,28,0,18,2,6,12,4,20,24},{23,9,15,27,31,17,11,29,1,..., dimensions={0} | all-to-all | bytes 524288 | tf_op jit(solution)/shard_map/all_to_all | solution.py:27
  86.2 4.1 %last.1 = f32[2048,128]{1,0:T(8,128)} custom-call(s32[1]{0:T(128)S(6)} %copy.11.live_ref, f32[128,512]{1,0:T(8,128)S(1)} %bitcast.12, f32[512,512]{1,0:T(8,128)S(1)} %get-tuple-element.61.inverse_ref, f32[2048,128]{1,0:T(8,128)S(1)} %get-tuple-element.62.residual_ref, bf16[2048,512]{1,0:T(8,128)(2,1)} %get-tuple-element.58.next_high.high_ref, ...), custom_call_target="tpu_custom_call" | custom-call | flops 805306368 | bytes 6553604 | tf_op jit(solution)/shard_map/last/pallas_call | solution.py:287
  (6 shorter events, 0.1 us)
Async XLA Ops:
  27.6 2.4 %copy-start = (f32[2048,128]{1,0:T(8,128)S(1)}, f32[2048,128]{1,0:T(8,128)}, u32[]{:S(2)}) copy-start(f32[2048,128]{1,0:T(8,128)} %residual_ref.3) | copy-start | bytes 3145732
  27.7 2.4 %collective-permute-start = (f32[768,256]{1,0:T(8,128)S(1)}, f32[768,256]{1,0:T(8,128)S(1)}, u32[]{:S(2)}, u32[]{:S(2)}) collective-permute-start(f32[768,256]{1,0:T(8,128)S(1)} %get-tuple-element.63.held_ref), channel_id=1, source_target_pairs={{1,0},{0,1},{3,2},{2,3},{5,4},{4,5},{7,6},{6,7},{9,8},{8,9},{11,10... | collective-permute-start | bytes 2359304 | tf_op jit(solution)/shard_map/ppermute | solution.py:358
  29.7 5.5 %copy-start.1 = (bf16[2048,512]{1,0:T(8,128)(2,1)}, bf16[2048,512]{1,0:T(8,128)(2,1)S(1)}, u32[]{:S(2)}) copy-start(bf16[2048,512]{1,0:T(8,128)(2,1)S(1)} %get-tuple-element.43.samples_ref) | copy-start | bytes 6291460
  35.2 12.6 %all-to-all-start.4 = ((f32[16,8,512]{2,1,0:T(8,128)}), f32[16,8,512]{2,1,0:T(8,128)S(1)}, u32[]{:S(2)}, u32[]{:S(2)}) async-start(f32[16,8,512]{2,1,0:T(8,128)} %bitcast.5), calls=%async_computation.4 | async-start | bytes 524288 | tf_op jit(solution)/shard_map/all_to_all | solution.py:27

commit v16 on v15

--- a/solution.py
+++ b/solution.py
@@ -11,7 +11,7 @@
 F32 = jnp.float32
 BF16 = jnp.bfloat16
 ROWS_STEP = 512
-HALF_STEP = 1024
+HALF_STEP = 512
 LIMIT = 24 * 2**20
 POINTS_SEED = 14
 SUMS_SEED = 152

time: 92.1 us -> 91.9 us (level); the launches traced: 90.4 us -> 92.7 us
  blocking collectives: 57.5 us -> 60 us
    all_to_all x4, blocking collectives: 57.5 us -> 60 us  [exchange(): return lax.all_to_all(x, 'rows', 0, 0, axis_index_groups=[order])]
  transfers between devices with their start and end apart: 2 -> 2, of which waited for: 2 -> 2; matrix products, arithmetic and copies ran while one was open for 0% -> 0% of each run, Pallas kernels for 9% -> 8%
where the time goes in v16:
time: 91.9 us; the launch traced here: 92.7 us
  blocking collectives  60 us (65%)
  Pallas kernels  24.2 us (26%)
  starting transfers between devices  6.03 us (7%)
  waiting for transfers between devices  1.39 us (2%)
    all_to_all x4, blocking collectives, exchange(): return lax.all_to_all(x, 'rows', 0, 0, axis_index_groups=[order])  60 us
    pallas_call x6, Pallas kernels, local(): pl.pallas_call(kernel, out_shape=[SPACES[p](shape, dtype) for p, shape, d...  24.2 us
    all_to_all x1, starting transfers between devices, exchange(): return lax.all_to_all(x, 'rows', 0, 0, axis_index_groups=[order])  6.03 us
  transfers between devices with their start and end apart: 2, of which 2 were waited for; matrix products, arithmetic and copies ran while one was open for 0% of the time, Pallas kernels for 8%

profile of v16, /device:TPU:0, one launch (start us, length us, event | category | flops | bytes accessed | tf_op | source)
XLA Modules:
  0.0 92.7 jit_solution(7838039927258700708)
XLA Ops:
  0.7 2.8 %pick.1 = (f32[48,256]{1,0:T(8,128)S(1)}, s32[1,1024]{1,0:T(1,128)S(1)}, s32[1]{0:T(128)S(4)}) custom-call(s32[1]{0:T(128)S(6)} %copy.11.live_ref, s32[2,512]{1,0:T(2,128)} %ids_ref.1, f32[2048,256]{1,0:T(8,128)} %samples_ref.3), custom_call_target="tpu_custom_call" | custom-call | flops 100663296 | bytes 2101252 | tf_op jit(solution)/shard_map/pick/pallas_call | solution.py:287
  3.5 27.0 %conditional.1 = (f32[768,256]{1,0:T(8,128)S(1)}) conditional(s32[]{:T(128)} %bitcast.4, f32[48,256]{1,0:T(8,128)S(1)} %get-tuple-element.42, f32[48,256]{1,0:T(8,128)S(1)} %get-tuple-element.42, (s32[2,512]{1,0:T(2,128)}, f32[2048,256]{1,0:T(8,128)}) %tuple.16), branch_computations={%region_0.1_spmd, %region_1.2_spmd, %region_2.4_spmd} | conditional | flops 1610797824 | bytes 6938754 | solution.py:357
  3.5 0.1 broadcast_in_dim.9
  3.6 26.9 %all_to_all.37 = f32[16,48,256]{2,1,0:T(8,128)S(1)} all-to-all(f32[16,48,256]{2,1,0:T(8,128)S(1)} %broadcast_in_dim.9), channel_id=1, replica_groups={{14,12,2,28,0,10,4,26,8,30,16,20,24,22,18,6},{15,13,3,29,1,11,5,27,9,31..., dimensions={0} | all-to-all | bytes 1572864 | tf_op jit(solution)/shard_map/cond/branch_1_fun/all_to_all | solution.py:27
  30.5 0.0 copy-start
  30.5 0.0 collective-permute-start
  30.5 1.9 %own.1 = (bf16[2,512,512]{2,1,0:T(8,128)(2,1)S(1)}, bf16[2048,512]{1,0:T(8,128)(2,1)S(1)}) custom-call(s32[1]{0:T(128)S(6)} %copy.11.live_ref, s32[1,1024]{1,0:T(1,128)S(1)} %get-tuple-element.40.slots_ref, f32[768,256]{1,0:T(8,128)S(1)} %get-tuple-element.63.held_ref, f32[2048,256]{1,0:T(8,128)} %samples_ref.3), custom_call_target="tpu_custom_call" | custom-call | flops 805306368 | bytes 2887684 | tf_op jit(solution)/shard_map/own/pallas_call | solution.py:287
  32.4 0.0 copy-start.1
  32.5 0.3 collective-permute-done.refs_0_
  32.8 0.0 copy-done
  32.8 4.9 %first.1 = (bf16[2048,512]{1,0:T(8,128)(2,1)}, bf16[2048,512]{1,0:T(8,128)(2,1)}, f32[128,512]{1,0:T(8,128)}, s32[1,1024]{1,0:T(1,128)}, bf16[1,512,512]{2,1,0:T(8,128)(2,1)}, /*index=5*/f32[768,256]{1,0:T(8,128)}) custom-call(s32[1]{0:T(128)S(6)} %copy.11.live_ref, f32[2048,128]{1,0:T(8,128)S(1)} %copy-done, ...), custom_call_target="tpu_custom_call" | custom-call | flops 2415919104 | bytes 4984836 | tf_op jit(solution)/shard_map/first/pallas_call | solution.py:287
  37.7 0.0 copy-done.1
  37.7 6.0 %all-to-all-start.4 = ((f32[16,8,512]{2,1,0:T(8,128)}), f32[16,8,512]{2,1,0:T(8,128)S(1)}, u32[]{:S(2)}, u32[]{:S(2)}) async-start(f32[16,8,512]{2,1,0:T(8,128)} %bitcast.5), calls=%async_computation.4 | async-start | bytes 524288 | tf_op jit(solution)/shard_map/all_to_all | solution.py:27
  43.7 5.6 %beside.1 = (bf16[2048,512]{1,0:T(8,128)(2,1)}, bf16[2048,512]{1,0:T(8,128)(2,1)}, f32[512,512]{1,0:T(8,128)S(1)}) custom-call(s32[1]{0:T(128)S(6)} %copy.11.live_ref, bf16[2048,512]{1,0:T(8,128)(2,1)} %copy-done.1, s32[1,1024]{1,0:T(1,128)} %get-tuple-element.48.slots_ref, bf16[1,512,512]{2,1,0:T(8,128)(2,1)} %get-tuple-element.49.found_ref, ...), custom_call_target="tpu_custom_call" | custom-call | flops 1610612736 | bytes 5509124 | tf_op jit(solution)/shard_map/beside/pallas_call | solution.py:287
  49.3 1.1 %all-to-all-done.4 = f32[16,8,512]{2,1,0:T(8,128)S(1)} async-done(((f32[16,8,512]{2,1,0:T(8,128)}), f32[16,8,512]{2,1,0:T(8,128)S(1)}, u32[]{:S(2)}, u32[]{:S(2)}) %all-to-all-start.4) | async-done | bytes 262176 | tf_op jit(solution)/shard_map/all_to_all | solution.py:27
  50.4 10.9 %all_to_all.40 = f32[16,8,512]{2,1,0:T(8,128)S(1)} all-to-all(f32[16,8,512]{2,1,0:T(8,128)S(1)} %broadcast_in_dim.20), channel_id=1, replica_groups={{22,8,14,26,30,16,10,28,0,18,2,6,12,4,20,24},{23,9,15,27,31,17,11,29,1,..., dimensions={0} | all-to-all | bytes 524288 | tf_op jit(solution)/shard_map/all_to_all | solution.py:27
  61.3 4.9 %middle.1 = (f32[2048,128]{1,0:T(8,128)S(1)}, f32[128,512]{1,0:T(8,128)S(1)}, f32[512,512]{1,0:T(8,128)S(1)}) custom-call(s32[1]{0:T(128)S(6)} %copy.11.live_ref, f32[128,512]{1,0:T(8,128)S(1)} %bitcast.11, f32[512,512]{1,0:T(8,128)S(1)} %get-tuple-element.55.inverse_ref, f32[2048,128]{1,0:T(8,128)} %residual_ref.3, ...), custom_call_target="tpu_custom_call" | custom-call | flops 1610612736 | bytes 12845060 | tf_op jit(solution)/shard_map/middle/pallas_call | solution.py:287
  66.2 11.0 %all_to_all.41 = f32[16,8,512]{2,1,0:T(8,128)S(1)} all-to-all(f32[16,8,512]{2,1,0:T(8,128)S(1)} %bitcast.16), channel_id=1, replica_groups={{22,8,14,26,30,16,10,28,0,18,2,6,12,4,20,24},{23,9,15,27,31,17,11,29,1,..., dimensions={0} | all-to-all | bytes 524288 | tf_op jit(solution)/shard_map/all_to_all | solution.py:27
  77.3 11.2 %all_to_all.42 = f32[16,8,512]{2,1,0:T(8,128)S(1)} all-to-all(f32[16,8,512]{2,1,0:T(8,128)S(1)} %broadcast_in_dim.26), channel_id=1, replica_groups={{22,8,14,26,30,16,10,28,0,18,2,6,12,4,20,24},{23,9,15,27,31,17,11,29,1,..., dimensions={0} | all-to-all | bytes 524288 | tf_op jit(solution)/shard_map/all_to_all | solution.py:27
  88.5 4.1 %last.1 = f32[2048,128]{1,0:T(8,128)} custom-call(s32[1]{0:T(128)S(6)} %copy.11.live_ref, f32[128,512]{1,0:T(8,128)S(1)} %bitcast.12, f32[512,512]{1,0:T(8,128)S(1)} %get-tuple-element.61.inverse_ref, f32[2048,128]{1,0:T(8,128)S(1)} %get-tuple-element.62.residual_ref, bf16[2048,512]{1,0:T(8,128)(2,1)} %get-tuple-element.58.next_high.high_ref, ...), custom_call_target="tpu_custom_call" | custom-call | flops 805306368 | bytes 6553604 | tf_op jit(solution)/shard_map/last/pallas_call | solution.py:287
  (4 shorter events, 0.1 us)
Async XLA Ops:
  30.5 2.3 %copy-start = (f32[2048,128]{1,0:T(8,128)S(1)}, f32[2048,128]{1,0:T(8,128)}, u32[]{:S(2)}) copy-start(f32[2048,128]{1,0:T(8,128)} %residual_ref.3) | copy-start | bytes 3145732
  30.5 2.3 %collective-permute-start = (f32[768,256]{1,0:T(8,128)S(1)}, f32[768,256]{1,0:T(8,128)S(1)}, u32[]{:S(2)}, u32[]{:S(2)}) collective-permute-start(f32[768,256]{1,0:T(8,128)S(1)} %get-tuple-element.63.held_ref), channel_id=1, source_target_pairs={{1,0},{0,1},{3,2},{2,3},{5,4},{4,5},{7,6},{6,7},{9,8},{8,9},{11,10... | collective-permute-start | bytes 2359304 | tf_op jit(solution)/shard_map/ppermute | solution.py:358
  32.4 5.2 %copy-start.1 = (bf16[2048,512]{1,0:T(8,128)(2,1)}, bf16[2048,512]{1,0:T(8,128)(2,1)S(1)}, u32[]{:S(2)}) copy-start(bf16[2048,512]{1,0:T(8,128)(2,1)S(1)} %get-tuple-element.43.samples_ref) | copy-start | bytes 6291460
  37.7 12.7 %all-to-all-start.4 = ((f32[16,8,512]{2,1,0:T(8,128)}), f32[16,8,512]{2,1,0:T(8,128)S(1)}, u32[]{:S(2)}, u32[]{:S(2)}) async-start(f32[16,8,512]{2,1,0:T(8,128)} %bitcast.5), calls=%async_computation.4 | async-start | bytes 524288 | tf_op jit(solution)/shard_map/all_to_all | solution.py:27
